TPU v7x, 32 devices: a whole 2x2x4 slice. The times are simulated.
32 devices in a mesh: tm: 8 (over z, y), sta: 4 (over x, core).
Axes of the slice: x: 2, y: 2, z: 4, core: 2. Of those that a mesh axis runs over, the one named last changes fastest.
Arguments:
- traces: bfloat16 [8, 270336], P('sta', 'tm'), may hold values from -64 to 64
- station_flags: int32 [8], P('sta'), may hold values 0 or 1
- tile_mask: int32 [4, 4], replicated, may hold values 0 or 1
- band_block: int32 [1], replicated, may hold values from 1 to 137
- stacks: float32 [8, 8, 2, 3072], P('sta', None, None, 'tm'), may hold values from -6 to 6
Outputs:
- stacked: float32 [8, 8, 2, 3072], P('sta', None, None, 'tm')
All inputs are finite; a program needn't handle non-finite values. No bound on the sum of `station_flags` on one device may be relied on, other than what follows from the above.
Results may differ from a plain program's by a relative error of at most 0.0003.
Values may be sent and summed in bfloat16 or wider, within the bound.
No kernel may reach another device: no remote copies, remote signals or barrier semaphores. Data moves between devices by JAX's collectives and lax.ppermute only.
A program may use at most 128 MiB of HBM per device.

v0:
```python
import functools
import math

import jax
import jax.numpy as jnp
import numpy as np
from jax import lax
from jax.experimental import pallas as pl
from jax.experimental.pallas import tpu as pltpu
from jax.sharding import PartitionSpec as P

HALF_WIN = 512
SMOOTH = 32
EPS_MEAN = 1e-06
EPS_POWER = 1e-06
LANES = 128
SPAN = 2 * HALF_WIN
TILES = SPAN // LANES
HALF_TILES = HALF_WIN // LANES
PAD = 16
HIGH = lax.Precision.HIGHEST
BF = jnp.bfloat16
F32 = jnp.float32


def up_to(value, step):
    return -(-value // step) * step


def sincos(turns):
    quarter = jnp.round(turns * 4.0)
    rest = turns - quarter * 0.25
    y = rest * (2.0 * math.pi)
    y2 = y * y
    s = y + y * y2 * (-1.0 / 6 + y2 * (1.0 / 120 + y2 * (-1.0 / 5040 + y2 * (1.0 / 362880))))
    c = 1.0 + y2 * (-0.5 + y2 * (1.0 / 24 + y2 * (-1.0 / 720 + y2 * (1.0 / 40320))))
    q = quarter - 4.0 * jnp.floor(quarter * 0.25)
    swap = (q == 1.0) | (q == 3.0)
    sine = jnp.where(swap, c, s)
    cosine = jnp.where(swap, s, c)
    sine = jnp.where(q >= 2.0, -sine, sine)
    cosine = jnp.where((q == 1.0) | (q == 2.0), -cosine, cosine)
    return sine, cosine


def turns_of(product, period):
    whole = jnp.floor(product * (1.0 / period))
    return (product - whole * period) * (1.0 / period)


def split2(value):
    high = value.astype(BF)
    return high, (value - high.astype(F32)).astype(BF)


def iota(shape, axis):
    return lax.broadcasted_iota(jnp.int32, shape, axis)


def iota_f(shape, axis):
    return iota(shape, axis).astype(F32)


def window_table():
    low = np.arange(LANES)
    upto = (low[:, None] <= low[None, :]).astype(np.float32)
    onward = (low[:, None] >= low[None, :]).astype(np.float32)
    return np.concatenate([upto, onward, np.ones((LANES, LANES), np.float32)], axis=1)


def np_split(value):
    high = value.astype(jnp.bfloat16).astype(np.float64)
    return high, (value - high).astype(jnp.bfloat16).astype(np.float64)


class Sizes:
    def __init__(self, stations, length, tm_count, bins):
        self.stations, self.length, self.tm, self.bins = stations, length, tm_count, bins
        self.rows = length // SPAN
        self.rows_pad = up_to(self.rows, PAD)
        self.block = min(tm_count, 16)
        self.blocks = tm_count // self.block
        self.folds = -(-(bins + self.rows - 1) // self.rows)
        self.spec_lanes = self.rows * LANES
        self.edge_lanes = 2 * stations * SPAN
        self.payload = self.spec_lanes + self.edge_lanes
        assert length % SPAN == 0 and tm_count % self.block == 0
        assert 2 * stations * PAD * 2 <= LANES and self.folds <= PAD
        assert self.rows >= 2 and 5 * self.rows_pad <= 256

    def first_table(self):
        j2 = np.arange(self.tm)[:, None] + self.tm * np.arange(self.rows)[None, :]
        j2 = j2.reshape(self.blocks, self.block, self.rows).transpose(0, 2, 1).reshape(self.blocks, -1)
        period = self.tm * self.rows
        angle = 2.0 * np.pi / period * (j2[:, :, None] * np.arange(self.rows) % period)
        parts = np.concatenate([np.cos(angle), -np.sin(angle)], axis=1)
        parts = np.pad(parts, ((0, 0), (0, 0), (0, self.rows_pad - self.rows)))
        high, low = np_split(parts)
        return np.concatenate([high, high, high, low, low], axis=2).astype(jnp.bfloat16)

    def shift_table(self):
        angle = 2.0 * np.pi / self.length * (
            np.arange(self.rows)[:, None] * np.arange(SPAN)[None, :] % self.length
        )
        return np.stack([np.cos(angle), -np.sin(angle)]).astype(np.float32)


def transform_kernel(z, band, place, flags, x, first, shift, window, out, xs, sums, stack, weight, acc):
    rows, pad, block = z.rows, z.rows_pad, z.block
    top = 8
    for s in range(z.stations):
        xs[s, 0:top, :] = jnp.zeros((top, SPAN), F32)
        xs[s, top + (rows // 8) * 8 : top + pad, :] = jnp.zeros((pad - (rows // 8) * 8, SPAN), F32)
    for a in range(rows):
        piece = x[:, a * SPAN : (a + 1) * SPAN].astype(F32)
        xs[:, top + a, :] = piece
    for s in range(z.stations):
        for c in range(TILES):
            magnitude = jnp.abs(xs[s, top : top + pad, c * LANES : (c + 1) * LANES]).astype(BF)
            sums[s, c, 0:top, :] = jnp.zeros((top, 3 * LANES), F32)
            sums[s, c, top : top + pad, :] = jnp.dot(magnitude, window[...], preferred_element_type=F32)
            sums[s, c, top + pad : top + pad + 8, :] = jnp.zeros((8, 3 * LANES), F32)

        def tile(kind, c):
            turn, cc = divmod(c, TILES)
            return sums[s, cc, top + turn : top + turn + pad, kind * LANES : (kind + 1) * LANES]

        whole = [tile(2, c) for c in range(1 - HALF_TILES, TILES + HALF_TILES - 1)]
        flag = flags[s].astype(F32)
        row = iota((pad, LANES), 0)
        for c in range(TILES):
            total = tile(1, c - HALF_TILES) + tile(0, c + HALF_TILES)
            for d in range(2 * HALF_TILES - 1):
                total = total + whole[c + d]
            here = xs[s, top : top + pad, c * LANES : (c + 1) * LANES]
            value = flag * here / (total * (1.0 / (2 * HALF_WIN + 1)) + EPS_MEAN)
            edge = 0 if c < HALF_TILES else rows - 1
            value = jnp.where(row == edge, 0.0, value)
            high = value.astype(BF)
            left = value - high.astype(F32)
            mid = left.astype(BF)
            low = (left - mid.astype(F32)).astype(BF)
            for k, part in enumerate((high, mid, low, high, mid)):
                stack[s, k * pad : (k + 1) * pad, c * LANES : (c + 1) * LANES] = part
    fold0 = band[0] // rows
    order = iota((PAD, SPAN), 0) + fold0
    lane = iota((PAD, SPAN), 1)
    turns = jnp.bitwise_and(order * lane, SPAN - 1).astype(F32) * (1.0 / SPAN)
    sine, cosine = sincos(turns)
    (sin_h, sin_l), (cos_h, cos_l) = split2(sine), split2(cosine)
    nothing = jnp.zeros((PAD, SPAN), BF)
    for h, (cc, ss) in enumerate(((cos_h, sin_h), (cos_l, sin_l))):
        at = h * 4 * PAD
        weight[at : at + PAD, 0:SPAN] = cc
        weight[at + PAD : at + 2 * PAD, 0:SPAN] = -ss
        weight[at : at + PAD, SPAN : 2 * SPAN] = ss
        weight[at + PAD : at + 2 * PAD, SPAN : 2 * SPAN] = cc
        for k in (2, 3):
            for part in range(2):
                weight[at + k * PAD : at + (k + 1) * PAD, part * SPAN : (part + 1) * SPAN] = nothing
    acc[...] = jnp.zeros_like(acc)
    here = place[0]
    residue = pl.program_id(0) * block + iota((block, 256), 0)
    start = turns_of((here * residue).astype(F32), z.tm)

    def step(c, carry):
        lanes = pl.ds(pl.multiple_of(c * 256, 256), 256)
        lanes_im = pl.ds(pl.multiple_of(SPAN + c * 256, 256), 256)
        offset = c * 256 + iota((block, 256), 1)
        turn = start + (residue * offset).astype(F32) * (1.0 / (z.tm * z.length))
        sn, cs = sincos(turn)
        r_re, r_im = cs[None], -sn[None]
        m_re = shift[0, :, lanes][:, None, :]
        m_im = shift[1, :, lanes][:, None, :]
        t_re = (m_re * r_re - m_im * r_im).reshape(rows * block, 256)
        t_im = (m_re * r_im + m_im * r_re).reshape(rows * block, 256)
        for s in range(z.stations):
            f = jnp.dot(first[0], stack[s, :, lanes], preferred_element_type=F32)
            f_re, f_im = f[: rows * block], f[rows * block :]
            z_re = f_re * t_re - f_im * t_im
            z_im = f_re * t_im + f_im * t_re
            part = jnp.zeros((rows * block, LANES), F32)
            for value, w in ((z_re, weight[:, lanes]), (z_im, weight[:, lanes_im])):
                for piece in split2(value):
                    part = part + lax.dot_general(
                        piece, w, (((1,), (1,)), ((), ())), preferred_element_type=F32
                    )
            acc[s] = acc[s] + part
        return carry

    lax.fori_loop(0, SPAN // 256, step, 0)
    total = acc[0]
    for s in range(1, z.stations):
        total = total + pltpu.roll(acc[s], s * 2 * PAD, 1)
    total = total + pltpu.roll(total, LANES // 2, 1)
    high = total.astype(BF).astype(F32)
    low = total - high
    both = jnp.where(iota(total.shape, 1) < LANES // 2, high, low)
    for m in range(rows):
        out[:, m * LANES : (m + 1) * LANES] = both[m * block : (m + 1) * block].astype(BF)
    at = z.spec_lanes
    for begin in (0, z.length - SPAN):
        for s in range(z.stations):
            line = x[s : s + 1, begin : begin + SPAN].astype(F32)
            out[:, at : at + SPAN] = jnp.broadcast_to(line, (block, SPAN)).astype(BF)
            at += SPAN


def transform(z, band, place, flags, x):
    smem = pl.BlockSpec(memory_space=pltpu.SMEM)
    vmem = pl.BlockSpec(memory_space=pltpu.VMEM)
    width = 5 * z.rows_pad
    height = 2 * z.rows * z.block
    return pl.pallas_call(
        functools.partial(transform_kernel, z),
        grid=(z.blocks,),
        in_specs=[
            smem,
            smem,
            smem,
            vmem,
            pl.BlockSpec((1, height, width), lambda i: (i, 0, 0)),
            vmem,
            vmem,
        ],
        out_specs=pl.BlockSpec((z.block, z.payload), lambda i: (i, 0)),
        out_shape=jax.ShapeDtypeStruct((z.tm, z.payload), BF),
        scratch_shapes=[
            pltpu.VMEM((z.stations, 8 + z.rows_pad, SPAN), F32),
            pltpu.VMEM((z.stations, TILES, 16 + z.rows_pad, 3 * LANES), F32),
            pltpu.VMEM((z.stations, width, SPAN), BF),
            pltpu.VMEM((LANES, 2 * SPAN), BF),
            pltpu.VMEM((z.stations, z.rows * z.block, LANES), F32),
        ],
        name="transform",
    )(band, place, flags, x, jnp.asarray(z.first_table()), jnp.asarray(z.shift_table()),
      jnp.asarray(window_table(), BF))


def spectrum_kernel(z, band, place, flags, got, window, out):
    rows, tm, bins = z.rows, z.tm, z.bins
    base = band[0]
    residue = place[0]
    first = base % rows
    spot = iota_f((1, bins), 1) + first.astype(F32)
    fold = jnp.floor((spot + 0.5) * (1.0 / rows))
    rest = spot - fold * rows
    which = iota_f((rows, tm, bins), 0).reshape(rows * tm, bins)
    choose = (which == rest).astype(F32).astype(BF)
    parts = jnp.concatenate(
        [got[:, m * LANES : (m + 1) * LANES].astype(F32) for m in range(rows)], axis=0
    ).astype(BF)
    placed = lax.dot_general(parts, choose, (((0,), (0,)), ((), ())), preferred_element_type=F32)
    keep = (iota_f((PAD, bins), 0) == fold).astype(F32)
    folded = [
        jnp.sum(placed[k * PAD : (k + 1) * PAD] * keep, axis=0, keepdims=True)
        for k in range(2 * 2 * z.stations)
    ]
    spec = [folded[k] + folded[k + 2 * z.stations] for k in range(2 * z.stations)]
    count = 2 * TILES
    pieces = []
    for s in range(z.stations):
        for i in range(count):
            side = 1 if i < TILES else 0
            at = z.spec_lanes + (side * z.stations + s) * SPAN + (i % TILES) * LANES
            value = got[:, at : at + LANES].astype(F32)
            pieces.append(pltpu.roll(value, 1, 0) if side else value)
    magnitude = jnp.abs(jnp.concatenate(pieces, axis=0)).astype(BF)
    sums = jnp.dot(magnitude, window[...], preferred_element_type=F32)
    inner = iota((tm, LANES), 0) != 0
    p_turns = turns_of((residue * iota((tm, LANES), 0)).astype(F32), tm)
    p_sin, p_cos = sincos(p_turns)

    freq = (residue + tm * (base + iota((1, bins), 1))).astype(F32)
    step = iota_f((PAD, bins), 0)
    step = step - jnp.where(step >= TILES, float(TILES), 0.0) - HALF_TILES
    a_sin, a_cos = sincos(turns_of(step * freq, tm * (z.length // LANES)))
    real_row = iota((PAD, bins), 0) < TILES
    table = jnp.concatenate(
        [jnp.where(real_row, a_cos, a_sin), jnp.where(real_row, -a_sin, a_cos)], axis=1
    )
    l_sin, l_cos = sincos(turns_of(iota_f((LANES, bins), 0) * freq, tm * z.length))
    near = jnp.abs(iota((bins, bins), 0) - iota((bins, bins), 1)) <= SMOOTH
    near = near.astype(F32).astype(BF)

    for s in range(z.stations):
        def get(kind, i):
            at = (s * count + i) * tm
            return sums[at : at + tm, kind * LANES : (kind + 1) * LANES]

        reals, imags = [], []
        flag = flags[s].astype(F32)
        for i in range(HALF_TILES, HALF_TILES + TILES):
            terms = [(i - HALF_TILES, 1), (i + HALF_TILES, 0)]
            terms += [(i + d, 2) for d in range(1 - HALF_TILES, HALF_TILES)]
            own, other = jnp.zeros((tm, LANES), F32), jnp.zeros((tm, LANES), F32)
            for j, kind in terms:
                if (j < TILES) == (i < TILES):
                    own = own + get(kind, j)
                else:
                    other = other + get(kind, j)
            total = own + jnp.where(inner, other, 0.0)
            value = flag * pieces[s * count + i] / (total * (1.0 / (2 * HALF_WIN + 1)) + EPS_MEAN)
            reals.append(jnp.sum(value * p_cos, axis=0, keepdims=True))
            imags.append(-jnp.sum(value * p_sin, axis=0, keepdims=True))
        mixed = jnp.concatenate(reals + imags, axis=0)
        spread = lax.dot_general(
            mixed, table, (((0,), (0,)), ((), ())), precision=HIGH, preferred_element_type=F32
        )
        g_re, g_im = spread[:, :bins], spread[:, bins:]
        re = spec[2 * s] + jnp.sum(g_re * l_cos + g_im * l_sin, axis=0, keepdims=True)
        im = spec[2 * s + 1] + jnp.sum(g_im * l_cos - g_re * l_sin, axis=0, keepdims=True)
        power = re * re + im * im
        high = power.astype(BF)
        left = power - high.astype(F32)
        mid = left.astype(BF)
        low = (left - mid.astype(F32)).astype(BF)
        stacked = jnp.concatenate(
            [high.astype(F32), mid.astype(F32), low.astype(F32), jnp.zeros((5, bins), F32)], axis=0
        ).astype(BF)
        smooth = jnp.dot(stacked, near, preferred_element_type=F32)
        smooth = (smooth[0:1] + smooth[1:2] + smooth[2:3]) * (1.0 / (2 * SMOOTH + 1))
        scale = 1.0 / jnp.sqrt(smooth + EPS_POWER)
        out[2 * s : 2 * s + 1, :] = re * scale
        out[2 * s + 1 : 2 * s + 2, :] = im * scale


def spectrum(z, band, place, flags, got):
    smem = pl.BlockSpec(memory_space=pltpu.SMEM)
    vmem = pl.BlockSpec(memory_space=pltpu.VMEM)
    return pl.pallas_call(
        functools.partial(spectrum_kernel, z),
        in_specs=[smem, smem, smem, vmem, vmem],
        out_specs=vmem,
        out_shape=jax.ShapeDtypeStruct((2 * z.stations, z.bins), F32),
        name="spectrum",
    )(band, place, flags, got, jnp.asarray(window_table(), BF))


def shards(traces, station_flags, tile_mask, band_block, stacks):
    tm_count = lax.axis_size("tm")
    sta_here = lax.axis_index("sta")
    stations, length = traces.shape
    z = Sizes(stations, length, tm_count, stacks.shape[-1])
    place = lax.axis_index("tm").astype(jnp.int32).reshape(1)
    sent = transform(z, band_block, place, station_flags, traces)
    got = lax.all_to_all(sent, "tm", split_axis=0, concat_axis=0, tiled=True)
    white = spectrum(z, band_block, place, station_flags, got)
    every = lax.all_gather(white, "sta", axis=0, tiled=True).reshape(-1, 2, z.bins)
    mine = white.reshape(stations, 2, z.bins)
    other_real, other_imag = every[:, 0], every[:, 1]
    real, imag = mine[:, 0], mine[:, 1]
    mask_row = lax.dynamic_index_in_dim(tile_mask, sta_here, 0, keepdims=False).astype(F32)
    column_mask = jnp.repeat(mask_row, stations)
    cross_real = real[:, None, :] * other_real[None] + imag[:, None, :] * other_imag[None]
    cross_imag = imag[:, None, :] * other_real[None] - real[:, None, :] * other_imag[None]
    return stacks + jnp.stack([cross_real, cross_imag], axis=2) * column_mask[None, :, None, None]


def solution(mesh):
    return jax.shard_map(
        shards,
        mesh=mesh,
        in_specs=(P("sta", "tm"), P("sta"), P(), P(), P("sta", None, None, "tm")),
        out_specs=P("sta", None, None, "tm"),
        check_vma=False,
    )
```

profile of v0, /device:TPU:0, one launch (start us, length us, event | category | flops | bytes accessed | tf_op | source)
XLA Modules:
  0.0 37.2 jit_solution(9577988762658563243)
XLA Ops:
  0.7 6.5 %transform.1 = bf16[8,8320]{1,0:T(8,128)(2,1)} custom-call(s32[1]{0:T(128)S(6)} %copy.24.band, s32[1]{0:T(128)} %bitcast.place, s32[2]{0:T(128)} %flags.3, bf16[2,33792]{1,0:T(2,128)(2,1)} %x.1, bf16[1,528,240]{2,1,0:T(8,128)(2,1)} %constant.21.clone.first, f32[2,33,1024]{2,1,0:T(8,128)} %constant.22.clone.shift, bf16[128,384]{1,0:T(8,128)(2,1)} %constant.23.clone.window), custom_call_target="tpu_custom_call" | custom-call | tf_op jit(solution)/shard_map/transform/pallas_call | solution.py:214
  7.2 0.5 %broadcast.56 = bf16[]{:T(256)} broadcast(bf16[]{:T(256)} %constant.30), dimensions={} | broadcast | bytes 4 | tf_op jit(solution)/shard_map/all_to_all | solution.py:347
  7.7 1.6 %reduce = bf16[8,8320]{1,0:T(8,128)(2,1)S(1)} reduce(bf16[8,1,8320]{2,0,1:T(8,128)(2,1)} %bitcast.16, bf16[]{:T(256)} %broadcast.56), dimensions={1}, to_apply=%copy.11.reduce_sub_computation | reduce | bytes 266242 | tf_op jit(solution)/shard_map/all_to_all | solution.py:347
  9.3 0.8 %reshape.39 = bf16[8,2,4160]{2,1,0:T(2,128)(2,1)} reshape(bf16[8,8320]{1,0:T(8,128)(2,1)S(1)} %reduce) | data formatting | bytes 266240
  10.1 7.3 %all-to-all-start = ((bf16[8,2,4160]{2,1,0:T(2,128)(2,1)}), bf16[8,2,4160]{2,1,0:T(2,128)(2,1)S(1)}, u32[]{:S(2)}, u32[]{:S(2)}) async-start(bf16[8,2,4160]{2,1,0:T(2,128)(2,1)} %reshape.39), calls=%async_computation | async-start | bytes 270336 | tf_op jit(solution)/shard_map/all_to_all | solution.py:347
  17.4 0.7 %convert_bitcast_fusion = f32[4]{0:T(128)S(1)} fusion(s32[4,4]{1,0:T(4,128)} %param.11, s32[]{:T(128)S(6)} %select_n.4), kind=kLoop, calls=%fused_computation.9 | loop fusion | flops 4 | bytes 36 | tf_op jit(solution)/shard_map/convert_element_type | solution.py:353
  18.1 0.1 broadcast_in_dim.3
  18.1 0.1 mul.102
  18.2 6.5 %all-to-all-done = bf16[8,2,4160]{2,1,0:T(2,128)(2,1)S(1)} async-done(((bf16[8,2,4160]{2,1,0:T(2,128)(2,1)}), bf16[8,2,4160]{2,1,0:T(2,128)(2,1)S(1)}, u32[]{:S(2)}, u32[]{:S(2)}) %all-to-all-start) | async-done | bytes 133152 | tf_op jit(solution)/shard_map/all_to_all | solution.py:347
  24.8 0.1 reshape.40
  24.9 0.7 %copy.22 = bf16[8,1,8320]{2,0,1:T(8,128)(2,1)} copy(bf16[8,1,8320]{2,1,0:T(2,128)(2,1)S(1)} %reshape.40) | data formatting | bytes 266240
  25.6 3.4 %spectrum.1 = f32[4,384]{1,0:T(4,128)} custom-call(s32[1]{0:T(128)S(6)} %copy.24.band, s32[1]{0:T(128)} %bitcast.place, s32[2]{0:T(128)} %flags.3, bf16[8,8320]{1,0:T(8,128)(2,1)} %bitcast.17, bf16[128,384]{1,0:T(8,128)(2,1)} %constant.23.clone.window), custom_call_target="tpu_custom_call" | custom-call | tf_op jit(solution)/shard_map/spectrum/pallas_call | solution.py:331
  29.0 0.7 %reshape.34 = f32[2,2,384]{2,1,0:T(2,128)S(1)} reshape(f32[4,384]{1,0:T(4,128)} %spectrum.1) | data formatting | bytes 12288 | tf_op jit(solution)/shard_map/reshape | solution.py:350
  29.7 0.0 copy-start
  29.7 0.7 %copy-done = f32[4,384]{1,0:T(4,128)S(1)} copy-done((f32[4,384]{1,0:T(4,128)S(1)}, f32[4,384]{1,0:T(4,128)}, u32[]{:S(2)}) %copy-start) | copy-done | bytes 6168
  30.4 5.2 %all-gather = f32[4,4,384]{2,1,0:T(4,128)S(1)} all-gather(f32[1,4,384]{2,1,0:T(4,128)S(1)} %bitcast.18), channel_id=1, replica_groups=mesh['tm'=8,'sta'=4] {'sta'}, dimensions={0}, use_global_device_ids=true | all-gather | bytes 30720 | tf_op jit(solution)/shard_map/all_gather | solution.py:349
  35.6 0.0 copy-start.1
  35.7 0.7 %copy-done.1 = f32[2,8,2,384]{3,2,1,0:T(2,128)S(1)} copy-done((f32[2,8,2,384]{3,2,1,0:T(2,128)S(1)}, f32[2,8,2,384]{3,2,1,0:T(2,128)}, u32[]{:S(2)}) %copy-start.1) | copy-done | bytes 49176
  36.4 0.7 %fusion = f32[2,8,2,384]{3,2,1,0:T(2,128)} fusion(f32[2,8,2,384]{3,2,1,0:T(2,128)S(1)} %copy-done.1, f32[2,8,1,384]{3,2,1,0:T(1,128)S(1)} %get-tuple-element.6, f32[2,8,1,384]{3,2,1,0:T(1,128)S(1)} %get-tuple-element.5, f32[8]{0:T(128)S(1)} %mul.102), kind=kLoop, calls=%fused_computation.2 | loop fusion | flops 36864 | bytes 147488 | tf_op jit(solution)/shard_map/add | solution.py:357
  (6 shorter events, 0.1 us)
Async XLA Ops:
  10.1 14.7 %all-to-all-start = ((bf16[8,2,4160]{2,1,0:T(2,128)(2,1)}), bf16[8,2,4160]{2,1,0:T(2,128)(2,1)S(1)}, u32[]{:S(2)}, u32[]{:S(2)}) async-start(bf16[8,2,4160]{2,1,0:T(2,128)(2,1)} %reshape.39), calls=%async_computation | async-start | bytes 270336 | tf_op jit(solution)/shard_map/all_to_all | solution.py:347
  29.7 0.7 %copy-start = (f32[4,384]{1,0:T(4,128)S(1)}, f32[4,384]{1,0:T(4,128)}, u32[]{:S(2)}) copy-start(f32[4,384]{1,0:T(4,128)} %spectrum.1) | copy-start | bytes 18436
  35.6 0.8 %copy-start.1 = (f32[2,8,2,384]{3,2,1,0:T(2,128)S(1)}, f32[2,8,2,384]{3,2,1,0:T(2,128)}, u32[]{:S(2)}) copy-start(f32[2,8,2,384]{3,2,1,0:T(2,128)} %param.13) | copy-start | bytes 147460
where the time goes:
time: 37.6 us; the launch traced here: 37.2 us
  Pallas kernels  9.93 us (26%)
  starting transfers between devices  7.31 us (19%)
  waiting for transfers between devices  6.53 us (17%)
  blocking collectives  5.2 us (14%)
  local copies, waits for them, and re-layouts  4.45 us (12%)
  other arithmetic  3.02 us (8%)
  between operations  0.71 us (2%)
    all_to_all x1, starting transfers between devices, shards(): got = lax.all_to_all(sent, 'tm', split_axis=0, concat_axis=0, tiled=True)  7.31 us
    pallas_call x1, Pallas kernels, transform(): pl.pallas_call(functools.partial(transform_kernel, z), grid=(z.blocks,),...  6.54 us
    all_to_all x1, waiting for transfers between devices, shards(): got = lax.all_to_all(sent, 'tm', split_axis=0, concat_axis=0, tiled=True)  6.53 us
    all_gather x1, blocking collectives, shards(): lax.all_gather(white, 'sta', axis=0, tiled=True).reshape(-1, 2, z.bins)  5.2 us
    pallas_call x1, Pallas kernels, spectrum(): pl.pallas_call(functools.partial(spectrum_kernel, z), in_specs=[smem, sme...  3.39 us
    unnamed x9, local copies, waits for them, and re-layouts  3.03 us
    all_to_all x1, other arithmetic, shards(): got = lax.all_to_all(sent, 'tm', split_axis=0, concat_axis=0, tiled=True)  1.58 us
  transfers between devices with their start and end apart: 1, of which 1 were waited for; matrix products, arithmetic and copies ran while one was open for 2% of the time, Pallas kernels for 0%

commit v1 on v0

v1 whole, which is shorter than its diff:
```python
import functools
import math

import jax
import jax.numpy as jnp
import numpy as np
from jax import lax
from jax.experimental import pallas as pl
from jax.experimental.pallas import tpu as pltpu
from jax.sharding import PartitionSpec as P

HALF_WIN = 512
SMOOTH = 32
EPS_MEAN = 1e-06
EPS_POWER = 1e-06
LANES = 128
SPAN = 2 * HALF_WIN
TILES = SPAN // LANES
HALF_TILES = HALF_WIN // LANES
PAD = 16
VMEM_LIMIT = 16 * 1024 * 1024
BF = jnp.bfloat16
F32 = jnp.float32


def up_to(value, step):
    return -(-value // step) * step


def sincos(turns):
    quarter = jnp.round(turns * 4.0)
    rest = turns - quarter * 0.25
    y = rest * (2.0 * math.pi)
    y2 = y * y
    s = y + y * y2 * (-1.0 / 6 + y2 * (1.0 / 120 + y2 * (-1.0 / 5040 + y2 * (1.0 / 362880))))
    c = 1.0 + y2 * (-0.5 + y2 * (1.0 / 24 + y2 * (-1.0 / 720 + y2 * (1.0 / 40320))))
    q = quarter - 4.0 * jnp.floor(quarter * 0.25)
    swap = (q == 1.0) | (q == 3.0)
    sine = jnp.where(swap, c, s)
    cosine = jnp.where(swap, s, c)
    sine = jnp.where(q >= 2.0, -sine, sine)
    cosine = jnp.where((q == 1.0) | (q == 2.0), -cosine, cosine)
    return sine, cosine


def turns_of(product, period):
    whole = jnp.floor(product * (1.0 / period))
    return (product - whole * period) * (1.0 / period)


def split2(value):
    high = value.astype(BF)
    return high, (value - high.astype(F32)).astype(BF)


def iota(shape, axis):
    return lax.broadcasted_iota(jnp.int32, shape, axis)


def iota_f(shape, axis):
    return iota(shape, axis).astype(F32)


def window_tables():
    row, lane = iota((LANES, LANES), 0), iota((LANES, LANES), 1)
    upto = (row <= lane).astype(F32).astype(BF)
    onward = (row >= lane).astype(F32).astype(BF)
    return upto, onward, jnp.ones((LANES, LANES), BF)


def np_split(value):
    high = value.astype(jnp.bfloat16).astype(np.float64)
    return high, (value - high).astype(jnp.bfloat16).astype(np.float64)


class Sizes:
    def __init__(self, stations, length, tm_count, bins):
        self.stations, self.length, self.tm, self.bins = stations, length, tm_count, bins
        self.rows = length // SPAN
        self.half = self.rows // 2 + 1
        self.pad = up_to(self.rows, PAD)
        self.block = min(tm_count, 16)
        self.blocks = tm_count // self.block
        self.folds = -(-(bins + self.rows - 1) // self.rows)
        self.spec_rows = up_to(2 * self.half, 8)
        self.edge_rows = 2 * stations * TILES
        self.sent_rows = self.spec_rows + self.edge_rows
        assert length % SPAN == 0 and tm_count % self.block == 0
        assert stations == 2 and self.folds <= PAD
        assert self.rows >= 2 and 4 * self.pad <= 256

    def first_table(self):
        j2 = np.arange(self.tm)[:, None] + self.tm * np.arange(self.half)[None, :]
        j2 = j2.reshape(self.blocks, self.block, self.half).transpose(0, 2, 1).reshape(self.blocks, -1)
        period = self.tm * self.rows
        angle = 2.0 * np.pi / period * (j2[:, :, None] * np.arange(self.rows) % period)
        parts = np.concatenate([np.cos(angle), -np.sin(angle)], axis=1)
        parts = np.pad(parts, ((0, 0), (0, 0), (0, self.pad - self.rows)))
        high, low = np_split(parts)
        return np.concatenate([high, high, low, low], axis=2).astype(jnp.bfloat16)

    def shift_table(self):
        angle = 2.0 * np.pi / self.length * (
            np.arange(self.half)[:, None] * np.arange(SPAN)[None, :] % self.length
        )
        return np.stack([np.cos(angle), -np.sin(angle)]).astype(np.float32)


def normalize(z, flags, x, xs, wide, stack, edges):
    rows, pad, top = z.rows, z.pad, 8
    full = rows // 8 * 8
    for s in range(z.stations):
        xs[s, 0:top, :] = jnp.zeros((top, SPAN), F32)
        xs[s, top + full : top + pad + 8, :] = jnp.zeros((pad + 8 - full, SPAN), F32)
    for a in range(rows):
        xs[:, top + a, :] = x[:, a * SPAN : (a + 1) * SPAN].astype(F32)
    for s in range(z.stations):
        for side, a in ((0, 0), (1, rows - 1)):
            for c in range(TILES):
                at = (side * z.stations + s) * TILES + c
                edges[at : at + 1, :] = xs[s, top + a : top + a + 1, c * LANES : (c + 1) * LANES]
    upto, onward, ones = window_tables()
    kernel = jnp.concatenate([onward] + [ones] * (2 * HALF_TILES - 1) + [upto], axis=0)
    row = iota((pad, LANES), 0)
    for s in range(z.stations):
        for turn, (lo, hi) in ((-1, (HALF_WIN, SPAN)), (0, (0, SPAN)), (1, (0, HALF_WIN))):
            at = HALF_WIN + turn * SPAN + lo
            wide[s, :, at : at + hi - lo] = jnp.abs(
                xs[s, top + turn : top + turn + pad, lo:hi]
            ).astype(BF)
        for c in range(TILES):
            here = wide[s, :, c * LANES : c * LANES + SPAN + LANES]
            total = jnp.dot(here, kernel, preferred_element_type=F32)
            value = xs[s, top : top + pad, c * LANES : (c + 1) * LANES] * flags[s].astype(F32)
            value = value / (total * (1.0 / (2 * HALF_WIN + 1)) + EPS_MEAN)
            edge = 0 if c < HALF_TILES else rows - 1
            high, low = split2(jnp.where(row == edge, 0.0, value))
            for k, part in enumerate((high, low, high, low)):
                stack[s, k * pad : (k + 1) * pad, c * LANES : (c + 1) * LANES] = part


def fold_weights(z, band, weight):
    for kind in range(2):
        order = iota((PAD, SPAN), 0) + (band[0] // z.rows + kind)
        turns = jnp.bitwise_and(order * iota((PAD, SPAN), 1), SPAN - 1).astype(F32) * (1.0 / SPAN)
        sine, cosine = sincos(turns)
        for h, (s, c) in enumerate(zip(split2(sine), split2(cosine))):
            table = ((c, s), (-s, c)) if kind == 0 else ((c, -s), (-s, -c))
            for part in range(2):
                at = h * 4 * PAD + kind * 2 * PAD + part * PAD
                weight[at : at + PAD, 0:SPAN] = table[part][0]
                weight[at : at + PAD, SPAN : 2 * SPAN] = table[part][1]


def transform_kernel(
    z, band, place, flags, x, first, shift, out, xs, wide, stack, edges, weight, acc, both, spec
):
    half, block, tm = z.half, z.block, z.tm
    height = half * block
    index = pl.program_id(0)

    def prologue():
        normalize(z, flags, x, xs, wide, stack, edges)
        fold_weights(z, band, weight)
        spec[:, z.spec_rows - 8 : z.spec_rows, :] = jnp.zeros((tm, 8, LANES), F32)

    if z.blocks == 1:
        prologue()
    else:
        pl.when(index == 0)(prologue)
    acc[...] = jnp.zeros_like(acc)
    width = 256
    residue = index * block + iota((block, width), 0)
    start = turns_of((place[0] * residue).astype(F32), tm)

    def step(c, carry):
        lanes = pl.ds(pl.multiple_of(c * width, width), width)
        lanes_im = pl.ds(pl.multiple_of(SPAN + c * width, width), width)
        offset = c * width + iota((block, width), 1)
        turn = start + (residue * offset).astype(F32) * (1.0 / (tm * z.length))
        sn, cs = sincos(turn)
        r_re, r_im = cs[None], -sn[None]
        m_re = shift[0, :, lanes][:, None, :]
        m_im = shift[1, :, lanes][:, None, :]
        t_re = (m_re * r_re - m_im * r_im).reshape(height, width)
        t_im = (m_re * r_im + m_im * r_re).reshape(height, width)
        w = jnp.concatenate([weight[:, lanes], weight[:, lanes_im]] * 2, axis=1)
        for s in range(z.stations):
            f = jnp.dot(first[0], stack[s, :, lanes], preferred_element_type=F32)
            f_re, f_im = f[:height], f[height:]
            re_h, re_l = split2(f_re * t_re - f_im * t_im)
            im_h, im_l = split2(f_re * t_im + f_im * t_re)
            value = jnp.concatenate([re_h, im_h, re_l, im_l], axis=1)
            acc[s] += lax.dot_general(
                value, w, (((1,), (1,)), ((), ())), preferred_element_type=F32
            )
        return carry

    lax.fori_loop(0, SPAN // width, step, 0)
    zero, one = (acc[s] + pltpu.roll(acc[s], LANES // 2, 1) for s in range(2))
    lane = iota((height, LANES), 1)
    early = jnp.bitwise_and(lane, LANES // 2 - 1) < LANES // 4
    direct = jnp.where(early, zero, pltpu.roll(one, LANES // 4, 1))
    mirror = jnp.where(early, pltpu.roll(zero, LANES // 4, 1), one)
    for kind, value in enumerate((direct, mirror)):
        high = value.astype(BF).astype(F32)
        both[kind] = jnp.where(lane < LANES // 2, high, value - high)
    for k in range(block):
        here = index * block + k
        there = jnp.where(here == 0, 0, tm - here) if z.blocks > 1 else (tm - k) % tm
        here = here if z.blocks > 1 else k
        rows = pl.ds(k, half, stride=block)
        spec[here, 0:half, :] = both[0, rows, :]
        spec[there, half : 2 * half, :] = both[1, rows, :]

    def finish():
        ends = edges[...].astype(BF)

        def one_row(k, carry):
            out[k, 0 : z.spec_rows, :] = spec[k].astype(BF)
            out[k, z.spec_rows : z.sent_rows, :] = ends
            return carry

        if z.blocks == 1:
            for k in range(tm):
                one_row(k, 0)
        else:
            lax.fori_loop(0, tm, one_row, 0)

    if z.blocks == 1:
        finish()
    else:
        pl.when(index == z.blocks - 1)(finish)


SMEM_SPEC = pl.BlockSpec(memory_space=pltpu.SMEM)
VMEM_SPEC = pl.BlockSpec(memory_space=pltpu.VMEM)


def params():
    return pltpu.CompilerParams(vmem_limit_bytes=VMEM_LIMIT)


def transform(z, band, place, flags, x):
    width = 4 * z.pad
    height = z.half * z.block
    return pl.pallas_call(
        functools.partial(transform_kernel, z),
        grid=(z.blocks,),
        in_specs=[
            SMEM_SPEC,
            SMEM_SPEC,
            SMEM_SPEC,
            VMEM_SPEC,
            pl.BlockSpec((1, 2 * height, width), lambda i: (i, 0, 0)),
            VMEM_SPEC,
        ],
        out_specs=VMEM_SPEC,
        out_shape=jax.ShapeDtypeStruct((z.tm, z.sent_rows, LANES), BF),
        scratch_shapes=[
            pltpu.VMEM((z.stations, 16 + z.pad, SPAN), F32),
            pltpu.VMEM((z.stations, z.pad, 2 * SPAN), BF),
            pltpu.VMEM((z.stations, width, SPAN), BF),
            pltpu.VMEM((z.edge_rows, LANES), F32),
            pltpu.VMEM((LANES, 2 * SPAN), BF),
            pltpu.VMEM((z.stations, height, LANES), F32),
            pltpu.VMEM((2, height, LANES), F32),
            pltpu.VMEM((z.tm, z.spec_rows, LANES), F32),
        ],
        compiler_params=params(),
        name="transform",
    )(band, place, flags, x, jnp.asarray(z.first_table()), jnp.asarray(z.shift_table()))


def table_kernel(z, band, place, choose, keep, steps, turns, near, phase):
    rows, tm, bins, half = z.rows, z.tm, z.bins, z.half
    base, residue = band[0], place[0]
    spot = iota_f((1, bins), 1) + (base % rows).astype(F32)
    fold = jnp.floor((spot + 0.5) * (1.0 / rows))
    rest = spot - fold * rows
    row = iota_f((z.spec_rows, bins), 0)
    last = (rows - 1 + half + (residue == 0).astype(jnp.int32)).astype(F32)
    mirror = last - row
    target = jnp.where(row < half, row, jnp.where(mirror >= half, mirror, -1.0))
    one = (target == rest).astype(F32).astype(BF)
    for p in range(tm):
        choose[p] = one
    keep[...] = (iota_f((PAD, bins), 0) == fold).astype(F32)
    freq = (residue + tm * (base + iota((1, bins), 1))).astype(F32)
    step = iota_f((TILES, bins), 0) - HALF_TILES
    sine, cosine = sincos(turns_of(step * freq, tm * (z.length // LANES)))
    table = jnp.concatenate(
        [jnp.concatenate([cosine, -sine], axis=1), jnp.concatenate([sine, cosine], axis=1)], axis=0
    )
    high, low = split2(table)
    for k, part in enumerate((high, high, low, low)):
        steps[k * 2 * TILES : (k + 1) * 2 * TILES, :] = part
    sine, cosine = sincos(turns_of(iota_f((LANES, bins), 0) * freq, tm * z.length))
    turns[0] = cosine
    turns[1] = sine
    gap = jnp.abs(iota((bins, bins), 0) - iota((bins, bins), 1))
    near[...] = (gap <= SMOOTH).astype(F32).astype(BF)
    p_sin, p_cos = sincos(turns_of((residue * iota((tm, LANES), 0)).astype(F32), tm))
    phase[0] = p_cos
    phase[1] = -p_sin


def tables(z, band, place):
    return pl.pallas_call(
        functools.partial(table_kernel, z),
        in_specs=[SMEM_SPEC, SMEM_SPEC],
        out_specs=[VMEM_SPEC] * 6,
        out_shape=[
            jax.ShapeDtypeStruct((z.tm, z.spec_rows, z.bins), BF),
            jax.ShapeDtypeStruct((PAD, z.bins), F32),
            jax.ShapeDtypeStruct((8 * TILES, 2 * z.bins), BF),
            jax.ShapeDtypeStruct((2, LANES, z.bins), F32),
            jax.ShapeDtypeStruct((z.bins, z.bins), BF),
            jax.ShapeDtypeStruct((2, z.tm, LANES), F32),
        ],
        compiler_params=params(),
        cost_estimate=pl.CostEstimate(flops=4000000, bytes_accessed=2000000, transcendentals=0),
        name="tables",
    )(band, place)


def sublane_sums(value, row):
    total = value
    for shift in (1, 2, 4):
        total = total + jnp.where(row >= shift, pltpu.roll(total, shift, 0), 0.0)
    return total - value, total


def spectrum_kernel(z, flags, got, choose, keep, steps, turns, near, phase, out):
    tm, bins, at = z.tm, z.bins, z.spec_rows
    parts = got[:, 0:at, :].astype(F32).reshape(tm * at, LANES).astype(BF)
    weights = choose[...].astype(F32).reshape(tm * at, bins).astype(BF)
    placed = lax.dot_general(parts, weights, (((0,), (0,)), ((), ())), preferred_element_type=F32)
    mask = keep[...]
    folded = [
        jnp.sum(placed[k * PAD : (k + 1) * PAD] * mask, axis=0, keepdims=True)
        for k in range(4 * z.stations)
    ]
    spec = [folded[k] + folded[k + 2 * z.stations] for k in range(2 * z.stations)]
    upto, onward, ones = window_tables()
    row = iota((TILES, LANES), 0)
    late = row >= HALF_TILES
    sides = []
    side_rows = z.stations * TILES
    for side, table in ((0, upto), (1, onward)):
        rows = slice(at + side * side_rows, at + (side + 1) * side_rows)
        value = got[:, rows, :].astype(F32).reshape(tm * side_rows, LANES)
        sums = jnp.dot(
            jnp.abs(value).astype(BF),
            jnp.concatenate([table, ones], axis=1),
            preferred_element_type=F32,
        )
        sides.append((value, sums))
    mixed = []
    for s in range(z.stations):
        real = jnp.zeros((TILES, LANES), F32)
        imag = jnp.zeros((TILES, LANES), F32)
        flag = flags[s].astype(F32)
        for p in range(tm):
            begin = (p * z.stations + s) * TILES
            before = ((p - 1) % tm * z.stations + s) * TILES
            value_r, sums_r = (v[begin : begin + TILES] for v in sides[0])
            value_l, sums_l = (v[before : before + TILES] for v in sides[1])
            earlier, _ = sublane_sums(sums_r[:, LANES:], row)
            right = sums_r[:, :LANES] + earlier
            tail = sums_l[:, LANES:]
            for shift in (1, 2, 4):
                tail = tail + jnp.where(row < TILES - shift, pltpu.roll(tail, TILES - shift, 0), 0.0)
            left = sums_l[:, :LANES] + jnp.where(
                row < TILES - 1, pltpu.roll(tail, TILES - 1, 0), 0.0
            )
            total = left + right if p else jnp.where(late, right, left)
            sample = pltpu.roll(jnp.where(late, value_l, value_r), HALF_TILES, 0)
            value = flag * sample / (total * (1.0 / (2 * HALF_WIN + 1)) + EPS_MEAN)
            real = real + value * phase[0, p : p + 1, :]
            imag = imag + value * phase[1, p : p + 1, :]
        mixed.append(jnp.concatenate([real, imag], axis=0))
    high, low = split2(jnp.concatenate(mixed, axis=1))
    spread = lax.dot_general(
        jnp.concatenate([high, low, high, low], axis=0),
        steps[...],
        (((0,), (0,)), ((), ())),
        preferred_element_type=F32,
    )
    cosine, sine = turns[0], turns[1]
    pieces = []
    for s in range(z.stations):
        g_re = spread[s * LANES : (s + 1) * LANES, :bins]
        g_im = spread[s * LANES : (s + 1) * LANES, bins:]
        spec[2 * s] += jnp.sum(g_re * cosine + g_im * sine, axis=0, keepdims=True)
        spec[2 * s + 1] += jnp.sum(g_im * cosine - g_re * sine, axis=0, keepdims=True)
        power = spec[2 * s] * spec[2 * s] + spec[2 * s + 1] * spec[2 * s + 1]
        for _ in range(3):
            part = power.astype(BF).astype(F32)
            pieces.append(part)
            power = power - part
    pieces.append(jnp.zeros((8 - len(pieces), bins), F32))
    smooth = jnp.dot(
        jnp.concatenate(pieces, axis=0).astype(BF), near[...], preferred_element_type=F32
    )
    for s in range(z.stations):
        mean = smooth[3 * s : 3 * s + 1] + smooth[3 * s + 1 : 3 * s + 2] + smooth[3 * s + 2 : 3 * s + 3]
        scale = 1.0 / jnp.sqrt(mean * (1.0 / (2 * SMOOTH + 1)) + EPS_POWER)
        out[2 * s : 2 * s + 1, :] = spec[2 * s] * scale
        out[2 * s + 1 : 2 * s + 2, :] = spec[2 * s + 1] * scale


def spectrum(z, flags, got, made):
    return pl.pallas_call(
        functools.partial(spectrum_kernel, z),
        in_specs=[SMEM_SPEC] + [VMEM_SPEC] * 7,
        out_specs=VMEM_SPEC,
        out_shape=jax.ShapeDtypeStruct((2 * z.stations, z.bins), F32),
        compiler_params=params(),
        name="spectrum",
    )(flags, got, *made)


def cross_kernel(z, offsets, mask, where, stacks, *refs):
    pieces, out = refs[:-1], refs[-1]
    here = where[0]
    mine = pieces[0][...]
    bins = z.bins
    sides = []
    for i in range(z.stations):
        re, im = mine[2 * i : 2 * i + 1], mine[2 * i + 1 : 2 * i + 2]
        sides.append((jnp.concatenate([re, im], axis=0), jnp.concatenate([im, -re], axis=0)))
    for offset, piece in zip(offsets, pieces):
        source = here ^ offset
        on = mask[here, source].astype(F32)
        for j in range(z.stations):
            re = jnp.broadcast_to(piece[2 * j : 2 * j + 1, :] * on, (2, bins))
            im = jnp.broadcast_to(piece[2 * j + 1 : 2 * j + 2, :] * on, (2, bins))
            column = source * z.stations + j
            for i, (p, q) in enumerate(sides):
                out[i, column] = stacks[i, column] + (re * p + im * q)


def cross(z, offsets, mask, where, stacks, pieces):
    return pl.pallas_call(
        functools.partial(cross_kernel, z, offsets),
        in_specs=[SMEM_SPEC, SMEM_SPEC] + [VMEM_SPEC] * (1 + len(pieces)),
        out_specs=VMEM_SPEC,
        out_shape=jax.ShapeDtypeStruct(stacks.shape, F32),
        compiler_params=params(),
        name="cross",
    )(mask, where, stacks, *pieces)


def shards(traces, station_flags, tile_mask, band_block, stacks):
    tm_count, sta_count = lax.axis_size("tm"), lax.axis_size("sta")
    stations, length = traces.shape
    z = Sizes(stations, length, tm_count, stacks.shape[-1])
    assert sta_count & (sta_count - 1) == 0
    place = lax.axis_index("tm").astype(jnp.int32).reshape(1)
    where = lax.axis_index("sta").astype(jnp.int32).reshape(1)
    sent = transform(z, band_block, place, station_flags, traces)
    got = lax.all_to_all(sent, "tm", split_axis=0, concat_axis=0, tiled=True)
    made = tables(z, band_block, place)
    white = spectrum(z, station_flags, got, made)
    offsets, pieces = [0], [white]
    bit = sta_count // 2
    while bit:
        pairs = [(i, i ^ bit) for i in range(sta_count)]
        pieces += [lax.ppermute(piece, "sta", pairs) for piece in pieces]
        offsets += [offset ^ bit for offset in offsets]
        bit //= 2
    return cross(z, offsets, tile_mask, where, stacks, pieces)


def solution(mesh):
    return jax.shard_map(
        shards,
        mesh=mesh,
        in_specs=(P("sta", "tm"), P("sta"), P(), P(), P("sta", None, None, "tm")),
        out_specs=P("sta", None, None, "tm"),
        check_vma=False,
    )
```

time: 37.6 us -> 31.9 us (0.85)
  blocking collectives: 5.2 us -> 0 us
  waiting for transfers between devices: 6.53 us -> 10.3 us
  other arithmetic: 3.02 us -> 0 us
  starting transfers between devices: 7.31 us -> 8.88 us
  Pallas kernels: 9.93 us -> 8.38 us
  local copies, waits for them, and re-layouts: 4.45 us -> 3.39 us
    all_gather x1 -> x0, blocking collectives: 5.2 us -> none  [shards(): lax.all_gather(white, 'sta', axis=0, tiled=True).reshape(-1, 2, z.bins)]
    ppermute x0 -> x3, waiting for transfers between devices: none -> 3.29 us  [shards(): pieces += [lax.ppermute(piece, 'sta', pairs) for piece in pieces]]
    all_to_all x1 -> x0, other arithmetic: 1.58 us -> none  [shards(): got = lax.all_to_all(sent, 'tm', split_axis=0, concat_axis=0, tiled=True)]
    ppermute x0 -> x3, starting transfers between devices: none -> 1.57 us  [shards(): pieces += [lax.ppermute(piece, 'sta', pairs) for piece in pieces]]
    pallas_call x1, Pallas kernels: 6.54 us -> 5.33 us  [transform(): pl.pallas_call(functools.partial(transform_kernel, z), grid=(z.blocks,),...]
    add x2 -> x0, other arithmetic: 0.75 us -> none  [the longest x1 0.71 us: shards(): stacks + jnp.stack([cross_real, cross_imag], axis=2) * column_mask[None,...]
    reshape x2 -> x0, local copies, waits for them, and re-layouts: 0.73 us -> none  [the longest x1 0.71 us: shards(): mine = white.reshape(stations, 2, z.bins)]
    convert_element_type x1 -> x0, other arithmetic: 0.69 us -> none  [shards(): lax.dynamic_index_in_dim(tile_mask, sta_here, 0, keepdims=False).astype(F32)]
  transfers between devices with their start and end apart: 1 -> 4, of which waited for: 1 -> 3; matrix products, arithmetic and copies ran while one was open for 2% -> 0% of each run, Pallas kernels for 0% -> 1%
where the time goes in v1:
time: 31.9 us; the launch traced here: 31.6 us
  waiting for transfers between devices  10.3 us (32%)
  starting transfers between devices  8.88 us (28%)
  Pallas kernels  8.38 us (26%)
  local copies, waits for them, and re-layouts  3.39 us (11%)
  between operations  0.68 us (2%)
    all_to_all x1, starting transfers between devices, shards(): got = lax.all_to_all(sent, 'tm', split_axis=0, concat_axis=0, tiled=True)  7.31 us
    all_to_all x1, waiting for transfers between devices, shards(): got = lax.all_to_all(sent, 'tm', split_axis=0, concat_axis=0, tiled=True)  7.02 us
    pallas_call x1, Pallas kernels, transform(): pl.pallas_call(functools.partial(transform_kernel, z), grid=(z.blocks,),...  5.33 us
    unnamed x12, local copies, waits for them, and re-layouts  3.39 us
    ppermute x3, waiting for transfers between devices, shards(): pieces += [lax.ppermute(piece, 'sta', pairs) for piece in pieces]  3.29 us
    ppermute x3, starting transfers between devices, shards(): pieces += [lax.ppermute(piece, 'sta', pairs) for piece in pieces]  1.57 us
    pallas_call x1, Pallas kernels, spectrum(): pl.pallas_call(functools.partial(spectrum_kernel, z), in_specs=[SMEM_SPEC...  1.38 us
    pallas_call x1, Pallas kernels, cross(): pl.pallas_call(functools.partial(cross_kernel, z, offsets), in_specs=[SME...  1.24 us
  transfers between devices with their start and end apart: 4, of which 3 were waited for; matrix products, arithmetic and copies ran while one was open for 0% of the time, Pallas kernels for 1%

profile of v1, /device:TPU:0, one launch (start us, length us, event | category | flops | bytes accessed | tf_op | source)
XLA Modules:
  0.0 31.6 jit_solution(12458888421311768290)
XLA Ops:
  0.7 0.0 copy-start.5
  0.7 0.6 %copy-done.5 = s32[2]{0:T(128)S(1)} copy-done((s32[2]{0:T(128)S(1)}, s32[2]{0:T(128)}, u32[]{:S(2)}) %copy-start.5) | copy-done | bytes 32
  1.3 0.0 copy-start
  1.3 0.9 %copy-done = f32[2,17,1024]{2,1,0:T(8,128)S(1)} copy-done((f32[2,17,1024]{2,1,0:T(8,128)S(1)}, f32[2,17,1024]{2,1,0:T(8,128)}, u32[]{:S(2)}) %copy-start) | copy-done | bytes 139288
  2.2 0.0 copy-start.1
  2.2 0.9 %copy-done.1 = bf16[1,272,192]{2,1,0:T(8,128)(2,1)S(1)} copy-done((bf16[1,272,192]{2,1,0:T(8,128)(2,1)S(1)}, bf16[1,272,192]{2,1,0:T(8,128)(2,1)}, u32[]{:S(2)}) %copy-start.1) | copy-done | bytes 104472
  3.1 0.0 copy-start.2
  3.1 0.9 %copy-done.2 = bf16[2,33792]{1,0:T(2,128)(2,1)S(1)} copy-done((bf16[2,33792]{1,0:T(2,128)(2,1)S(1)}, bf16[2,33792]{1,0:T(2,128)(2,1)}, u32[]{:S(2)}) %copy-start.2) | copy-done | bytes 135192
  4.0 5.3 %transform.1 = bf16[8,72,128]{2,1,0:T(8,128)(2,1)} custom-call(s32[1]{0:T(128)S(6)} %copy.8.band, s32[1]{0:T(128)} %bitcast.1.place, s32[2]{0:T(128)S(1)} %copy-done.5, bf16[2,33792]{1,0:T(2,128)(2,1)S(1)} %copy-done.2, bf16[1,272,192]{2,1,0:T(8,128)(2,1)S(1)} %copy-done.1, f32[2,17,1024]{2,1,0:T(8,128)S(1)} %copy-done), custom_call_target="tpu_custom_call" | custom-call | tf_op jit(solution)/shard_map/transform/pallas_call | solution.py:247
  9.4 7.3 %all-to-all-start = ((bf16[8,72,128]{2,1,0:T(8,128)(2,1)}), bf16[8,72,128]{2,1,0:T(8,128)(2,1)S(1)}, u32[]{:S(2)}, u32[]{:S(2)}) async-start(bf16[8,72,128]{2,1,0:T(8,128)(2,1)} %transform.1), calls=%async_computation | async-start | bytes 294912 | tf_op jit(solution)/shard_map/all_to_all | solution.py:463
  16.7 0.4 %tables.1 = (bf16[8,40,384]{2,1,0:T(8,128)(2,1)S(1)}, f32[16,384]{1,0:T(8,128)S(1)}, bf16[64,768]{1,0:T(8,128)(2,1)S(1)}, f32[2,128,384]{2,1,0:T(8,128)S(1)}, bf...) custom-call(s32[1]{0:T(128)S(6)} %copy.8.band, s32[1]{0:T(128)} %bitcast.1.place), custom_call_target="tpu_custom_call" | custom-call | flops 4000000 | bytes 2000000 | tf_op jit(solution)/shard_map/tables/pallas_call | solution.py:309
  17.1 7.0 %all-to-all-done.got = bf16[8,72,128]{2,1,0:T(8,128)(2,1)S(1)} async-done(((bf16[8,72,128]{2,1,0:T(8,128)(2,1)}), bf16[8,72,128]{2,1,0:T(8,128)(2,1)S(1)}, u32[]{:S(2)}, u32[]{:S(2)}) %all-to-all-start) | async-done | bytes 147488 | tf_op jit(solution)/shard_map/all_to_all | solution.py:463
  24.1 0.0 copy-start.3
  24.2 1.4 %spectrum.1.refs_0_ = f32[4,384]{1,0:T(4,128)S(1)} custom-call(s32[2]{0:T(128)S(1)} %copy-done.5, bf16[8,72,128]{2,1,0:T(8,128)(2,1)S(1)} %all-to-all-done.got, bf16[8,40,384]{2,1,0:T(8,128)(2,1)S(1)} %get-tuple-element.11.choose, f32[16,384]{1,0:T(8,128)S(1)} %get-tuple-element.12.keep, bf16[64,768]{1,0:T(8,128)(2,1)S(1)} %get-tuple-element.13.steps, ...), custom_call_target="tpu_custom_call" | custom-call | tf_op jit(solution)/shard_map/spectrum/pallas_call | solution.py:414
  25.5 1.6 %collective-permute-start = (f32[4,384]{1,0:T(4,128)S(1)}, f32[4,384]{1,0:T(4,128)S(1)}, u32[]{:S(2)}, u32[]{:S(2)}) collective-permute-start(f32[4,384]{1,0:T(4,128)S(1)} %spectrum.1.refs_0_), channel_id=1, source_target_pairs={{0,2},{1,3},{2,0},{3,1},{4,6},{5,7},{6,4},{7,5},{8,10},{9,11},{10,... | collective-permute-start | bytes 18440 | tf_op jit(solution)/shard_map/ppermute | solution.py:470
  27.1 0.0 collective-permute-start.1
  27.1 2.1 %collective-permute-done.refs_1_ = f32[4,384]{1,0:T(4,128)S(1)} collective-permute-done((f32[4,384]{1,0:T(4,128)S(1)}, f32[4,384]{1,0:T(4,128)S(1)}, u32[]{:S(2)}, u32[]{:S(2)}) %collective-permute-start) | collective-permute-done | bytes 6176 | tf_op jit(solution)/shard_map/ppermute | solution.py:470
  29.2 0.0 collective-permute-start.2
  29.2 0.0 copy-start.4
  29.2 0.0 collective-permute-done.1.refs_2_
  29.2 1.2 %collective-permute-done.2.refs_3_ = f32[4,384]{1,0:T(4,128)S(1)} collective-permute-done((f32[4,384]{1,0:T(4,128)S(1)}, f32[4,384]{1,0:T(4,128)S(1)}, u32[]{:S(2)}, u32[]{:S(2)}) %collective-permute-start.2) | collective-permute-done | bytes 6176 | tf_op jit(solution)/shard_map/ppermute | solution.py:470
  30.4 0.0 copy-done.3
  30.4 0.0 copy-done.4
  30.4 1.2 %cross.1 = f32[2,8,2,384]{3,2,1,0:T(2,128)} custom-call(s32[4,4]{1,0:T(4,128)S(1)} %copy-done.4, s32[1]{0:T(128)} %bitcast.where, f32[2,8,2,384]{3,2,1,0:T(2,128)S(1)} %copy-done.3, f32[4,384]{1,0:T(4,128)S(1)} %spectrum.1.refs_0_, f32[4,384]{1,0:T(4,128)S(1)} %collective-permute-done.refs_1_, f32[4,384]{1,0:T(4,128)S(1)} %collective-permute-done.1.refs_2_, ...), custom_call_target="tpu_custom_call" | custom-call | tf_op jit(solution)/shard_map/cross/pallas_call | solution.py:445
Async XLA Ops:
  0.7 0.7 %copy-start.5 = (s32[2]{0:T(128)S(1)}, s32[2]{0:T(128)}, u32[]{:S(2)}) copy-start(s32[2]{0:T(128)} %flags.3) | copy-start | bytes 28
  1.3 0.9 %copy-start = (f32[2,17,1024]{2,1,0:T(8,128)S(1)}, f32[2,17,1024]{2,1,0:T(8,128)}, u32[]{:S(2)}) copy-start(f32[2,17,1024]{2,1,0:T(8,128)} %constant.14.clone.shift) | copy-start | bytes 417796
  2.2 0.9 %copy-start.1 = (bf16[1,272,192]{2,1,0:T(8,128)(2,1)S(1)}, bf16[1,272,192]{2,1,0:T(8,128)(2,1)}, u32[]{:S(2)}) copy-start(bf16[1,272,192]{2,1,0:T(8,128)(2,1)} %constant.13.clone.first) | copy-start | bytes 313348
  3.1 0.9 %copy-start.2 = (bf16[2,33792]{1,0:T(2,128)(2,1)S(1)}, bf16[2,33792]{1,0:T(2,128)(2,1)}, u32[]{:S(2)}) copy-start(bf16[2,33792]{1,0:T(2,128)(2,1)} %x.1) | copy-start | bytes 405508
  9.4 14.8 %all-to-all-start = ((bf16[8,72,128]{2,1,0:T(8,128)(2,1)}), bf16[8,72,128]{2,1,0:T(8,128)(2,1)S(1)}, u32[]{:S(2)}, u32[]{:S(2)}) async-start(bf16[8,72,128]{2,1,0:T(8,128)(2,1)} %transform.1), calls=%async_computation | async-start | bytes 294912 | tf_op jit(solution)/shard_map/all_to_all | solution.py:463
  24.1 6.3 %copy-start.3 = (f32[2,8,2,384]{3,2,1,0:T(2,128)S(1)}, f32[2,8,2,384]{3,2,1,0:T(2,128)}, u32[]{:S(2)}) copy-start(f32[2,8,2,384]{3,2,1,0:T(2,128)} %stacks.1) | copy-start | bytes 147460
  25.5 3.7 %collective-permute-start = (f32[4,384]{1,0:T(4,128)S(1)}, f32[4,384]{1,0:T(4,128)S(1)}, u32[]{:S(2)}, u32[]{:S(2)}) collective-permute-start(f32[4,384]{1,0:T(4,128)S(1)} %spectrum.1.refs_0_), channel_id=1, source_target_pairs={{0,2},{1,3},{2,0},{3,1},{4,6},{5,7},{6,4},{7,5},{8,10},{9,11},{10,... | collective-permute-start | bytes 18440 | tf_op jit(solution)/shard_map/ppermute | solution.py:470
  27.1 2.1 %collective-permute-start.1 = (f32[4,384]{1,0:T(4,128)S(1)}, f32[4,384]{1,0:T(4,128)S(1)}, u32[]{:S(2)}, u32[]{:S(2)}) collective-permute-start(f32[4,384]{1,0:T(4,128)S(1)} %spectrum.1.refs_0_), channel_id=1, source_target_pairs={{0,1},{1,0},{2,3},{3,2},{4,5},{5,4},{6,7},{7,6},{8,9},{9,8},{10,11... | collective-permute-start | bytes 18440 | tf_op jit(solution)/shard_map/ppermute | solution.py:470
  29.2 1.2 %collective-permute-start.2 = (f32[4,384]{1,0:T(4,128)S(1)}, f32[4,384]{1,0:T(4,128)S(1)}, u32[]{:S(2)}, u32[]{:S(2)}) collective-permute-start(f32[4,384]{1,0:T(4,128)S(1)} %collective-permute-done.refs_1_), channel_id=1, source_target_pairs={{0,1},{1,0},{2,3},{3,2},{4,5},{5,4},{6,7},{7,6},{8,9},{9,8},{10,11... | collective-permute-start | bytes 18440 | tf_op jit(solution)/shard_map/ppermute | solution.py:470
  29.2 1.2 %copy-start.4 = (s32[4,4]{1,0:T(4,128)S(1)}, s32[4,4]{1,0:T(4,128)}, u32[]{:S(2)}) copy-start(s32[4,4]{1,0:T(4,128)} %mask.1) | copy-start | bytes 196

commit v2 on v1

--- a/solution.py
+++ b/solution.py
@@ -18,6 +18,8 @@
 TILES = SPAN // LANES
 HALF_TILES = HALF_WIN // LANES
 PAD = 16
+GROUP = 1
+position = lax.axis_index
 VMEM_LIMIT = 16 * 1024 * 1024
 BF = jnp.bfloat16
 F32 = jnp.float32
@@ -79,6 +81,9 @@
         self.rows = length // SPAN
         self.half = self.rows // 2 + 1
         self.pad = up_to(self.rows, PAD)
+        self.full = self.rows // PAD * PAD
+        self.tail = self.rows - self.full
+        self.depth = 3 * self.full + PAD
         self.block = min(tm_count, 16)
         self.blocks = tm_count // self.block
         self.folds = -(-(bins + self.rows - 1) // self.rows)
@@ -87,31 +92,39 @@
         self.sent_rows = self.spec_rows + self.edge_rows
         assert length % SPAN == 0 and tm_count % self.block == 0
         assert stations == 2 and self.folds <= PAD
-        assert self.rows >= 2 and 4 * self.pad <= 256
+        assert self.rows >= 2 and 0 < 3 * self.tail <= 8
+
+    def row_order(self):
+        j2 = np.arange(self.tm)[:, None] + self.tm * np.arange(self.half)[None, :]
+        return j2.reshape(self.blocks, self.block, self.half).transpose(0, 2, 1).reshape(self.blocks, -1)
 
     def first_table(self):
-        j2 = np.arange(self.tm)[:, None] + self.tm * np.arange(self.half)[None, :]
-        j2 = j2.reshape(self.blocks, self.block, self.half).transpose(0, 2, 1).reshape(self.blocks, -1)
-        period = self.tm * self.rows
-        angle = 2.0 * np.pi / period * (j2[:, :, None] * np.arange(self.rows) % period)
-        parts = np.concatenate([np.cos(angle), -np.sin(angle)], axis=1)
-        parts = np.pad(parts, ((0, 0), (0, 0), (0, self.pad - self.rows)))
+        j2 = self.row_order()[:, None, :, None]
+        tile = np.arange(TILES)[None, :, None, None]
+        total = self.tm * self.length
+        time = np.arange(self.rows) * SPAN + tile * LANES
+        angle = 2.0 * np.pi / total * (j2 * time % total)
+        parts = np.concatenate([np.cos(angle), -np.sin(angle)], axis=2)
         high, low = np_split(parts)
-        return np.concatenate([high, high, low, low], axis=2).astype(jnp.bfloat16)
-
-    def shift_table(self):
-        angle = 2.0 * np.pi / self.length * (
-            np.arange(self.half)[:, None] * np.arange(SPAN)[None, :] % self.length
+        full = self.full
+        pieces = [piece[..., :full] for piece in (high, high, low)]
+        for piece in (high, high, low):
+            rest = piece[..., full:]
+            pieces.append(np.pad(rest, ((0, 0), (0, 0), (0, 0), (0, self.tail - rest.shape[-1]))))
+        table = np.concatenate(pieces, axis=3)
+        gap = ((0, 0), (0, 0), (0, 0), (0, self.depth - table.shape[-1]))
+        return np.pad(table, gap).astype(jnp.bfloat16)
+
+    def lane_table(self):
+        angle = 2.0 * np.pi / (self.tm * self.length) * (
+            self.row_order()[:, :, None] * np.arange(LANES)
         )
-        return np.stack([np.cos(angle), -np.sin(angle)]).astype(np.float32)
-
-
-def normalize(z, flags, x, xs, wide, stack, edges):
+        return np.stack([np.cos(angle), -np.sin(angle)], axis=1).astype(np.float32)
+
+
+def normalize(z, x, xs, sums, stack, edges):
     rows, pad, top = z.rows, z.pad, 8
-    full = rows // 8 * 8
-    for s in range(z.stations):
-        xs[s, 0:top, :] = jnp.zeros((top, SPAN), F32)
-        xs[s, top + full : top + pad + 8, :] = jnp.zeros((pad + 8 - full, SPAN), F32)
+    short = up_to(rows, 8)
     for a in range(rows):
         xs[:, top + a, :] = x[:, a * SPAN : (a + 1) * SPAN].astype(F32)
     for s in range(z.stations):
@@ -120,84 +133,172 @@
                 at = (side * z.stations + s) * TILES + c
                 edges[at : at + 1, :] = xs[s, top + a : top + a + 1, c * LANES : (c + 1) * LANES]
     upto, onward, ones = window_tables()
-    kernel = jnp.concatenate([onward] + [ones] * (2 * HALF_TILES - 1) + [upto], axis=0)
-    row = iota((pad, LANES), 0)
-    for s in range(z.stations):
-        for turn, (lo, hi) in ((-1, (HALF_WIN, SPAN)), (0, (0, SPAN)), (1, (0, HALF_WIN))):
-            at = HALF_WIN + turn * SPAN + lo
-            wide[s, :, at : at + hi - lo] = jnp.abs(
-                xs[s, top + turn : top + turn + pad, lo:hi]
-            ).astype(BF)
+    kernel = jnp.concatenate([upto, onward, ones], axis=1)
+    group = 4
+    for s in range(z.stations):
+        for c0 in range(0, TILES, group):
+            part = jnp.concatenate(
+                [
+                    jnp.abs(xs[s, top : top + pad, c * LANES : (c + 1) * LANES]).astype(BF)
+                    for c in range(c0, c0 + group)
+                ],
+                axis=0,
+            )
+            got = jnp.dot(part, kernel, preferred_element_type=F32)
+            for k in range(group):
+                sums[s, c0 + k, top : top + short, :] = got[k * pad : k * pad + short]
+    blank = jnp.zeros((1, HALF_WIN), F32)
+    for s in range(z.stations):
+        xs[s, top : top + 1, 0:HALF_WIN] = blank
+        xs[s, top + rows - 1 : top + rows, HALF_WIN:SPAN] = blank
+    for s in range(z.stations):
+
+        def tile(kind, c):
+            turn, cc = divmod(c, TILES)
+            lines = slice(top + turn, top + turn + short)
+            return sums[s, cc, lines, kind * LANES : (kind + 1) * LANES]
+
+        ones_ = [tile(2, c) for c in range(1 - HALF_TILES, TILES + HALF_TILES - 1)]
+        twos = [ones_[c] + ones_[c + 1] for c in range(len(ones_) - 1)]
         for c in range(TILES):
-            here = wide[s, :, c * LANES : c * LANES + SPAN + LANES]
-            total = jnp.dot(here, kernel, preferred_element_type=F32)
-            value = xs[s, top : top + pad, c * LANES : (c + 1) * LANES] * flags[s].astype(F32)
+            inner = (twos[c] + twos[c + 2]) + (twos[c + 4] + ones_[c + 6])
+            total = inner + (tile(1, c - HALF_TILES) + tile(0, c + HALF_TILES))
+            value = xs[s, top : top + short, c * LANES : (c + 1) * LANES]
             value = value / (total * (1.0 / (2 * HALF_WIN + 1)) + EPS_MEAN)
-            edge = 0 if c < HALF_TILES else rows - 1
-            high, low = split2(jnp.where(row == edge, 0.0, value))
-            for k, part in enumerate((high, low, high, low)):
-                stack[s, k * pad : (k + 1) * pad, c * LANES : (c + 1) * LANES] = part
-
-
-def fold_weights(z, band, weight):
+            high, low = split2(value[: z.full])
+            lanes = slice((c * z.stations + s) * LANES, (c * z.stations + s + 1) * LANES)
+            for k, part in enumerate((high, low, high)):
+                stack[k * z.full : (k + 1) * z.full, lanes] = part
+            rest = value[z.full :]
+            high = rest.astype(BF).astype(F32)
+            rest = high + pltpu.roll(rest - high, z.tail, 0) + pltpu.roll(high, 2 * z.tail, 0)
+            rest = jnp.concatenate([rest, jnp.zeros((PAD - rest.shape[0], LANES), F32)], axis=0)
+            stack[3 * z.full :, lanes] = rest.astype(BF)
+
+
+def fold_waves(fold):
+    lane = iota((PAD, SPAN), 1)
     for kind in range(2):
-        order = iota((PAD, SPAN), 0) + (band[0] // z.rows + kind)
-        turns = jnp.bitwise_and(order * iota((PAD, SPAN), 1), SPAN - 1).astype(F32) * (1.0 / SPAN)
-        sine, cosine = sincos(turns)
+        turns = jnp.bitwise_and((iota((PAD, SPAN), 0) + kind) * lane, SPAN - 1).astype(F32)
+        sine, cosine = sincos(turns * (1.0 / SPAN))
+        fold[kind, 0] = cosine
+        fold[kind, 1] = sine
+
+
+def fold_weights(z, base, fold, weight):
+    spot = iota((TILES, LANES), 0) * LANES + iota((TILES, LANES), 1)
+    turns = jnp.bitwise_and((base // z.rows) * spot, SPAN - 1).astype(F32)
+    sine, cosine = sincos(turns * (1.0 / SPAN))
+    b_cos = jnp.concatenate([cosine[c : c + 1] for c in range(TILES)], axis=1)
+    b_sin = jnp.concatenate([sine[c : c + 1] for c in range(TILES)], axis=1)
+    for kind in range(2):
+        w_cos, w_sin = fold[kind, 0], fold[kind, 1]
+        sine = w_sin * b_cos + w_cos * b_sin
+        cosine = w_cos * b_cos - w_sin * b_sin
         for h, (s, c) in enumerate(zip(split2(sine), split2(cosine))):
             table = ((c, s), (-s, c)) if kind == 0 else ((c, -s), (-s, -c))
             for part in range(2):
                 at = h * 4 * PAD + kind * 2 * PAD + part * PAD
-                weight[at : at + PAD, 0:SPAN] = table[part][0]
-                weight[at : at + PAD, SPAN : 2 * SPAN] = table[part][1]
+                for tile in range(TILES):
+                    for side in range(2):
+                        to = (2 * tile + side) * LANES
+                        weight[at : at + PAD, to : to + LANES] = table[part][side][
+                            :, tile * LANES : (tile + 1) * LANES
+                        ]
 
 
 def transform_kernel(
-    z, band, place, flags, x, first, shift, out, xs, wide, stack, edges, weight, acc, both, spec
+    z, band, flags, x, first, lanes_table, out,
+    band_s, flags_s, x_v, first_v, lanes_v, xs, sums, stack, edges, fold, weight, acc, both, spec, sems,
 ):
     half, block, tm = z.half, z.block, z.tm
     height = half * block
     index = pl.program_id(0)
+    top, rows, pad = 8, z.rows, z.pad
+
+    get_first = pltpu.make_async_copy(first.at[index], first_v, sems.at[3])
+    get_lanes = pltpu.make_async_copy(lanes_table.at[index], lanes_v, sems.at[4])
 
     def prologue():
-        normalize(z, flags, x, xs, wide, stack, edges)
-        fold_weights(z, band, weight)
+        copies = [
+            pltpu.make_async_copy(band, band_s, sems.at[0]),
+            pltpu.make_async_copy(flags, flags_s, sems.at[1]),
+            pltpu.make_async_copy(x, x_v, sems.at[2]),
+        ]
+        for copy in copies:
+            copy.start()
+        get_lanes.start()
+        get_first.start()
+        full = rows // 8 * 8
+        for s in range(z.stations):
+            xs[s, top + full : top + pad, :] = jnp.zeros((pad - full, SPAN), F32)
+            for c in range(TILES):
+                sums[s, c, 0:top, :] = jnp.zeros((top, 3 * LANES), F32)
+                sums[s, c, top + up_to(rows, 8) :, :] = jnp.zeros((8, 3 * LANES), F32)
         spec[:, z.spec_rows - 8 : z.spec_rows, :] = jnp.zeros((tm, 8, LANES), F32)
+        fold_waves(fold)
+        for copy in copies:
+            copy.wait()
+        fold_weights(z, band_s[0, 0], fold, weight)
+        normalize(z, x_v, xs, sums, stack, edges)
 
     if z.blocks == 1:
         prologue()
     else:
         pl.when(index == 0)(prologue)
-    acc[...] = jnp.zeros_like(acc)
-    width = 256
-    residue = index * block + iota((block, width), 0)
-    start = turns_of((place[0] * residue).astype(F32), tm)
-
-    def step(c, carry):
-        lanes = pl.ds(pl.multiple_of(c * width, width), width)
-        lanes_im = pl.ds(pl.multiple_of(SPAN + c * width, width), width)
-        offset = c * width + iota((block, width), 1)
-        turn = start + (residue * offset).astype(F32) * (1.0 / (tm * z.length))
-        sn, cs = sincos(turn)
-        r_re, r_im = cs[None], -sn[None]
-        m_re = shift[0, :, lanes][:, None, :]
-        m_im = shift[1, :, lanes][:, None, :]
-        t_re = (m_re * r_re - m_im * r_im).reshape(height, width)
-        t_im = (m_re * r_im + m_im * r_re).reshape(height, width)
-        w = jnp.concatenate([weight[:, lanes], weight[:, lanes_im]] * 2, axis=1)
+
+        @pl.when(index > 0)
+        def _():
+            get_lanes.start()
+            get_first.start()
+
+    get_lanes.wait()
+    residue = index * block + iota((block, LANES), 0)
+    sine, cosine = sincos(turns_of((position("tm") * residue).astype(F32), tm))
+    l_re = lanes_v[0].reshape(half, block, LANES)
+    l_im = lanes_v[1].reshape(half, block, LANES)
+    t_re = (l_re * cosine[None] + l_im * sine[None]).reshape(height, LANES)
+    t_im = (l_im * cosine[None] - l_re * sine[None]).reshape(height, LANES)
+    get_first.wait()
+    wide_lanes = z.stations * LANES
+
+    def first_stage(c):
+        return jnp.dot(
+            first_v[c],
+            stack[:, c * wide_lanes : (c + 1) * wide_lanes],
+            preferred_element_type=F32,
+        )
+
+    def second_stage(c0, parts):
+        w = weight[:, 2 * c0 * LANES : 2 * (c0 + GROUP) * LANES]
         for s in range(z.stations):
-            f = jnp.dot(first[0], stack[s, :, lanes], preferred_element_type=F32)
-            f_re, f_im = f[:height], f[height:]
-            re_h, re_l = split2(f_re * t_re - f_im * t_im)
-            im_h, im_l = split2(f_re * t_im + f_im * t_re)
-            value = jnp.concatenate([re_h, im_h, re_l, im_l], axis=1)
-            acc[s] += lax.dot_general(
-                value, w, (((1,), (1,)), ((), ())), preferred_element_type=F32
-            )
-        return carry
-
-    lax.fori_loop(0, SPAN // width, step, 0)
-    zero, one = (acc[s] + pltpu.roll(acc[s], LANES // 2, 1) for s in range(2))
+            left = jnp.concatenate([jnp.concatenate(piece, axis=1) for piece in parts[s]], axis=0)
+            got = lax.dot_general(left, w, (((1,), (1,)), ((), ())), preferred_element_type=F32)
+            value = got[:height] + got[height:]
+            acc[s] = value if c0 == 0 else acc[s] + value
+
+    waiting = None
+    coming = [first_stage(c) for c in range(GROUP)]
+    for c0 in range(0, TILES, GROUP):
+        current = coming
+        parts = [[[], []] for _ in range(z.stations)]
+        for f in current:
+            for s in range(z.stations):
+                f_re = f[:height, s * LANES : (s + 1) * LANES]
+                f_im = f[height:, s * LANES : (s + 1) * LANES]
+                for value in (f_re * t_re - f_im * t_im, f_re * t_im + f_im * t_re):
+                    high, low = split2(value)
+                    parts[s][0].append(high)
+                    parts[s][1].append(low)
+        if c0 + GROUP < TILES:
+            coming = [first_stage(c) for c in range(c0 + GROUP, c0 + 2 * GROUP)]
+        if waiting is not None:
+            second_stage(c0 - GROUP, waiting)
+        waiting = parts
+    second_stage(TILES - GROUP, waiting)
+    zero, one = (
+        (acc[s] + pltpu.roll(acc[s], LANES // 2, 1)) * flags_s[s].astype(F32) for s in range(2)
+    )
     lane = iota((height, LANES), 1)
     early = jnp.bitwise_and(lane, LANES // 2 - 1) < LANES // 4
     direct = jnp.where(early, zero, pltpu.roll(one, LANES // 4, 1))
@@ -209,9 +310,9 @@
         here = index * block + k
         there = jnp.where(here == 0, 0, tm - here) if z.blocks > 1 else (tm - k) % tm
         here = here if z.blocks > 1 else k
-        rows = pl.ds(k, half, stride=block)
-        spec[here, 0:half, :] = both[0, rows, :]
-        spec[there, half : 2 * half, :] = both[1, rows, :]
+        lines = pl.ds(k, half, stride=block)
+        spec[here, 0:half, :] = both[0, lines, :]
+        spec[there, half : 2 * half, :] = both[1, lines, :]
 
     def finish():
         ends = edges[...].astype(BF)
@@ -235,46 +336,59 @@
 
 SMEM_SPEC = pl.BlockSpec(memory_space=pltpu.SMEM)
 VMEM_SPEC = pl.BlockSpec(memory_space=pltpu.VMEM)
+HBM_SPEC = pl.BlockSpec(memory_space=pltpu.HBM)
 
 
 def params():
     return pltpu.CompilerParams(vmem_limit_bytes=VMEM_LIMIT)
 
 
-def transform(z, band, place, flags, x):
-    width = 4 * z.pad
+def transform(z, band, flags, x):
+    band = band.reshape(1, 1)
     height = z.half * z.block
+    first, lanes = z.first_table(), z.lane_table()
     return pl.pallas_call(
         functools.partial(transform_kernel, z),
         grid=(z.blocks,),
-        in_specs=[
-            SMEM_SPEC,
-            SMEM_SPEC,
-            SMEM_SPEC,
-            VMEM_SPEC,
-            pl.BlockSpec((1, 2 * height, width), lambda i: (i, 0, 0)),
-            VMEM_SPEC,
-        ],
+        in_specs=[HBM_SPEC] * 5,
         out_specs=VMEM_SPEC,
         out_shape=jax.ShapeDtypeStruct((z.tm, z.sent_rows, LANES), BF),
         scratch_shapes=[
-            pltpu.VMEM((z.stations, 16 + z.pad, SPAN), F32),
-            pltpu.VMEM((z.stations, z.pad, 2 * SPAN), BF),
-            pltpu.VMEM((z.stations, width, SPAN), BF),
+            pltpu.SMEM((1, 1), jnp.int32),
+            pltpu.SMEM((z.stations,), jnp.int32),
+            pltpu.VMEM(x.shape, BF),
+            pltpu.VMEM(first.shape[1:], BF),
+            pltpu.VMEM(lanes.shape[1:], F32),
+            pltpu.VMEM((z.stations, 8 + z.pad, SPAN), F32),
+            pltpu.VMEM((z.stations, TILES, 16 + up_to(z.rows, 8), 3 * LANES), F32),
+            pltpu.VMEM((z.depth, z.stations * SPAN), BF),
             pltpu.VMEM((z.edge_rows, LANES), F32),
+            pltpu.VMEM((2, 2, PAD, SPAN), F32),
             pltpu.VMEM((LANES, 2 * SPAN), BF),
             pltpu.VMEM((z.stations, height, LANES), F32),
             pltpu.VMEM((2, height, LANES), F32),
             pltpu.VMEM((z.tm, z.spec_rows, LANES), F32),
+            pltpu.SemaphoreType.DMA((5,)),
         ],
-        compiler_params=params(),
         name="transform",
-    )(band, place, flags, x, jnp.asarray(z.first_table()), jnp.asarray(z.shift_table()))
-
-
-def table_kernel(z, band, place, choose, keep, steps, turns, near, phase):
+    )(band, flags, x, jnp.asarray(first), jnp.asarray(lanes))
+
+
+def table_kernel(
+    z, band, flags, choose, keep, steps, turns, near, phase, switch, band_s, flags_s, sems
+):
     rows, tm, bins, half = z.rows, z.tm, z.bins, z.half
-    base, residue = band[0], place[0]
+    copies = [
+        pltpu.make_async_copy(band, band_s, sems.at[0]),
+        pltpu.make_async_copy(flags, flags_s, sems.at[1]),
+    ]
+    for copy in copies:
+        copy.start()
+    for copy in copies:
+        copy.wait()
+    base, residue = band_s[0, 0], position("tm")
+    for s in range(z.stations):
+        switch[s] = jnp.full((TILES, LANES), flags_s[s].astype(F32))
     spot = iota_f((1, bins), 1) + (base % rows).astype(F32)
     fold = jnp.floor((spot + 0.5) * (1.0 / rows))
     rest = spot - fold * rows
@@ -305,11 +419,16 @@
     phase[1] = -p_sin
 
 
-def tables(z, band, place):
+def tables(z, band, flags):
     return pl.pallas_call(
         functools.partial(table_kernel, z),
-        in_specs=[SMEM_SPEC, SMEM_SPEC],
-        out_specs=[VMEM_SPEC] * 6,
+        in_specs=[HBM_SPEC, HBM_SPEC],
+        out_specs=[VMEM_SPEC] * 7,
+        scratch_shapes=[
+            pltpu.SMEM((1, 1), jnp.int32),
+            pltpu.SMEM((z.stations,), jnp.int32),
+            pltpu.SemaphoreType.DMA((2,)),
+        ],
         out_shape=[
             jax.ShapeDtypeStruct((z.tm, z.spec_rows, z.bins), BF),
             jax.ShapeDtypeStruct((PAD, z.bins), F32),
@@ -317,11 +436,12 @@
             jax.ShapeDtypeStruct((2, LANES, z.bins), F32),
             jax.ShapeDtypeStruct((z.bins, z.bins), BF),
             jax.ShapeDtypeStruct((2, z.tm, LANES), F32),
+            jax.ShapeDtypeStruct((z.stations, TILES, LANES), F32),
         ],
         compiler_params=params(),
         cost_estimate=pl.CostEstimate(flops=4000000, bytes_accessed=2000000, transcendentals=0),
         name="tables",
-    )(band, place)
+    )(band.reshape(1, 1), flags)
 
 
 def sublane_sums(value, row):
@@ -331,7 +451,7 @@
     return total - value, total
 
 
-def spectrum_kernel(z, flags, got, choose, keep, steps, turns, near, phase, out):
+def spectrum_kernel(z, got, choose, keep, steps, turns, near, phase, switch, out):
     tm, bins, at = z.tm, z.bins, z.spec_rows
     parts = got[:, 0:at, :].astype(F32).reshape(tm * at, LANES).astype(BF)
     weights = choose[...].astype(F32).reshape(tm * at, bins).astype(BF)
@@ -360,7 +480,7 @@
     for s in range(z.stations):
         real = jnp.zeros((TILES, LANES), F32)
         imag = jnp.zeros((TILES, LANES), F32)
-        flag = flags[s].astype(F32)
+        flag = switch[s]
         for p in range(tm):
             begin = (p * z.stations + s) * TILES
             before = ((p - 1) % tm * z.stations + s) * TILES
@@ -410,20 +530,20 @@
         out[2 * s + 1 : 2 * s + 2, :] = spec[2 * s + 1] * scale
 
 
-def spectrum(z, flags, got, made):
+def spectrum(z, got, made):
     return pl.pallas_call(
         functools.partial(spectrum_kernel, z),
-        in_specs=[SMEM_SPEC] + [VMEM_SPEC] * 7,
+        in_specs=[VMEM_SPEC] * 8,
         out_specs=VMEM_SPEC,
         out_shape=jax.ShapeDtypeStruct((2 * z.stations, z.bins), F32),
         compiler_params=params(),
         name="spectrum",
-    )(flags, got, *made)
-
-
-def cross_kernel(z, offsets, mask, where, stacks, *refs):
+    )(got, *made)
+
+
+def cross_kernel(z, offsets, mask, stacks, *refs):
     pieces, out = refs[:-1], refs[-1]
-    here = where[0]
+    here = position("sta")
     mine = pieces[0][...]
     bins = z.bins
     sides = []
@@ -441,15 +561,15 @@
                 out[i, column] = stacks[i, column] + (re * p + im * q)
 
 
-def cross(z, offsets, mask, where, stacks, pieces):
+def cross(z, offsets, mask, stacks, pieces):
     return pl.pallas_call(
         functools.partial(cross_kernel, z, offsets),
-        in_specs=[SMEM_SPEC, SMEM_SPEC] + [VMEM_SPEC] * (1 + len(pieces)),
+        in_specs=[SMEM_SPEC] + [VMEM_SPEC] * (1 + len(pieces)),
         out_specs=VMEM_SPEC,
         out_shape=jax.ShapeDtypeStruct(stacks.shape, F32),
         compiler_params=params(),
         name="cross",
-    )(mask, where, stacks, *pieces)
+    )(mask, stacks, *pieces)
 
 
 def shards(traces, station_flags, tile_mask, band_block, stacks):
@@ -457,12 +577,10 @@
     stations, length = traces.shape
     z = Sizes(stations, length, tm_count, stacks.shape[-1])
     assert sta_count & (sta_count - 1) == 0
-    place = lax.axis_index("tm").astype(jnp.int32).reshape(1)
-    where = lax.axis_index("sta").astype(jnp.int32).reshape(1)
-    sent = transform(z, band_block, place, station_flags, traces)
+    sent = transform(z, band_block, station_flags, traces)
     got = lax.all_to_all(sent, "tm", split_axis=0, concat_axis=0, tiled=True)
-    made = tables(z, band_block, place)
-    white = spectrum(z, station_flags, got, made)
+    made = tables(z, band_block, station_flags)
+    white = spectrum(z, got, made)
     offsets, pieces = [0], [white]
     bit = sta_count // 2
     while bit:
@@ -470,7 +588,7 @@
         pieces += [lax.ppermute(piece, "sta", pairs) for piece in pieces]
         offsets += [offset ^ bit for offset in offsets]
         bit //= 2
-    return cross(z, offsets, tile_mask, where, stacks, pieces)
+    return cross(z, offsets, tile_mask, stacks, pieces)
 
 
 def solution(mesh):

time: 31.9 us -> 26.3 us (0.82)
  local copies, waits for them, and re-layouts: 3.39 us -> 0.66 us
  Pallas kernels: 8.38 us -> 6.71 us
  waiting for transfers between devices: 10.3 us -> 9.08 us
    unnamed x12 -> x6, local copies, waits for them, and re-layouts: 3.39 us -> 0.66 us
    pallas_call x1, Pallas kernels: 5.33 us -> 3.62 us  [transform(): pl.pallas_call(functools.partial(transform_kernel, z), grid=(z.blocks,),...]
    all_to_all x1, waiting for transfers between devices: 7.02 us -> 5.78 us  [shards(): got = lax.all_to_all(sent, 'tm', split_axis=0, concat_axis=0, tiled=True)]
  transfers between devices with their start and end apart: 4 -> 4, of which waited for: 3 -> 3; matrix products, arithmetic and copies ran while one was open for 0% -> 0% of each run, Pallas kernels for 1% -> 4%
where the time goes in v2:
time: 26.3 us; the launch traced here: 26 us
  waiting for transfers between devices  9.08 us (35%)
  starting transfers between devices  8.89 us (34%)
  Pallas kernels  6.71 us (26%)
  between operations  0.68 us (3%)
  local copies, waits for them, and re-layouts  0.66 us (3%)
    all_to_all x1, starting transfers between devices, shards(): got = lax.all_to_all(sent, 'tm', split_axis=0, concat_axis=0, tiled=True)  7.32 us
    all_to_all x1, waiting for transfers between devices, shards(): got = lax.all_to_all(sent, 'tm', split_axis=0, concat_axis=0, tiled=True)  5.78 us
    pallas_call x1, Pallas kernels, transform(): pl.pallas_call(functools.partial(transform_kernel, z), grid=(z.blocks,),...  3.62 us
    ppermute x3, waiting for transfers between devices, shards(): pieces += [lax.ppermute(piece, 'sta', pairs) for piece in pieces]  3.29 us
    ppermute x3, starting transfers between devices, shards(): pieces += [lax.ppermute(piece, 'sta', pairs) for piece in pieces]  1.57 us
    pallas_call x1, Pallas kernels, cross(): pl.pallas_call(functools.partial(cross_kernel, z, offsets), in_specs=[SME...  1.24 us
    pallas_call x1, Pallas kernels, tables(): pl.pallas_call(functools.partial(table_kernel, z), in_specs=[HBM_SPEC, HB...  1.01 us
    pallas_call x1, Pallas kernels, spectrum(): pl.pallas_call(functools.partial(spectrum_kernel, z), in_specs=[VMEM_SPEC...  0.84 us
  transfers between devices with their start and end apart: 4, of which 3 were waited for; matrix products, arithmetic and copies ran while one was open for 0% of the time, Pallas kernels for 4%

profile of v2, /device:TPU:0, one launch (start us, length us, event | category | flops | bytes accessed | tf_op | source)
XLA Modules:
  0.0 26.0 jit_solution(2743030028645722664)
XLA Ops:
  0.7 3.6 %transform.1 = bf16[8,72,128]{2,1,0:T(8,128)(2,1)} custom-call(s32[1,1]{1,0:T(1,128)} %bitcast.1.band, s32[2]{0:T(128)} %flags.3, bf16[2,33792]{1,0:T(2,128)(2,1)} %x.1, bf16[1,8,272,112]{3,2,1,0:T(8,128)(2,1)} %constant.4.clone.first, f32[1,2,136,128]{3,2,1,0:T(8,128)} %constant.5.clone.lanes_table), custom_call_target="tpu_custom_call" | custom-call | tf_op jit(solution)/shard_map/transform/pallas_call | solution.py:350
  4.3 7.3 %all-to-all-start = ((bf16[8,72,128]{2,1,0:T(8,128)(2,1)}), bf16[8,72,128]{2,1,0:T(8,128)(2,1)S(1)}, u32[]{:S(2)}, u32[]{:S(2)}) async-start(bf16[8,72,128]{2,1,0:T(8,128)(2,1)} %transform.1), calls=%async_computation | async-start | bytes 294912 | tf_op jit(solution)/shard_map/all_to_all | solution.py:581
  11.6 0.0 copy-start.2
  11.6 0.7 %copy-done.2 = s32[2]{0:T(128)S(1)} copy-done((s32[2]{0:T(128)S(1)}, s32[2]{0:T(128)}, u32[]{:S(2)}) %copy-start.2) | copy-done | bytes 32
  12.3 1.0 %tables.1 = (bf16[8,40,384]{2,1,0:T(8,128)(2,1)S(1)}, f32[16,384]{1,0:T(8,128)S(1)}, bf16[64,768]{1,0:T(8,128)(2,1)S(1)}, f32[2,128,384]{2,1,0:T(8,128)S(1)}, bf...) custom-call(s32[1,1]{1,0:T(1,128)} %bitcast.2.band, s32[2]{0:T(128)S(1)} %copy-done.2), custom_call_target="tpu_custom_call" | custom-call | flops 4000000 | bytes 2000000 | tf_op jit(solution)/shard_map/tables/pallas_call | solution.py:423
  13.3 5.8 %all-to-all-done.got = bf16[8,72,128]{2,1,0:T(8,128)(2,1)S(1)} async-done(((bf16[8,72,128]{2,1,0:T(8,128)(2,1)}), bf16[8,72,128]{2,1,0:T(8,128)(2,1)S(1)}, u32[]{:S(2)}, u32[]{:S(2)}) %all-to-all-start) | async-done | bytes 147488 | tf_op jit(solution)/shard_map/all_to_all | solution.py:581
  19.1 0.0 copy-start
  19.1 0.0 copy-start.1
  19.1 0.8 %spectrum.1.refs_0_ = f32[4,384]{1,0:T(4,128)S(1)} custom-call(bf16[8,72,128]{2,1,0:T(8,128)(2,1)S(1)} %all-to-all-done.got, bf16[8,40,384]{2,1,0:T(8,128)(2,1)S(1)} %get-tuple-element.12.choose, f32[16,384]{1,0:T(8,128)S(1)} %get-tuple-element.13.keep, bf16[64,768]{1,0:T(8,128)(2,1)S(1)} %get-tuple-element.14.steps, ...), custom_call_target="tpu_custom_call" | custom-call | tf_op jit(solution)/shard_map/spectrum/pallas_call | solution.py:534
  19.9 1.6 %collective-permute-start = (f32[4,384]{1,0:T(4,128)S(1)}, f32[4,384]{1,0:T(4,128)S(1)}, u32[]{:S(2)}, u32[]{:S(2)}) collective-permute-start(f32[4,384]{1,0:T(4,128)S(1)} %spectrum.1.refs_0_), channel_id=1, source_target_pairs={{0,2},{1,3},{2,0},{3,1},{4,6},{5,7},{6,4},{7,5},{8,10},{9,11},{10,... | collective-permute-start | bytes 18440 | tf_op jit(solution)/shard_map/ppermute | solution.py:588
  21.5 0.0 collective-permute-start.1
  21.5 2.1 %collective-permute-done.refs_1_ = f32[4,384]{1,0:T(4,128)S(1)} collective-permute-done((f32[4,384]{1,0:T(4,128)S(1)}, f32[4,384]{1,0:T(4,128)S(1)}, u32[]{:S(2)}, u32[]{:S(2)}) %collective-permute-start) | collective-permute-done | bytes 6176 | tf_op jit(solution)/shard_map/ppermute | solution.py:588
  23.6 0.0 collective-permute-start.2
  23.6 0.0 collective-permute-done.1.refs_2_
  23.6 1.2 %collective-permute-done.2.refs_3_ = f32[4,384]{1,0:T(4,128)S(1)} collective-permute-done((f32[4,384]{1,0:T(4,128)S(1)}, f32[4,384]{1,0:T(4,128)S(1)}, u32[]{:S(2)}, u32[]{:S(2)}) %collective-permute-start.2) | collective-permute-done | bytes 6176 | tf_op jit(solution)/shard_map/ppermute | solution.py:588
  24.8 0.0 copy-done
  24.8 0.0 copy-done.1
  24.8 1.2 %cross.1 = f32[2,8,2,384]{3,2,1,0:T(2,128)} custom-call(s32[4,4]{1,0:T(4,128)S(1)} %copy-done.1, f32[2,8,2,384]{3,2,1,0:T(2,128)S(1)} %copy-done, f32[4,384]{1,0:T(4,128)S(1)} %spectrum.1.refs_0_, f32[4,384]{1,0:T(4,128)S(1)} %collective-permute-done.refs_1_, f32[4,384]{1,0:T(4,128)S(1)} %collective-permute-done.1.refs_2_, ...), custom_call_target="tpu_custom_call" | custom-call | tf_op jit(solution)/shard_map/cross/pallas_call | solution.py:565
Async XLA Ops:
  4.3 14.8 %all-to-all-start = ((bf16[8,72,128]{2,1,0:T(8,128)(2,1)}), bf16[8,72,128]{2,1,0:T(8,128)(2,1)S(1)}, u32[]{:S(2)}, u32[]{:S(2)}) async-start(bf16[8,72,128]{2,1,0:T(8,128)(2,1)} %transform.1), calls=%async_computation | async-start | bytes 294912 | tf_op jit(solution)/shard_map/all_to_all | solution.py:581
  11.6 0.7 %copy-start.2 = (s32[2]{0:T(128)S(1)}, s32[2]{0:T(128)}, u32[]{:S(2)}) copy-start(s32[2]{0:T(128)} %flags.3) | copy-start | bytes 28
  19.1 5.7 %copy-start = (f32[2,8,2,384]{3,2,1,0:T(2,128)S(1)}, f32[2,8,2,384]{3,2,1,0:T(2,128)}, u32[]{:S(2)}) copy-start(f32[2,8,2,384]{3,2,1,0:T(2,128)} %stacks.1) | copy-start | bytes 147460
  19.1 5.7 %copy-start.1 = (s32[4,4]{1,0:T(4,128)S(1)}, s32[4,4]{1,0:T(4,128)}, u32[]{:S(2)}) copy-start(s32[4,4]{1,0:T(4,128)} %mask.1) | copy-start | bytes 196
  19.9 3.7 %collective-permute-start = (f32[4,384]{1,0:T(4,128)S(1)}, f32[4,384]{1,0:T(4,128)S(1)}, u32[]{:S(2)}, u32[]{:S(2)}) collective-permute-start(f32[4,384]{1,0:T(4,128)S(1)} %spectrum.1.refs_0_), channel_id=1, source_target_pairs={{0,2},{1,3},{2,0},{3,1},{4,6},{5,7},{6,4},{7,5},{8,10},{9,11},{10,... | collective-permute-start | bytes 18440 | tf_op jit(solution)/shard_map/ppermute | solution.py:588
  21.5 2.1 %collective-permute-start.1 = (f32[4,384]{1,0:T(4,128)S(1)}, f32[4,384]{1,0:T(4,128)S(1)}, u32[]{:S(2)}, u32[]{:S(2)}) collective-permute-start(f32[4,384]{1,0:T(4,128)S(1)} %spectrum.1.refs_0_), channel_id=1, source_target_pairs={{0,1},{1,0},{2,3},{3,2},{4,5},{5,4},{6,7},{7,6},{8,9},{9,8},{10,11... | collective-permute-start | bytes 18440 | tf_op jit(solution)/shard_map/ppermute | solution.py:588
  23.6 1.2 %collective-permute-start.2 = (f32[4,384]{1,0:T(4,128)S(1)}, f32[4,384]{1,0:T(4,128)S(1)}, u32[]{:S(2)}, u32[]{:S(2)}) collective-permute-start(f32[4,384]{1,0:T(4,128)S(1)} %collective-permute-done.refs_1_), channel_id=1, source_target_pairs={{0,1},{1,0},{2,3},{3,2},{4,5},{5,4},{6,7},{7,6},{8,9},{9,8},{10,11... | collective-permute-start | bytes 18440 | tf_op jit(solution)/shard_map/ppermute | solution.py:588

commit v3 on v2

--- a/solution.py
+++ b/solution.py
@@ -18,7 +18,9 @@
 TILES = SPAN // LANES
 HALF_TILES = HALF_WIN // LANES
 PAD = 16
-GROUP = 1
+BAND_TOP = 137
+WIDTH = 2 * LANES
+CHUNKS = SPAN // WIDTH
 position = lax.axis_index
 VMEM_LIMIT = 16 * 1024 * 1024
 BF = jnp.bfloat16
@@ -86,45 +88,40 @@
         self.depth = 3 * self.full + PAD
         self.block = min(tm_count, 16)
         self.blocks = tm_count // self.block
-        self.folds = -(-(bins + self.rows - 1) // self.rows)
+        self.folds = (BAND_TOP + bins - 1) // self.rows + 1
         self.spec_rows = up_to(2 * self.half, 8)
         self.edge_rows = 2 * stations * TILES
         self.sent_rows = self.spec_rows + self.edge_rows
         assert length % SPAN == 0 and tm_count % self.block == 0
         assert stations == 2 and self.folds <= PAD
-        assert self.rows >= 2 and 0 < 3 * self.tail <= 8
+        assert self.rows >= 2 and 0 < 3 * self.tail <= 8 and self.depth <= LANES
 
     def row_order(self):
         j2 = np.arange(self.tm)[:, None] + self.tm * np.arange(self.half)[None, :]
         return j2.reshape(self.blocks, self.block, self.half).transpose(0, 2, 1).reshape(self.blocks, -1)
 
     def first_table(self):
-        j2 = self.row_order()[:, None, :, None]
-        tile = np.arange(TILES)[None, :, None, None]
-        total = self.tm * self.length
-        time = np.arange(self.rows) * SPAN + tile * LANES
-        angle = 2.0 * np.pi / total * (j2 * time % total)
-        parts = np.concatenate([np.cos(angle), -np.sin(angle)], axis=2)
-        high, low = np_split(parts)
-        full = self.full
-        pieces = [piece[..., :full] for piece in (high, high, low)]
-        for piece in (high, high, low):
-            rest = piece[..., full:]
-            pieces.append(np.pad(rest, ((0, 0), (0, 0), (0, 0), (0, self.tail - rest.shape[-1]))))
-        table = np.concatenate(pieces, axis=3)
-        gap = ((0, 0), (0, 0), (0, 0), (0, self.depth - table.shape[-1]))
-        return np.pad(table, gap).astype(jnp.bfloat16)
-
-    def lane_table(self):
-        angle = 2.0 * np.pi / (self.tm * self.length) * (
-            self.row_order()[:, :, None] * np.arange(LANES)
-        )
-        return np.stack([np.cos(angle), -np.sin(angle)], axis=1).astype(np.float32)
-
-
-def normalize(z, x, xs, sums, stack, edges):
-    rows, pad, top = z.rows, z.pad, 8
-    short = up_to(rows, 8)
+        period = self.tm * self.rows
+        angle = 2.0 * np.pi / period * (self.row_order()[:, :, None] * np.arange(self.rows) % period)
+        parts = np.concatenate([np.cos(angle), -np.sin(angle)], axis=1)
+        full, rest = parts[..., : self.full], parts[..., self.full :]
+        table = np.concatenate([full, full, full, rest, rest, rest], axis=2)
+        return np.pad(table, ((0, 0), (0, 0), (0, LANES - table.shape[2]))).astype(np.float32)
+
+    def low_lanes(self, lane):
+        at = 3 * self.full
+        third = (lane >= 2 * self.full) & (lane < at)
+        return third | ((lane >= at + 2 * self.tail) & (lane < at + 3 * self.tail))
+
+    def turn_table(self):
+        order = self.row_order().reshape(self.blocks, 1, -1, 1)
+        time = np.arange(SPAN).reshape(CHUNKS, 1, WIDTH)
+        angle = 2.0 * np.pi / (self.tm * self.length) * (order * time)
+        return np.stack([np.cos(angle), -np.sin(angle)], axis=2).astype(np.float32)
+
+
+def unpack(z, x, xs, edges):
+    rows, top = z.rows, 8
     for a in range(rows):
         xs[:, top + a, :] = x[:, a * SPAN : (a + 1) * SPAN].astype(F32)
     for s in range(z.stations):
@@ -132,103 +129,95 @@
             for c in range(TILES):
                 at = (side * z.stations + s) * TILES + c
                 edges[at : at + 1, :] = xs[s, top + a : top + a + 1, c * LANES : (c + 1) * LANES]
-    upto, onward, ones = window_tables()
-    kernel = jnp.concatenate([upto, onward, ones], axis=1)
+
+
+def window(z, s, xs, sums):
+    rows, pad, top = z.rows, z.pad, 8
+    short = up_to(rows, 8)
+    kernel = jnp.concatenate(window_tables()[:2], axis=1)
     group = 4
-    for s in range(z.stations):
-        for c0 in range(0, TILES, group):
-            part = jnp.concatenate(
-                [
-                    jnp.abs(xs[s, top : top + pad, c * LANES : (c + 1) * LANES]).astype(BF)
-                    for c in range(c0, c0 + group)
-                ],
-                axis=0,
-            )
-            got = jnp.dot(part, kernel, preferred_element_type=F32)
-            for k in range(group):
-                sums[s, c0 + k, top : top + short, :] = got[k * pad : k * pad + short]
+    for c0 in range(0, TILES, group):
+        parts = [
+            jnp.abs(xs[s, top : top + pad, c * LANES : (c + 1) * LANES])
+            for c in range(c0, c0 + group)
+        ]
+        part = jnp.concatenate([part.astype(BF) for part in parts], axis=0)
+        got = jnp.dot(part, kernel, preferred_element_type=F32)
+        for k in range(group):
+            value = got[k * pad : k * pad + short]
+            upto, onward = value[:, :LANES], value[:, LANES:]
+            sums[s, c0 + k, top : top + short, 0 : 2 * LANES] = value
+            sums[s, c0 + k, top : top + short, 2 * LANES :] = upto + (onward - parts[k][:short])
     blank = jnp.zeros((1, HALF_WIN), F32)
-    for s in range(z.stations):
-        xs[s, top : top + 1, 0:HALF_WIN] = blank
-        xs[s, top + rows - 1 : top + rows, HALF_WIN:SPAN] = blank
-    for s in range(z.stations):
-
-        def tile(kind, c):
-            turn, cc = divmod(c, TILES)
-            lines = slice(top + turn, top + turn + short)
-            return sums[s, cc, lines, kind * LANES : (kind + 1) * LANES]
-
-        ones_ = [tile(2, c) for c in range(1 - HALF_TILES, TILES + HALF_TILES - 1)]
-        twos = [ones_[c] + ones_[c + 1] for c in range(len(ones_) - 1)]
-        for c in range(TILES):
-            inner = (twos[c] + twos[c + 2]) + (twos[c + 4] + ones_[c + 6])
-            total = inner + (tile(1, c - HALF_TILES) + tile(0, c + HALF_TILES))
-            value = xs[s, top : top + short, c * LANES : (c + 1) * LANES]
-            value = value / (total * (1.0 / (2 * HALF_WIN + 1)) + EPS_MEAN)
-            high, low = split2(value[: z.full])
-            lanes = slice((c * z.stations + s) * LANES, (c * z.stations + s + 1) * LANES)
-            for k, part in enumerate((high, low, high)):
-                stack[k * z.full : (k + 1) * z.full, lanes] = part
-            rest = value[z.full :]
-            high = rest.astype(BF).astype(F32)
-            rest = high + pltpu.roll(rest - high, z.tail, 0) + pltpu.roll(high, 2 * z.tail, 0)
-            rest = jnp.concatenate([rest, jnp.zeros((PAD - rest.shape[0], LANES), F32)], axis=0)
-            stack[3 * z.full :, lanes] = rest.astype(BF)
-
-
-def fold_waves(fold):
+    xs[s, top : top + 1, 0:HALF_WIN] = blank
+    xs[s, top + rows - 1 : top + rows, HALF_WIN:SPAN] = blank
+
+
+def level(z, s, tiles, xs, sums, stack):
+    rows, top = z.rows, 8
+    short = up_to(rows, 8)
+
+    def tile(kind, c):
+        turn, cc = divmod(c, TILES)
+        lines = slice(top + turn, top + turn + short)
+        return sums[s, cc, lines, kind * LANES : (kind + 1) * LANES]
+
+    first = tiles[0] + 1 - HALF_TILES
+    single = [tile(2, c) for c in range(first, tiles[-1] + HALF_TILES)]
+    twos = [single[c] + single[c + 1] for c in range(len(single) - 1)]
+    for k, c in enumerate(tiles):
+        inner = (twos[k] + twos[k + 2]) + (twos[k + 4] + single[k + 6])
+        total = inner + (tile(1, c - HALF_TILES) + tile(0, c + HALF_TILES))
+        value = xs[s, top : top + short, c * LANES : (c + 1) * LANES]
+        value = value / (total * (1.0 / (2 * HALF_WIN + 1)) + EPS_MEAN)
+        high, low = split2(value[: z.full])
+        lanes = slice(c * LANES, (c + 1) * LANES)
+        for k2, part in enumerate((high, low, high)):
+            stack[s, k2 * z.full : (k2 + 1) * z.full, lanes] = part
+        rest = value[z.full :]
+        high = rest.astype(BF).astype(F32)
+        rest = high + pltpu.roll(rest - high, z.tail, 0) + pltpu.roll(high, 2 * z.tail, 0)
+        rest = jnp.concatenate([rest, jnp.zeros((PAD - rest.shape[0], LANES), F32)], axis=0)
+        stack[s, 3 * z.full :, lanes] = rest.astype(BF)
+
+
+def fold_weights(weight):
     lane = iota((PAD, SPAN), 1)
     for kind in range(2):
         turns = jnp.bitwise_and((iota((PAD, SPAN), 0) + kind) * lane, SPAN - 1).astype(F32)
         sine, cosine = sincos(turns * (1.0 / SPAN))
-        fold[kind, 0] = cosine
-        fold[kind, 1] = sine
-
-
-def fold_weights(z, base, fold, weight):
-    spot = iota((TILES, LANES), 0) * LANES + iota((TILES, LANES), 1)
-    turns = jnp.bitwise_and((base // z.rows) * spot, SPAN - 1).astype(F32)
-    sine, cosine = sincos(turns * (1.0 / SPAN))
-    b_cos = jnp.concatenate([cosine[c : c + 1] for c in range(TILES)], axis=1)
-    b_sin = jnp.concatenate([sine[c : c + 1] for c in range(TILES)], axis=1)
-    for kind in range(2):
-        w_cos, w_sin = fold[kind, 0], fold[kind, 1]
-        sine = w_sin * b_cos + w_cos * b_sin
-        cosine = w_cos * b_cos - w_sin * b_sin
         for h, (s, c) in enumerate(zip(split2(sine), split2(cosine))):
             table = ((c, s), (-s, c)) if kind == 0 else ((c, -s), (-s, -c))
             for part in range(2):
                 at = h * 4 * PAD + kind * 2 * PAD + part * PAD
-                for tile in range(TILES):
-                    for side in range(2):
-                        to = (2 * tile + side) * LANES
-                        weight[at : at + PAD, to : to + LANES] = table[part][side][
-                            :, tile * LANES : (tile + 1) * LANES
+                for side in range(2):
+                    for g in range(CHUNKS):
+                        to = (2 * g + side) * WIDTH
+                        weight[at : at + PAD, to : to + WIDTH] = table[part][side][
+                            :, g * WIDTH : (g + 1) * WIDTH
                         ]
 
 
 def transform_kernel(
-    z, band, flags, x, first, lanes_table, out,
-    band_s, flags_s, x_v, first_v, lanes_v, xs, sums, stack, edges, fold, weight, acc, both, spec, sems,
+    z, flags, x, first, turn, out,
+    flags_s, x_v, first_v, turn_v, table, xs, sums, stack, edges, weight, acc, both, spec, sems,
 ):
     half, block, tm = z.half, z.block, z.tm
     height = half * block
     index = pl.program_id(0)
     top, rows, pad = 8, z.rows, z.pad
-
-    get_first = pltpu.make_async_copy(first.at[index], first_v, sems.at[3])
-    get_lanes = pltpu.make_async_copy(lanes_table.at[index], lanes_v, sems.at[4])
+    get_first = pltpu.make_async_copy(first.at[index], first_v, sems.at[2])
+    get_turn = [
+        pltpu.make_async_copy(turn.at[index, g], turn_v.at[g], sems.at[3 + g]) for g in range(CHUNKS)
+    ]
 
     def prologue():
         copies = [
-            pltpu.make_async_copy(band, band_s, sems.at[0]),
+            pltpu.make_async_copy(x, x_v, sems.at[0]),
             pltpu.make_async_copy(flags, flags_s, sems.at[1]),
-            pltpu.make_async_copy(x, x_v, sems.at[2]),
         ]
-        for copy in copies:
+        for copy in copies + [get_first] + get_turn:
             copy.start()
-        get_lanes.start()
-        get_first.start()
         full = rows // 8 * 8
         for s in range(z.stations):
             xs[s, top + full : top + pad, :] = jnp.zeros((pad - full, SPAN), F32)
@@ -236,11 +225,14 @@
                 sums[s, c, 0:top, :] = jnp.zeros((top, 3 * LANES), F32)
                 sums[s, c, top + up_to(rows, 8) :, :] = jnp.zeros((8, 3 * LANES), F32)
         spec[:, z.spec_rows - 8 : z.spec_rows, :] = jnp.zeros((tm, 8, LANES), F32)
-        fold_waves(fold)
+        fold_weights(weight)
         for copy in copies:
             copy.wait()
-        fold_weights(z, band_s[0, 0], fold, weight)
-        normalize(z, x_v, xs, sums, stack, edges)
+        unpack(z, x_v, xs, edges)
+        for s in range(z.stations):
+            window(z, s, xs, sums)
+            if s == 0 or z.blocks > 1:
+                level(z, s, range(TILES), xs, sums, stack)
 
     if z.blocks == 1:
         prologue()
@@ -249,56 +241,60 @@
 
         @pl.when(index > 0)
         def _():
-            get_lanes.start()
-            get_first.start()
-
-    get_lanes.wait()
+            for copy in [get_first] + get_turn:
+                copy.start()
+
+    for copy in [get_first] + get_turn:
+        copy.wait()
     residue = index * block + iota((block, LANES), 0)
     sine, cosine = sincos(turns_of((position("tm") * residue).astype(F32), tm))
-    l_re = lanes_v[0].reshape(half, block, LANES)
-    l_im = lanes_v[1].reshape(half, block, LANES)
-    t_re = (l_re * cosine[None] + l_im * sine[None]).reshape(height, LANES)
-    t_im = (l_im * cosine[None] - l_re * sine[None]).reshape(height, LANES)
-    get_first.wait()
-    wide_lanes = z.stations * LANES
-
-    def first_stage(c):
+    f_re = first_v[:height].reshape(half, block, LANES)
+    f_im = first_v[height:].reshape(half, block, LANES)
+    low = z.low_lanes(iota((height, LANES), 1))
+    for k, value in enumerate(
+        (f_re * cosine[None] + f_im * sine[None], f_im * cosine[None] - f_re * sine[None])
+    ):
+        value = value.reshape(height, LANES)
+        high = value.astype(BF).astype(F32)
+        table[k * height : (k + 1) * height, :] = jnp.where(low, value - high, high).astype(BF)
+
+    def first_stage(s, g):
         return jnp.dot(
-            first_v[c],
-            stack[:, c * wide_lanes : (c + 1) * wide_lanes],
+            table[:, : z.depth],
+            stack[s, :, g * WIDTH : (g + 1) * WIDTH],
             preferred_element_type=F32,
         )
 
-    def second_stage(c0, parts):
-        w = weight[:, 2 * c0 * LANES : 2 * (c0 + GROUP) * LANES]
-        for s in range(z.stations):
-            left = jnp.concatenate([jnp.concatenate(piece, axis=1) for piece in parts[s]], axis=0)
-            got = lax.dot_general(left, w, (((1,), (1,)), ((), ())), preferred_element_type=F32)
-            value = got[:height] + got[height:]
-            acc[s] = value if c0 == 0 else acc[s] + value
-
+    def second_stage(s, g, parts):
+        w = weight[:, 2 * g * WIDTH : 2 * (g + 1) * WIDTH]
+        got = lax.dot_general(parts, w, (((1,), (1,)), ((), ())), preferred_element_type=F32)
+        value = got[:height] + got[height:]
+        acc[s] = value if g == 0 else acc[s] + value
+
+    def settle(s):
+        value = acc[s] + pltpu.roll(acc[s], LANES // 2, 1)
+        return value * flags_s[s].astype(F32)
+
+    steps = [(s, g) for s in range(z.stations) for g in range(CHUNKS)]
+    coming = first_stage(*steps[0])
     waiting = None
-    coming = [first_stage(c) for c in range(GROUP)]
-    for c0 in range(0, TILES, GROUP):
-        current = coming
-        parts = [[[], []] for _ in range(z.stations)]
-        for f in current:
-            for s in range(z.stations):
-                f_re = f[:height, s * LANES : (s + 1) * LANES]
-                f_im = f[height:, s * LANES : (s + 1) * LANES]
-                for value in (f_re * t_re - f_im * t_im, f_re * t_im + f_im * t_re):
-                    high, low = split2(value)
-                    parts[s][0].append(high)
-                    parts[s][1].append(low)
-        if c0 + GROUP < TILES:
-            coming = [first_stage(c) for c in range(c0 + GROUP, c0 + 2 * GROUP)]
+    for k, (s, g) in enumerate(steps):
+        f_re, f_im = coming[:height], coming[height:]
+        t_re, t_im = turn_v[g, 0], turn_v[g, 1]
+        re_h, re_l = split2(f_re * t_re - f_im * t_im)
+        im_h, im_l = split2(f_re * t_im + f_im * t_re)
+        parts = jnp.concatenate(
+            [jnp.concatenate([re_h, im_h], axis=1), jnp.concatenate([re_l, im_l], axis=1)], axis=0
+        )
+        if s == 0 and z.blocks == 1:
+            level(z, 1, range(2 * g, 2 * g + 2), xs, sums, stack)
+        if k + 1 < len(steps):
+            coming = first_stage(*steps[k + 1])
         if waiting is not None:
-            second_stage(c0 - GROUP, waiting)
+            second_stage(*steps[k - 1], waiting)
         waiting = parts
-    second_stage(TILES - GROUP, waiting)
-    zero, one = (
-        (acc[s] + pltpu.roll(acc[s], LANES // 2, 1)) * flags_s[s].astype(F32) for s in range(2)
-    )
+    second_stage(*steps[-1], waiting)
+    zero, one = settle(0), settle(1)
     lane = iota((height, LANES), 1)
     early = jnp.bitwise_and(lane, LANES // 2 - 1) < LANES // 4
     direct = jnp.where(early, zero, pltpu.roll(one, LANES // 4, 1))
@@ -343,53 +339,56 @@
     return pltpu.CompilerParams(vmem_limit_bytes=VMEM_LIMIT)
 
 
-def transform(z, band, flags, x):
-    band = band.reshape(1, 1)
+def transform(z, flags, x):
     height = z.half * z.block
-    first, lanes = z.first_table(), z.lane_table()
+    first, turn = z.first_table(), z.turn_table()
     return pl.pallas_call(
         functools.partial(transform_kernel, z),
         grid=(z.blocks,),
-        in_specs=[HBM_SPEC] * 5,
+        in_specs=[HBM_SPEC] * 4,
         out_specs=VMEM_SPEC,
         out_shape=jax.ShapeDtypeStruct((z.tm, z.sent_rows, LANES), BF),
         scratch_shapes=[
-            pltpu.SMEM((1, 1), jnp.int32),
             pltpu.SMEM((z.stations,), jnp.int32),
             pltpu.VMEM(x.shape, BF),
+            pltpu.VMEM(first.shape[1:], F32),
+            pltpu.VMEM(turn.shape[1:], F32),
             pltpu.VMEM(first.shape[1:], BF),
-            pltpu.VMEM(lanes.shape[1:], F32),
             pltpu.VMEM((z.stations, 8 + z.pad, SPAN), F32),
             pltpu.VMEM((z.stations, TILES, 16 + up_to(z.rows, 8), 3 * LANES), F32),
-            pltpu.VMEM((z.depth, z.stations * SPAN), BF),
+            pltpu.VMEM((z.stations, z.depth, SPAN), BF),
             pltpu.VMEM((z.edge_rows, LANES), F32),
-            pltpu.VMEM((2, 2, PAD, SPAN), F32),
             pltpu.VMEM((LANES, 2 * SPAN), BF),
             pltpu.VMEM((z.stations, height, LANES), F32),
             pltpu.VMEM((2, height, LANES), F32),
             pltpu.VMEM((z.tm, z.spec_rows, LANES), F32),
-            pltpu.SemaphoreType.DMA((5,)),
+            pltpu.SemaphoreType.DMA((3 + CHUNKS,)),
         ],
         name="transform",
-    )(band, flags, x, jnp.asarray(first), jnp.asarray(lanes))
+    )(flags, x, jnp.asarray(first), jnp.asarray(turn))
 
 
 def table_kernel(
-    z, band, flags, choose, keep, steps, turns, near, phase, switch, band_s, flags_s, sems
+    z, offsets, band, flags, mask, choose, keep, steps, turns, near, phase, switch, pairs,
+    band_s, flags_s, mask_s, sems,
 ):
     rows, tm, bins, half = z.rows, z.tm, z.bins, z.half
     copies = [
         pltpu.make_async_copy(band, band_s, sems.at[0]),
         pltpu.make_async_copy(flags, flags_s, sems.at[1]),
+        pltpu.make_async_copy(mask, mask_s, sems.at[2]),
     ]
     for copy in copies:
         copy.start()
     for copy in copies:
         copy.wait()
+    here = position("sta")
+    for k, offset in enumerate(offsets):
+        pairs[k] = jnp.full((2, LANES), mask_s[here, here ^ offset].astype(F32))
     base, residue = band_s[0, 0], position("tm")
     for s in range(z.stations):
         switch[s] = jnp.full((TILES, LANES), flags_s[s].astype(F32))
-    spot = iota_f((1, bins), 1) + (base % rows).astype(F32)
+    spot = iota_f((1, bins), 1) + base.astype(F32)
     fold = jnp.floor((spot + 0.5) * (1.0 / rows))
     rest = spot - fold * rows
     row = iota_f((z.spec_rows, bins), 0)
@@ -419,15 +418,16 @@
     phase[1] = -p_sin
 
 
-def tables(z, band, flags):
+def tables(z, offsets, band, flags, mask):
     return pl.pallas_call(
-        functools.partial(table_kernel, z),
-        in_specs=[HBM_SPEC, HBM_SPEC],
-        out_specs=[VMEM_SPEC] * 7,
+        functools.partial(table_kernel, z, offsets),
+        in_specs=[HBM_SPEC] * 3,
+        out_specs=[VMEM_SPEC] * 8,
         scratch_shapes=[
             pltpu.SMEM((1, 1), jnp.int32),
             pltpu.SMEM((z.stations,), jnp.int32),
-            pltpu.SemaphoreType.DMA((2,)),
+            pltpu.SMEM(mask.shape, jnp.int32),
+            pltpu.SemaphoreType.DMA((3,)),
         ],
         out_shape=[
             jax.ShapeDtypeStruct((z.tm, z.spec_rows, z.bins), BF),
@@ -437,11 +437,12 @@
             jax.ShapeDtypeStruct((z.bins, z.bins), BF),
             jax.ShapeDtypeStruct((2, z.tm, LANES), F32),
             jax.ShapeDtypeStruct((z.stations, TILES, LANES), F32),
+            jax.ShapeDtypeStruct((len(offsets), 2, LANES), F32),
         ],
         compiler_params=params(),
         cost_estimate=pl.CostEstimate(flops=4000000, bytes_accessed=2000000, transcendentals=0),
         name="tables",
-    )(band.reshape(1, 1), flags)
+    )(band.reshape(1, 1), flags, mask)
 
 
 def sublane_sums(value, row):
@@ -541,7 +542,7 @@
     )(got, *made)
 
 
-def cross_kernel(z, offsets, mask, stacks, *refs):
+def cross_kernel(z, offsets, pairs, stacks, *refs):
     pieces, out = refs[:-1], refs[-1]
     here = position("sta")
     mine = pieces[0][...]
@@ -550,26 +551,25 @@
     for i in range(z.stations):
         re, im = mine[2 * i : 2 * i + 1], mine[2 * i + 1 : 2 * i + 2]
         sides.append((jnp.concatenate([re, im], axis=0), jnp.concatenate([im, -re], axis=0)))
-    for offset, piece in zip(offsets, pieces):
-        source = here ^ offset
-        on = mask[here, source].astype(F32)
+    for k, (offset, piece) in enumerate(zip(offsets, pieces)):
+        on = jnp.concatenate([pairs[k]] * (bins // LANES), axis=1)
         for j in range(z.stations):
-            re = jnp.broadcast_to(piece[2 * j : 2 * j + 1, :] * on, (2, bins))
-            im = jnp.broadcast_to(piece[2 * j + 1 : 2 * j + 2, :] * on, (2, bins))
-            column = source * z.stations + j
+            re = jnp.broadcast_to(piece[2 * j : 2 * j + 1, :], (2, bins)) * on
+            im = jnp.broadcast_to(piece[2 * j + 1 : 2 * j + 2, :], (2, bins)) * on
+            column = (here ^ offset) * z.stations + j
             for i, (p, q) in enumerate(sides):
                 out[i, column] = stacks[i, column] + (re * p + im * q)
 
 
-def cross(z, offsets, mask, stacks, pieces):
+def cross(z, offsets, pairs, stacks, pieces):
     return pl.pallas_call(
         functools.partial(cross_kernel, z, offsets),
-        in_specs=[SMEM_SPEC] + [VMEM_SPEC] * (1 + len(pieces)),
+        in_specs=[VMEM_SPEC] * (2 + len(pieces)),
         out_specs=VMEM_SPEC,
         out_shape=jax.ShapeDtypeStruct(stacks.shape, F32),
         compiler_params=params(),
         name="cross",
-    )(mask, stacks, *pieces)
+    )(pairs, stacks, *pieces)
 
 
 def shards(traces, station_flags, tile_mask, band_block, stacks):
@@ -577,18 +577,18 @@
     stations, length = traces.shape
     z = Sizes(stations, length, tm_count, stacks.shape[-1])
     assert sta_count & (sta_count - 1) == 0
-    sent = transform(z, band_block, station_flags, traces)
+    sent = transform(z, station_flags, traces)
     got = lax.all_to_all(sent, "tm", split_axis=0, concat_axis=0, tiled=True)
-    made = tables(z, band_block, station_flags)
-    white = spectrum(z, got, made)
-    offsets, pieces = [0], [white]
-    bit = sta_count // 2
-    while bit:
-        pairs = [(i, i ^ bit) for i in range(sta_count)]
-        pieces += [lax.ppermute(piece, "sta", pairs) for piece in pieces]
+    offsets = [0]
+    bits = [1 << k for k in reversed(range(sta_count.bit_length() - 1))]
+    for bit in bits:
         offsets += [offset ^ bit for offset in offsets]
-        bit //= 2
-    return cross(z, offsets, tile_mask, stacks, pieces)
+    *made, pairs = tables(z, offsets, band_block, station_flags, tile_mask)
+    pieces = [spectrum(z, got, made)]
+    for bit in bits:
+        swap = [(i, i ^ bit) for i in range(sta_count)]
+        pieces += [lax.ppermute(piece, "sta", swap) for piece in pieces]
+    return cross(z, offsets, pairs, stacks, pieces)
 
 
 def solution(mesh):

time: 26.3 us -> 25.2 us (0.958)
  local copies, waits for them, and re-layouts: 0.66 us -> 0.01 us
  Pallas kernels: 6.71 us -> 6.13 us
    unnamed x6, local copies, waits for them, and re-layouts: 0.66 us -> 0.01 us
    pallas_call x2, Pallas kernels: 2.25 us -> 1.72 us  [the longest x1 1.05 us: tables(): pl.pallas_call(functools.partial(table_kernel, z, offsets), in_specs=[HBM...]
where the time goes in v3:
time: 25.2 us; the launch traced here: 24.9 us
  waiting for transfers between devices  9.03 us (36%)
  starting transfers between devices  9.01 us (36%)
  Pallas kernels  6.13 us (24%)
  between operations  0.7 us (3%)
    all_to_all x1, starting transfers between devices, shards(): got = lax.all_to_all(sent, 'tm', split_axis=0, concat_axis=0, tiled=True)  7.45 us
    all_to_all x1, waiting for transfers between devices, shards(): got = lax.all_to_all(sent, 'tm', split_axis=0, concat_axis=0, tiled=True)  5.72 us
    pallas_call x1, Pallas kernels, transform(): pl.pallas_call(functools.partial(transform_kernel, z), grid=(z.blocks,),...  3.55 us
    ppermute x3, waiting for transfers between devices, shards(): pieces += [lax.ppermute(piece, 'sta', swap) for piece in pieces]  3.3 us
    ppermute x3, starting transfers between devices, shards(): pieces += [lax.ppermute(piece, 'sta', swap) for piece in pieces]  1.56 us
    pallas_call x1, Pallas kernels, tables(): pl.pallas_call(functools.partial(table_kernel, z, offsets), in_specs=[HBM...  1.05 us
    pallas_call x1, Pallas kernels, spectrum(): pl.pallas_call(functools.partial(spectrum_kernel, z), in_specs=[VMEM_SPEC...  0.86 us
    pallas_call x1, Pallas kernels, cross(): pl.pallas_call(functools.partial(cross_kernel, z, offsets), in_specs=[VME...  0.67 us
  transfers between devices with their start and end apart: 4, of which 3 were waited for; matrix products, arithmetic and copies ran while one was open for 0% of the time, Pallas kernels for 4%

profile of v3, /device:TPU:0, one launch (start us, length us, event | category | flops | bytes accessed | tf_op | source)
XLA Modules:
  0.0 24.9 jit_solution(650508627184449417)
XLA Ops:
  0.0 0.0 copy-start.1
  0.0 0.0 copy-start.2
  0.0 3.6 %transform.1 = bf16[8,72,128]{2,1,0:T(8,128)(2,1)} custom-call(s32[2]{0:T(128)} %flags.3, bf16[2,33792]{1,0:T(2,128)(2,1)} %x.1, f32[1,272,128]{2,1,0:T(8,128)} %constant.4.clone.first, f32[1,4,2,136,256]{4,3,2,1,0:T(8,128)} %constant.5.clone.turn), custom_call_target="tpu_custom_call" | custom-call | tf_op jit(solution)/shard_map/transform/pallas_call | solution.py:345
  3.6 0.0 copy-start
  3.6 7.5 %all-to-all-start = ((bf16[8,72,128]{2,1,0:T(8,128)(2,1)}), bf16[8,72,128]{2,1,0:T(8,128)(2,1)S(1)}, u32[]{:S(2)}, u32[]{:S(2)}) async-start(bf16[8,72,128]{2,1,0:T(8,128)(2,1)} %transform.1), calls=%async_computation | async-start | bytes 294912 | tf_op jit(solution)/shard_map/all_to_all | solution.py:581
  11.7 0.0 copy-done.1
  11.7 0.0 copy-done.2
  11.7 1.1 %tables.1 = (bf16[8,40,384]{2,1,0:T(8,128)(2,1)S(1)}, f32[16,384]{1,0:T(8,128)S(1)}, bf16[64,768]{1,0:T(8,128)(2,1)S(1)}, f32[2,128,384]{2,1,0:T(8,128)S(1)}, bf...) custom-call(s32[1,1]{1,0:T(1,128)} %bitcast.1.band, ...), custom_call_target="tpu_custom_call" | custom-call | flops 4000000 | bytes 2000000 | tf_op jit(solution)/shard_map/tables/pallas_call | solution.py:422
  12.8 5.7 %all-to-all-done.got = bf16[8,72,128]{2,1,0:T(8,128)(2,1)S(1)} async-done(((bf16[8,72,128]{2,1,0:T(8,128)(2,1)}), bf16[8,72,128]{2,1,0:T(8,128)(2,1)S(1)}, u32[]{:S(2)}, u32[]{:S(2)}) %all-to-all-start) | async-done | bytes 147488 | tf_op jit(solution)/shard_map/all_to_all | solution.py:581
  18.5 0.9 %spectrum.1.refs_0_ = f32[4,384]{1,0:T(4,128)S(1)} custom-call(bf16[8,72,128]{2,1,0:T(8,128)(2,1)S(1)} %all-to-all-done.got, bf16[8,40,384]{2,1,0:T(8,128)(2,1)S(1)} %get-tuple-element.14.choose, f32[16,384]{1,0:T(8,128)S(1)} %get-tuple-element.15.keep, bf16[64,768]{1,0:T(8,128)(2,1)S(1)} %get-tuple-element.16.steps, ...), custom_call_target="tpu_custom_call" | custom-call | tf_op jit(solution)/shard_map/spectrum/pallas_call | solution.py:535
  19.3 1.6 %collective-permute-start = (f32[4,384]{1,0:T(4,128)S(1)}, f32[4,384]{1,0:T(4,128)S(1)}, u32[]{:S(2)}, u32[]{:S(2)}) collective-permute-start(f32[4,384]{1,0:T(4,128)S(1)} %spectrum.1.refs_0_), channel_id=1, source_target_pairs={{0,2},{1,3},{2,0},{3,1},{4,6},{5,7},{6,4},{7,5},{8,10},{9,11},{10,... | collective-permute-start | bytes 18440 | tf_op jit(solution)/shard_map/ppermute | solution.py:590
  20.9 0.0 collective-permute-start.1
  20.9 2.1 %collective-permute-done.refs_1_ = f32[4,384]{1,0:T(4,128)S(1)} collective-permute-done((f32[4,384]{1,0:T(4,128)S(1)}, f32[4,384]{1,0:T(4,128)S(1)}, u32[]{:S(2)}, u32[]{:S(2)}) %collective-permute-start) | collective-permute-done | bytes 6176 | tf_op jit(solution)/shard_map/ppermute | solution.py:590
  23.0 0.0 collective-permute-start.2
  23.0 0.0 collective-permute-done.1.refs_2_
  23.1 1.2 %collective-permute-done.2.refs_3_ = f32[4,384]{1,0:T(4,128)S(1)} collective-permute-done((f32[4,384]{1,0:T(4,128)S(1)}, f32[4,384]{1,0:T(4,128)S(1)}, u32[]{:S(2)}, u32[]{:S(2)}) %collective-permute-start.2) | collective-permute-done | bytes 6176 | tf_op jit(solution)/shard_map/ppermute | solution.py:590
  24.2 0.0 copy-done
  24.2 0.7 %cross.1 = f32[2,8,2,384]{3,2,1,0:T(2,128)} custom-call(f32[4,2,128]{2,1,0:T(2,128)S(1)} %get-tuple-element.13.pairs, f32[2,8,2,384]{3,2,1,0:T(2,128)S(1)} %copy-done, f32[4,384]{1,0:T(4,128)S(1)} %spectrum.1.refs_0_, f32[4,384]{1,0:T(4,128)S(1)} %collective-permute-done.refs_1_, f32[4,384]{1,0:T(4,128)S(1)} %collective-permute-done.1.refs_2_, ...), custom_call_target="tpu_custom_call" | custom-call | tf_op jit(solution)/shard_map/cross/pallas_call | solution.py:565
Async XLA Ops:
  0.0 11.7 %copy-start.1 = (s32[2]{0:T(128)S(1)}, s32[2]{0:T(128)}, u32[]{:S(2)}) copy-start(s32[2]{0:T(128)} %flags.3) | copy-start | bytes 28
  0.0 11.7 %copy-start.2 = (s32[4,4]{1,0:T(4,128)S(1)}, s32[4,4]{1,0:T(4,128)}, u32[]{:S(2)}) copy-start(s32[4,4]{1,0:T(4,128)} %mask.1) | copy-start | bytes 196
  3.6 20.7 %copy-start = (f32[2,8,2,384]{3,2,1,0:T(2,128)S(1)}, f32[2,8,2,384]{3,2,1,0:T(2,128)}, u32[]{:S(2)}) copy-start(f32[2,8,2,384]{3,2,1,0:T(2,128)} %stacks.1) | copy-start | bytes 147460
  3.6 14.9 %all-to-all-start = ((bf16[8,72,128]{2,1,0:T(8,128)(2,1)}), bf16[8,72,128]{2,1,0:T(8,128)(2,1)S(1)}, u32[]{:S(2)}, u32[]{:S(2)}) async-start(bf16[8,72,128]{2,1,0:T(8,128)(2,1)} %transform.1), calls=%async_computation | async-start | bytes 294912 | tf_op jit(solution)/shard_map/all_to_all | solution.py:581
  19.3 3.7 %collective-permute-start = (f32[4,384]{1,0:T(4,128)S(1)}, f32[4,384]{1,0:T(4,128)S(1)}, u32[]{:S(2)}, u32[]{:S(2)}) collective-permute-start(f32[4,384]{1,0:T(4,128)S(1)} %spectrum.1.refs_0_), channel_id=1, source_target_pairs={{0,2},{1,3},{2,0},{3,1},{4,6},{5,7},{6,4},{7,5},{8,10},{9,11},{10,... | collective-permute-start | bytes 18440 | tf_op jit(solution)/shard_map/ppermute | solution.py:590
  20.9 2.1 %collective-permute-start.1 = (f32[4,384]{1,0:T(4,128)S(1)}, f32[4,384]{1,0:T(4,128)S(1)}, u32[]{:S(2)}, u32[]{:S(2)}) collective-permute-start(f32[4,384]{1,0:T(4,128)S(1)} %spectrum.1.refs_0_), channel_id=1, source_target_pairs={{0,1},{1,0},{2,3},{3,2},{4,5},{5,4},{6,7},{7,6},{8,9},{9,8},{10,11... | collective-permute-start | bytes 18440 | tf_op jit(solution)/shard_map/ppermute | solution.py:590
  23.0 1.2 %collective-permute-start.2 = (f32[4,384]{1,0:T(4,128)S(1)}, f32[4,384]{1,0:T(4,128)S(1)}, u32[]{:S(2)}, u32[]{:S(2)}) collective-permute-start(f32[4,384]{1,0:T(4,128)S(1)} %collective-permute-done.refs_1_), channel_id=1, source_target_pairs={{0,1},{1,0},{2,3},{3,2},{4,5},{5,4},{6,7},{7,6},{8,9},{9,8},{10,11... | collective-permute-start | bytes 18440 | tf_op jit(solution)/shard_map/ppermute | solution.py:590

commit v4 on v3

--- a/solution.py
+++ b/solution.py
@@ -89,20 +89,32 @@
         self.block = min(tm_count, 16)
         self.blocks = tm_count // self.block
         self.folds = (BAND_TOP + bins - 1) // self.rows + 1
-        self.spec_rows = up_to(2 * self.half, 8)
+        self.lift = up_to(self.half, 2)
+        self.spec_rows = up_to(2 * self.lift, 8)
         self.edge_rows = 2 * stations * TILES
         self.sent_rows = self.spec_rows + self.edge_rows
         assert length % SPAN == 0 and tm_count % self.block == 0
         assert stations == 2 and self.folds <= PAD
         assert self.rows >= 2 and 0 < 3 * self.tail <= 8 and self.depth <= LANES
 
+    def parity_tables(self):
+        residue = np.arange(self.tm).reshape(-1, 2).T[:, None, :]
+        order = (residue + self.tm * np.arange(self.lift)[None, :, None]).reshape(2, -1)
+        return self.first_of(order), self.turn_of(order)
+
     def row_order(self):
         j2 = np.arange(self.tm)[:, None] + self.tm * np.arange(self.half)[None, :]
         return j2.reshape(self.blocks, self.block, self.half).transpose(0, 2, 1).reshape(self.blocks, -1)
 
     def first_table(self):
+        return self.first_of(self.row_order())
+
+    def turn_table(self):
+        return self.turn_of(self.row_order())
+
+    def first_of(self, order):
         period = self.tm * self.rows
-        angle = 2.0 * np.pi / period * (self.row_order()[:, :, None] * np.arange(self.rows) % period)
+        angle = 2.0 * np.pi / period * (order[:, :, None] * np.arange(self.rows) % period)
         parts = np.concatenate([np.cos(angle), -np.sin(angle)], axis=1)
         full, rest = parts[..., : self.full], parts[..., self.full :]
         table = np.concatenate([full, full, full, rest, rest, rest], axis=2)
@@ -113,8 +125,8 @@
         third = (lane >= 2 * self.full) & (lane < at)
         return third | ((lane >= at + 2 * self.tail) & (lane < at + 3 * self.tail))
 
-    def turn_table(self):
-        order = self.row_order().reshape(self.blocks, 1, -1, 1)
+    def turn_of(self, order):
+        order = order.reshape(order.shape[0], 1, -1, 1)
         time = np.arange(SPAN).reshape(CHUNKS, 1, WIDTH)
         angle = 2.0 * np.pi / (self.tm * self.length) * (order * time)
         return np.stack([np.cos(angle), -np.sin(angle)], axis=2).astype(np.float32)
@@ -369,7 +381,7 @@
 
 
 def table_kernel(
-    z, offsets, band, flags, mask, choose, keep, steps, turns, near, phase, switch, pairs,
+    z, offsets, split, band, flags, mask, choose, keep, steps, turns, near, phase, switch, pairs,
     band_s, flags_s, mask_s, sems,
 ):
     rows, tm, bins, half = z.rows, z.tm, z.bins, z.half
@@ -392,11 +404,10 @@
     fold = jnp.floor((spot + 0.5) * (1.0 / rows))
     rest = spot - fold * rows
     row = iota_f((z.spec_rows, bins), 0)
-    last = (rows - 1 + half + (residue == 0).astype(jnp.int32)).astype(F32)
-    mirror = last - row
-    target = jnp.where(row < half, row, jnp.where(mirror >= half, mirror, -1.0))
-    one = (target == rest).astype(F32).astype(BF)
-    for p in range(tm):
+    last = (rows - 1 + split + (residue == 0).astype(jnp.int32)).astype(F32)
+    mirror = jnp.where((row >= split) & (last - row >= half), last - row, -1.0)
+    one = (jnp.where(row < half, row, mirror) == rest).astype(F32).astype(BF)
+    for p in range(choose.shape[0]):
         choose[p] = one
     keep[...] = (iota_f((PAD, bins), 0) == fold).astype(F32)
     freq = (residue + tm * (base + iota((1, bins), 1))).astype(F32)
@@ -418,9 +429,9 @@
     phase[1] = -p_sin
 
 
-def tables(z, offsets, band, flags, mask):
+def tables(z, offsets, split, copies, band, flags, mask):
     return pl.pallas_call(
-        functools.partial(table_kernel, z, offsets),
+        functools.partial(table_kernel, z, offsets, split),
         in_specs=[HBM_SPEC] * 3,
         out_specs=[VMEM_SPEC] * 8,
         scratch_shapes=[
@@ -430,7 +441,7 @@
             pltpu.SemaphoreType.DMA((3,)),
         ],
         out_shape=[
-            jax.ShapeDtypeStruct((z.tm, z.spec_rows, z.bins), BF),
+            jax.ShapeDtypeStruct((copies, z.spec_rows, z.bins), BF),
             jax.ShapeDtypeStruct((PAD, z.bins), F32),
             jax.ShapeDtypeStruct((8 * TILES, 2 * z.bins), BF),
             jax.ShapeDtypeStruct((2, LANES, z.bins), F32),
@@ -457,6 +468,39 @@
     parts = got[:, 0:at, :].astype(F32).reshape(tm * at, LANES).astype(BF)
     weights = choose[...].astype(F32).reshape(tm * at, bins).astype(BF)
     placed = lax.dot_general(parts, weights, (((0,), (0,)), ((), ())), preferred_element_type=F32)
+    side_rows = z.stations * TILES
+    ends = [
+        got[:, at + k * side_rows : at + (k + 1) * side_rows, :].astype(F32).reshape(-1, LANES)
+        for k in range(2)
+    ]
+    whiten(z, placed, ends, keep, steps, turns, near, phase, switch, out)
+
+
+def gathered_kernel(
+    z, kept, came, went, choose, keep, steps, turns, near, phase, switch, out, ends
+):
+    tm = z.tm
+    piece = came[0].astype(F32)
+    total = kept[0] + (piece + pltpu.roll(piece, LANES // 2, 1))
+    placed = lax.dot_general(
+        halves(total), choose[0], (((0,), (0,)), ((), ())), preferred_element_type=F32
+    )
+    here = position("tm")
+    for s in range(tm):
+        source, slot = (went, s) if s < tm // 2 else (came, s - tm // 2)
+        ends[here ^ s] = source[1 + slot, 0 : z.edge_rows, :].astype(F32)
+    side_rows = z.stations * TILES
+    sides = [ends[:, k * side_rows : (k + 1) * side_rows, :].reshape(-1, LANES) for k in range(2)]
+    whiten(z, placed, sides, keep, steps, turns, near, phase, switch, out)
+
+
+def halves(value):
+    high = value.astype(BF).astype(F32)
+    return jnp.where(iota(value.shape, 1) < LANES // 2, high, value - high).astype(BF)
+
+
+def whiten(z, placed, ends, keep, steps, turns, near, phase, switch, out):
+    tm, bins = z.tm, z.bins
     mask = keep[...]
     folded = [
         jnp.sum(placed[k * PAD : (k + 1) * PAD] * mask, axis=0, keepdims=True)
@@ -467,10 +511,7 @@
     row = iota((TILES, LANES), 0)
     late = row >= HALF_TILES
     sides = []
-    side_rows = z.stations * TILES
-    for side, table in ((0, upto), (1, onward)):
-        rows = slice(at + side * side_rows, at + (side + 1) * side_rows)
-        value = got[:, rows, :].astype(F32).reshape(tm * side_rows, LANES)
+    for value, table in zip(ends, (upto, onward)):
         sums = jnp.dot(
             jnp.abs(value).astype(BF),
             jnp.concatenate([table, ones], axis=1),
@@ -542,6 +583,219 @@
     )(got, *made)
 
 
+def gathered(z, kept, came, went, made):
+    return pl.pallas_call(
+        functools.partial(gathered_kernel, z),
+        in_specs=[VMEM_SPEC] * 10,
+        out_specs=VMEM_SPEC,
+        out_shape=jax.ShapeDtypeStruct((2 * z.stations, z.bins), F32),
+        scratch_shapes=[pltpu.VMEM((z.tm, z.edge_rows, LANES), F32)],
+        compiler_params=params(),
+        name="spectrum",
+    )(kept, came, went, *made)
+
+
+def half_transform(z, parity, table, turn, stack, weight, flags, acc, both, spec, before):
+    count, lift = z.tm // 2, z.lift
+    height = lift * count
+
+    def first_stage(s, g):
+        return jnp.dot(
+            table[:, : z.depth],
+            stack[s, :, g * WIDTH : (g + 1) * WIDTH],
+            preferred_element_type=F32,
+        )
+
+    def second_stage(s, g, parts):
+        w = weight[:, 2 * g * WIDTH : 2 * (g + 1) * WIDTH]
+        got = lax.dot_general(parts, w, (((1,), (1,)), ((), ())), preferred_element_type=F32)
+        value = got[:height] + got[height:]
+        acc[s] = value if g == 0 else acc[s] + value
+
+    def settle(s):
+        return (acc[s] + pltpu.roll(acc[s], LANES // 2, 1)) * flags[s, 0:1, :]
+
+    steps = [(s, g) for s in range(z.stations) for g in range(CHUNKS)]
+    coming = first_stage(*steps[0])
+    waiting = None
+    for k, (s, g) in enumerate(steps):
+        f_re, f_im = coming[:height], coming[height:]
+        t_re, t_im = turn[g, 0], turn[g, 1]
+        re_h, re_l = split2(f_re * t_re - f_im * t_im)
+        im_h, im_l = split2(f_re * t_im + f_im * t_re)
+        parts = jnp.concatenate(
+            [jnp.concatenate([re_h, im_h], axis=1), jnp.concatenate([re_l, im_l], axis=1)], axis=0
+        )
+        if before is not None and s == 0:
+            before(g)
+        if k + 1 < len(steps):
+            coming = first_stage(*steps[k + 1])
+        if waiting is not None:
+            second_stage(*steps[k - 1], waiting)
+        waiting = parts
+    second_stage(*steps[-1], waiting)
+    zero, one = settle(0), settle(1)
+    lane = iota((height, LANES), 1)
+    early = jnp.bitwise_and(lane, LANES // 2 - 1) < LANES // 4
+    both[0] = jnp.where(early, zero, pltpu.roll(one, LANES // 4, 1))
+    both[1] = jnp.where(early, pltpu.roll(zero, LANES // 4, 1), one)
+    for j in range(count):
+        lines = pl.ds(j, lift, stride=count)
+        spec[j, 0:lift, :] = both[0, lines, :]
+        spec[lax.rem(2 * count - parity - j, count), lift : 2 * lift, :] = both[1, lines, :]
+
+
+def away_kernel(
+    z, flags, x, first, turn, message, stack, weight, home_table, home_turn, switch,
+    flags_s, x_v, first_v, turn_v, table, xs, sums, edges, acc, both, spec, sems,
+):
+    rows, pad, top = z.rows, z.pad, 8
+    count, height = z.tm // 2, z.lift * (z.tm // 2)
+    here = position("tm")
+    home = jnp.bitwise_and(here, 1)
+    away = 1 - home
+    copies = [
+        pltpu.make_async_copy(x, x_v, sems.at[0]),
+        pltpu.make_async_copy(flags, flags_s, sems.at[1]),
+        pltpu.make_async_copy(first, first_v, sems.at[2]),
+        pltpu.make_async_copy(turn.at[away], turn_v, sems.at[3]),
+        pltpu.make_async_copy(turn.at[home], home_turn, sems.at[4]),
+    ]
+    for copy in copies:
+        copy.start()
+    full = rows // 8 * 8
+    for s in range(z.stations):
+        xs[s, top + full : top + pad, :] = jnp.zeros((pad - full, SPAN), F32)
+        for c in range(TILES):
+            sums[s, c, 0:top, :] = jnp.zeros((top, 3 * LANES), F32)
+            sums[s, c, top + up_to(rows, 8) :, :] = jnp.zeros((8, 3 * LANES), F32)
+    spec[:, z.spec_rows - 8 : z.spec_rows, :] = jnp.zeros((count, 8, LANES), F32)
+    fold_weights(weight)
+    copies[0].wait()
+    copies[1].wait()
+    unpack(z, x_v, xs, edges)
+    for s in range(z.stations):
+        window(z, s, xs, sums)
+        switch[s] = jnp.full((TILES, LANES), flags_s[s].astype(F32))
+    level(z, 0, range(TILES), xs, sums, stack)
+    for copy in copies[2:]:
+        copy.wait()
+    low = z.low_lanes(iota((height, LANES), 1))
+    for parity, to in ((away, table), (home, home_table)):
+        residue = 2 * iota((count, LANES), 0) + parity
+        sine, cosine = sincos(turns_of((here * residue).astype(F32), z.tm))
+        f_re = first_v[parity, :height].reshape(z.lift, count, LANES)
+        f_im = first_v[parity, height:].reshape(z.lift, count, LANES)
+        for k, value in enumerate(
+            (f_re * cosine[None] + f_im * sine[None], f_im * cosine[None] - f_re * sine[None])
+        ):
+            value = value.reshape(height, LANES)
+            high = value.astype(BF).astype(F32)
+            to[k * height : (k + 1) * height, :] = jnp.where(low, value - high, high).astype(BF)
+    half_transform(
+        z, away, table, turn_v, stack, weight, switch, acc, both, spec,
+        lambda g: level(z, 1, range(2 * g, 2 * g + 2), xs, sums, stack),
+    )
+    for j in range(count):
+        message[j] = halves(spec[j])
+    message[count, 0 : z.edge_rows, :] = edges[...].astype(BF)
+    message[count, z.edge_rows :, :] = jnp.zeros((z.spec_rows - z.edge_rows, LANES), BF)
+
+
+def home_kernel(z, stack, weight, table, turn, switch, kept, acc, both):
+    kept[:, z.spec_rows - 8 : z.spec_rows, :] = jnp.zeros((z.tm // 2, 8, LANES), F32)
+    parity = jnp.bitwise_and(position("tm"), 1)
+    half_transform(z, parity, table, turn, stack, weight, switch, acc, both, kept, None)
+
+
+def split_transform(z, flags, x):
+    count, height = z.tm // 2, z.lift * (z.tm // 2)
+    first, turn = z.parity_tables()
+    state = [
+        jax.ShapeDtypeStruct((z.stations, z.depth, SPAN), BF),
+        jax.ShapeDtypeStruct((LANES, 2 * SPAN), BF),
+        jax.ShapeDtypeStruct(first.shape[1:], BF),
+        jax.ShapeDtypeStruct(turn.shape[1:], F32),
+        jax.ShapeDtypeStruct((z.stations, TILES, LANES), F32),
+    ]
+    inputs = [flags, x, jnp.asarray(first), jnp.asarray(turn)]
+    work = [
+        pltpu.VMEM((z.stations, height, LANES), F32),
+        pltpu.VMEM((2, height, LANES), F32),
+    ]
+    message, *state = pl.pallas_call(
+        functools.partial(away_kernel, z),
+        in_specs=[HBM_SPEC] * 4,
+        out_specs=[VMEM_SPEC] * 6,
+        out_shape=[jax.ShapeDtypeStruct((count + 1, z.spec_rows, LANES), BF)] + state,
+        scratch_shapes=[
+            pltpu.SMEM((z.stations,), jnp.int32),
+            pltpu.VMEM(x.shape, BF),
+            pltpu.VMEM(first.shape, F32),
+            pltpu.VMEM(turn.shape[1:], F32),
+            pltpu.VMEM(first.shape[1:], BF),
+            pltpu.VMEM((z.stations, 8 + z.pad, SPAN), F32),
+            pltpu.VMEM((z.stations, TILES, 16 + up_to(z.rows, 8), 3 * LANES), F32),
+            pltpu.VMEM((z.edge_rows, LANES), F32),
+            *work,
+            pltpu.VMEM((count, z.spec_rows, LANES), F32),
+            pltpu.SemaphoreType.DMA((5,)),
+        ],
+        compiler_params=params(),
+        name="away",
+    )(*(in_hbm(value) for value in inputs))
+
+    def home():
+        return pl.pallas_call(
+            functools.partial(home_kernel, z),
+            in_specs=[VMEM_SPEC] * 5,
+            out_specs=VMEM_SPEC,
+            out_shape=jax.ShapeDtypeStruct((count, z.spec_rows, LANES), F32),
+            scratch_shapes=work,
+            compiler_params=params(),
+            cost_estimate=pl.CostEstimate(flops=10**9, bytes_accessed=10**6, transcendentals=0),
+            name="home",
+        )(*state)
+
+    return message, home
+
+
+def in_hbm(value):
+    return pltpu.with_memory_space_constraint(value, pltpu.HBM)
+
+
+def merge_kernel(z, bit, kept, came, went, message, left):
+    slots = kept.shape[0]
+    ends = came.shape[0] - slots
+    side = jnp.bitwise_and(position("tm") >> bit, 1)
+    for i in range(slots // 2):
+        pair = []
+        for j in (2 * i, 2 * i + 1):
+            piece = came[j].astype(F32)
+            pair.append(kept[j] + (piece + pltpu.roll(piece, LANES // 2, 1)))
+        left[i] = jnp.where(side == 1, pair[1], pair[0])
+        message[i] = halves(jnp.where(side == 1, pair[0], pair[1]))
+    for s in range(ends):
+        message[slots // 2 + s] = went[slots + s]
+        message[slots // 2 + ends + s] = came[slots + s]
+
+
+def merge(z, bit, kept, came, went):
+    slots = kept.shape[0]
+    ends = came.shape[0] - slots
+    return pl.pallas_call(
+        functools.partial(merge_kernel, z, bit),
+        in_specs=[VMEM_SPEC] * 3,
+        out_specs=[VMEM_SPEC] * 2,
+        out_shape=[
+            jax.ShapeDtypeStruct((slots // 2 + 2 * ends, z.spec_rows, LANES), BF),
+            jax.ShapeDtypeStruct((slots // 2, z.spec_rows, LANES), F32),
+        ],
+        compiler_params=params(),
+        name="merge",
+    )(kept, came, went)
+
+
 def cross_kernel(z, offsets, pairs, stacks, *refs):
     pieces, out = refs[:-1], refs[-1]
     here = position("sta")
@@ -577,14 +831,29 @@
     stations, length = traces.shape
     z = Sizes(stations, length, tm_count, stacks.shape[-1])
     assert sta_count & (sta_count - 1) == 0
-    sent = transform(z, station_flags, traces)
-    got = lax.all_to_all(sent, "tm", split_axis=0, concat_axis=0, tiled=True)
     offsets = [0]
     bits = [1 << k for k in reversed(range(sta_count.bit_length() - 1))]
     for bit in bits:
         offsets += [offset ^ bit for offset in offsets]
-    *made, pairs = tables(z, offsets, band_block, station_flags, tile_mask)
-    pieces = [spectrum(z, got, made)]
+    if tm_count in (4, 8, 16):
+        message, home = split_transform(z, station_flags, traces)
+        for k in range(tm_count.bit_length() - 1):
+            swap = [(i, i ^ (1 << k)) for i in range(tm_count)]
+            came, went = lax.ppermute(message, "tm", swap), message
+            if k == 0:
+                kept = home()
+            if 2 << k < tm_count:
+                message, kept = merge(z, k + 1, kept, came, went)
+        *made, pairs = tables(z, offsets, z.lift, 1, band_block, station_flags, tile_mask)
+        white = gathered(z, kept, came, went, made)
+    else:
+        sent = transform(z, station_flags, traces)
+        got = lax.all_to_all(sent, "tm", split_axis=0, concat_axis=0, tiled=True)
+        *made, pairs = tables(
+            z, offsets, z.half, tm_count, band_block, station_flags, tile_mask
+        )
+        white = spectrum(z, got, made)
+    pieces = [white]
     for bit in bits:
         swap = [(i, i ^ bit) for i in range(sta_count)]
         pieces += [lax.ppermute(piece, "sta", swap) for piece in pieces]

time: 25.2 us -> 23.8 us (0.944)
  waiting for transfers between devices: 9.03 us -> 6.46 us
  starting transfers between devices: 9.01 us -> 10.2 us
    ppermute x0 -> x3, starting transfers between devices: none -> 8.3 us  [shards(): came, went = (lax.ppermute(message, 'tm', swap), message)]
    all_to_all x1 -> x0, starting transfers between devices: 7.45 us -> none  [shards(): got = lax.all_to_all(sent, 'tm', split_axis=0, concat_axis=0, tiled=True)]
    all_to_all x1 -> x0, waiting for transfers between devices: 5.72 us -> none  [shards(): got = lax.all_to_all(sent, 'tm', split_axis=0, concat_axis=0, tiled=True)]
    ppermute x0 -> x3, waiting for transfers between devices: none -> 3.48 us  [shards(): came, went = (lax.ppermute(message, 'tm', swap), message)]
    ppermute x3, starting transfers between devices: 1.56 us -> 1.89 us  [shards(): pieces += [lax.ppermute(piece, 'sta', swap) for piece in pieces]]
    ppermute x3, waiting for transfers between devices: 3.3 us -> 2.97 us  [shards(): pieces += [lax.ppermute(piece, 'sta', swap) for piece in pieces]]
    pallas_call x3 -> x6, Pallas kernels: 5.46 us -> 5.65 us  [the longest x1 2.59 us: split_transform(): pl.pallas_call(functools.partial(away_kernel, z), in_specs=[HBM_SPEC] * 4...]
  transfers between devices with their start and end apart: 4 -> 6, of which waited for: 3 -> 5; matrix products, arithmetic and copies ran while one was open for 0% -> 0% of each run, Pallas kernels for 4% -> 8%
where the time goes in v4:
time: 23.8 us; the launch traced here: 23.7 us
  starting transfers between devices  10.2 us (43%)
  waiting for transfers between devices  6.46 us (27%)
  Pallas kernels  6.32 us (27%)
  between operations  0.72 us (3%)
    ppermute x3, starting transfers between devices, shards(): came, went = (lax.ppermute(message, 'tm', swap), message)  8.3 us
    ppermute x3, waiting for transfers between devices, shards(): came, went = (lax.ppermute(message, 'tm', swap), message)  3.48 us
    ppermute x3, waiting for transfers between devices, shards(): pieces += [lax.ppermute(piece, 'sta', swap) for piece in pieces]  2.97 us
    pallas_call x1, Pallas kernels, split_transform(): pl.pallas_call(functools.partial(away_kernel, z), in_specs=[HBM_SPEC] * 4...  2.59 us
    ppermute x3, starting transfers between devices, shards(): pieces += [lax.ppermute(piece, 'sta', swap) for piece in pieces]  1.89 us
    pallas_call x1, Pallas kernels, tables(): pl.pallas_call(functools.partial(table_kernel, z, offsets, split), in_spe...  1.04 us
    pallas_call x1, Pallas kernels, home(): pl.pallas_call(functools.partial(home_kernel, z), in_specs=[VMEM_SPEC] *...  0.95 us
    pallas_call x1, Pallas kernels, gathered(): pl.pallas_call(functools.partial(gathered_kernel, z), in_specs=[VMEM_SPEC...  0.91 us
  transfers between devices with their start and end apart: 6, of which 5 were waited for; matrix products, arithmetic and copies ran while one was open for 0% of the time, Pallas kernels for 8%

profile of v4, /device:TPU:0, one launch (start us, length us, event | category | flops | bytes accessed | tf_op | source)
XLA Modules:
  0.0 23.7 jit_solution(7018130042098831276)
XLA Ops:
  0.0 2.6 %away.1 = (bf16[5,40,128]{2,1,0:T(8,128)(2,1)S(1)}, bf16[2,112,1024]{2,1,0:T(8,128)(2,1)S(1)}, bf16[128,2048]{1,0:T(8,128)(2,1)S(1)}, bf16[144,128]{1,0:T(8,128)...) custom-call(s32[2]{0:T(128)} %flags.3, bf16[2,33792]{1,0:T(2,128)(2,1)} %x.1, ...), custom_call_target="tpu_custom_call" | custom-call | tf_op jit(solution)/shard_map/away/pallas_call | solution.py:726
  2.6 3.1 %collective-permute-start = (bf16[5,40,128]{2,1,0:T(8,128)(2,1)S(1)}, bf16[5,40,128]{2,1,0:T(8,128)(2,1)S(1)}, u32[]{:S(2)}, u32[]{:S(2)}) collective-permute-start(bf16[5,40,128]{2,1,0:T(8,128)(2,1)S(1)} %get-tuple-element.29.went), channel_id=1, source_target_pairs={{0,4},{4,0},{8,12},{12,8},{16,20},{20,16},{24,28},{28,24},{1,5},{5... | collective-permute-start | bytes 153608 | tf_op jit(solution)/shard_map/ppermute | solution.py:842
  5.7 0.0 copy-start.1
  5.7 0.0 copy-start.2
  5.7 0.9 %home.1.kept = f32[4,40,128]{2,1,0:T(8,128)S(1)} custom-call(bf16[2,112,1024]{2,1,0:T(8,128)(2,1)S(1)} %get-tuple-element.24.stack, bf16[128,2048]{1,0:T(8,128)(2,1)S(1)} %get-tuple-element.25.weight, bf16[144,128]{1,0:T(8,128)(2,1)S(1)} %get-tuple-element.26.table, f32[4,2,72,256]{3,2,1,0:T(8,128)S(1)} %get-tuple-element.27.turn, ...), custom_call_target="tpu_custom_call" | custom-call | flops 1000000000 | bytes 1000000 | tf_op jit(solution)/shard_map/home/pallas_call | solution.py:749
  6.6 0.0 copy-start
  6.6 1.1 %collective-permute-done.came = bf16[5,40,128]{2,1,0:T(8,128)(2,1)S(1)} collective-permute-done((bf16[5,40,128]{2,1,0:T(8,128)(2,1)S(1)}, bf16[5,40,128]{2,1,0:T(8,128)(2,1)S(1)}, u32[]{:S(2)}, u32[]{:S(2)}) %collective-permute-start) | collective-permute-done | bytes 51232 | tf_op jit(solution)/shard_map/ppermute | solution.py:842
  7.7 0.1 merge.2
  7.8 2.1 %collective-permute-start.1 = (bf16[4,40,128]{2,1,0:T(8,128)(2,1)S(1)}, bf16[4,40,128]{2,1,0:T(8,128)(2,1)S(1)}, u32[]{:S(2)}, u32[]{:S(2)}) collective-permute-start(bf16[4,40,128]{2,1,0:T(8,128)(2,1)S(1)} %get-tuple-element.31.went), channel_id=1, source_target_pairs={{0,8},{4,12},{8,0},{12,4},{16,24},{20,28},{24,16},{28,20},{1,9},{5... | collective-permute-start | bytes 122888 | tf_op jit(solution)/shard_map/ppermute | solution.py:842
  10.0 2.0 %collective-permute-done.1.came = bf16[4,40,128]{2,1,0:T(8,128)(2,1)S(1)} collective-permute-done((bf16[4,40,128]{2,1,0:T(8,128)(2,1)S(1)}, bf16[4,40,128]{2,1,0:T(8,128)(2,1)S(1)}, u32[]{:S(2)}, u32[]{:S(2)}) %collective-permute-start.1) | collective-permute-done | bytes 40992 | tf_op jit(solution)/shard_map/ppermute | solution.py:842
  12.0 0.1 merge.3
  12.1 3.1 %collective-permute-start.2 = (bf16[5,40,128]{2,1,0:T(8,128)(2,1)S(1)}, bf16[5,40,128]{2,1,0:T(8,128)(2,1)S(1)}, u32[]{:S(2)}, u32[]{:S(2)}) collective-permute-start(bf16[5,40,128]{2,1,0:T(8,128)(2,1)S(1)} %get-tuple-element.33.went), channel_id=1, source_target_pairs={{0,16},{4,20},{8,24},{12,28},{16,0},{20,4},{24,8},{28,12},{1,17},{... | collective-permute-start | bytes 153608 | tf_op jit(solution)/shard_map/ppermute | solution.py:842
  15.8 0.0 copy-done.1
  15.8 0.0 copy-done.2
  15.8 1.0 %tables.1 = (bf16[1,40,384]{2,1,0:T(8,128)(2,1)S(1)}, f32[16,384]{1,0:T(8,128)S(1)}, bf16[64,768]{1,0:T(8,128)(2,1)S(1)}, f32[2,128,384]{2,1,0:T(8,128)S(1)}, bf...) custom-call(s32[1,1]{1,0:T(1,128)} %bitcast.1.band, ...), custom_call_target="tpu_custom_call" | custom-call | flops 4000000 | bytes 2000000 | tf_op jit(solution)/shard_map/tables/pallas_call | solution.py:433
  16.9 0.4 %collective-permute-done.2.came = bf16[5,40,128]{2,1,0:T(8,128)(2,1)S(1)} collective-permute-done((bf16[5,40,128]{2,1,0:T(8,128)(2,1)S(1)}, bf16[5,40,128]{2,1,0:T(8,128)(2,1)S(1)}, u32[]{:S(2)}, u32[]{:S(2)}) %collective-permute-start.2) | collective-permute-done | bytes 51232 | tf_op jit(solution)/shard_map/ppermute | solution.py:842
  17.3 0.9 %spectrum.1.refs_0_ = f32[4,384]{1,0:T(4,128)S(1)} custom-call(f32[1,40,128]{2,1,0:T(8,128)S(1)} %get-tuple-element.32.kept, bf16[5,40,128]{2,1,0:T(8,128)(2,1)S(1)} %collective-permute-done.2.came, bf16[5,40,128]{2,1,0:T(8,128)(2,1)S(1)} %get-tuple-element.33.went, bf16[1,40,384]{2,1,0:T(8,128)(2,1)S(1)} %get-tuple-element.34.choose, ...), custom_call_target="tpu_custom_call" | custom-call | tf_op jit(solution)/shard_map/spectrum/pallas_call | solution.py:587
  18.2 1.9 %collective-permute-start.3 = (f32[4,384]{1,0:T(4,128)S(1)}, f32[4,384]{1,0:T(4,128)S(1)}, u32[]{:S(2)}, u32[]{:S(2)}) collective-permute-start(f32[4,384]{1,0:T(4,128)S(1)} %spectrum.1.refs_0_), channel_id=1, source_target_pairs={{0,2},{1,3},{2,0},{3,1},{4,6},{5,7},{6,4},{7,5},{8,10},{9,11},{10,... | collective-permute-start | bytes 18440 | tf_op jit(solution)/shard_map/ppermute | solution.py:859
  20.0 0.0 collective-permute-start.4
  20.1 1.8 %collective-permute-done.3.refs_1_ = f32[4,384]{1,0:T(4,128)S(1)} collective-permute-done((f32[4,384]{1,0:T(4,128)S(1)}, f32[4,384]{1,0:T(4,128)S(1)}, u32[]{:S(2)}, u32[]{:S(2)}) %collective-permute-start.3) | collective-permute-done | bytes 6176 | tf_op jit(solution)/shard_map/ppermute | solution.py:859
  21.9 0.0 collective-permute-start.5
  21.9 0.0 collective-permute-done.4.refs_2_
  21.9 1.2 %collective-permute-done.5.refs_3_ = f32[4,384]{1,0:T(4,128)S(1)} collective-permute-done((f32[4,384]{1,0:T(4,128)S(1)}, f32[4,384]{1,0:T(4,128)S(1)}, u32[]{:S(2)}, u32[]{:S(2)}) %collective-permute-start.5) | collective-permute-done | bytes 6176 | tf_op jit(solution)/shard_map/ppermute | solution.py:859
  23.0 0.0 copy-done
  23.0 0.7 %cross.1 = f32[2,8,2,384]{3,2,1,0:T(2,128)} custom-call(f32[4,2,128]{2,1,0:T(2,128)S(1)} %get-tuple-element.23.pairs, f32[2,8,2,384]{3,2,1,0:T(2,128)S(1)} %copy-done, f32[4,384]{1,0:T(4,128)S(1)} %spectrum.1.refs_0_, f32[4,384]{1,0:T(4,128)S(1)} %collective-permute-done.3.refs_1_, f32[4,384]{1,0:T(4,128)S(1)} %collective-permute-done.4.refs_2_, ...), custom_call_target="tpu_custom_call" | custom-call | tf_op jit(solution)/shard_map/cross/pallas_call | solution.py:819
Async XLA Ops:
  2.6 5.1 %collective-permute-start = (bf16[5,40,128]{2,1,0:T(8,128)(2,1)S(1)}, bf16[5,40,128]{2,1,0:T(8,128)(2,1)S(1)}, u32[]{:S(2)}, u32[]{:S(2)}) collective-permute-start(bf16[5,40,128]{2,1,0:T(8,128)(2,1)S(1)} %get-tuple-element.29.went), channel_id=1, source_target_pairs={{0,4},{4,0},{8,12},{12,8},{16,20},{20,16},{24,28},{28,24},{1,5},{5... | collective-permute-start | bytes 153608 | tf_op jit(solution)/shard_map/ppermute | solution.py:842
  5.7 10.2 %copy-start.1 = (s32[2]{0:T(128)S(1)}, s32[2]{0:T(128)}, u32[]{:S(2)}) copy-start(s32[2]{0:T(128)} %flags.3) | copy-start | bytes 28
  5.7 10.2 %copy-start.2 = (s32[4,4]{1,0:T(4,128)S(1)}, s32[4,4]{1,0:T(4,128)}, u32[]{:S(2)}) copy-start(s32[4,4]{1,0:T(4,128)} %mask.1) | copy-start | bytes 196
  6.6 16.4 %copy-start = (f32[2,8,2,384]{3,2,1,0:T(2,128)S(1)}, f32[2,8,2,384]{3,2,1,0:T(2,128)}, u32[]{:S(2)}) copy-start(f32[2,8,2,384]{3,2,1,0:T(2,128)} %stacks.1) | copy-start | bytes 147460
  7.8 4.1 %collective-permute-start.1 = (bf16[4,40,128]{2,1,0:T(8,128)(2,1)S(1)}, bf16[4,40,128]{2,1,0:T(8,128)(2,1)S(1)}, u32[]{:S(2)}, u32[]{:S(2)}) collective-permute-start(bf16[4,40,128]{2,1,0:T(8,128)(2,1)S(1)} %get-tuple-element.31.went), channel_id=1, source_target_pairs={{0,8},{4,12},{8,0},{12,4},{16,24},{20,28},{24,16},{28,20},{1,9},{5... | collective-permute-start | bytes 122888 | tf_op jit(solution)/shard_map/ppermute | solution.py:842
  12.1 5.2 %collective-permute-start.2 = (bf16[5,40,128]{2,1,0:T(8,128)(2,1)S(1)}, bf16[5,40,128]{2,1,0:T(8,128)(2,1)S(1)}, u32[]{:S(2)}, u32[]{:S(2)}) collective-permute-start(bf16[5,40,128]{2,1,0:T(8,128)(2,1)S(1)} %get-tuple-element.33.went), channel_id=1, source_target_pairs={{0,16},{4,20},{8,24},{12,28},{16,0},{20,4},{24,8},{28,12},{1,17},{... | collective-permute-start | bytes 153608 | tf_op jit(solution)/shard_map/ppermute | solution.py:842
  18.2 3.7 %collective-permute-start.3 = (f32[4,384]{1,0:T(4,128)S(1)}, f32[4,384]{1,0:T(4,128)S(1)}, u32[]{:S(2)}, u32[]{:S(2)}) collective-permute-start(f32[4,384]{1,0:T(4,128)S(1)} %spectrum.1.refs_0_), channel_id=1, source_target_pairs={{0,2},{1,3},{2,0},{3,1},{4,6},{5,7},{6,4},{7,5},{8,10},{9,11},{10,... | collective-permute-start | bytes 18440 | tf_op jit(solution)/shard_map/ppermute | solution.py:859
  20.0 1.8 %collective-permute-start.4 = (f32[4,384]{1,0:T(4,128)S(1)}, f32[4,384]{1,0:T(4,128)S(1)}, u32[]{:S(2)}, u32[]{:S(2)}) collective-permute-start(f32[4,384]{1,0:T(4,128)S(1)} %spectrum.1.refs_0_), channel_id=1, source_target_pairs={{0,1},{1,0},{2,3},{3,2},{4,5},{5,4},{6,7},{7,6},{8,9},{9,8},{10,11... | collective-permute-start | bytes 18440 | tf_op jit(solution)/shard_map/ppermute | solution.py:859
  21.9 1.2 %collective-permute-start.5 = (f32[4,384]{1,0:T(4,128)S(1)}, f32[4,384]{1,0:T(4,128)S(1)}, u32[]{:S(2)}, u32[]{:S(2)}) collective-permute-start(f32[4,384]{1,0:T(4,128)S(1)} %collective-permute-done.3.refs_1_), channel_id=1, source_target_pairs={{0,1},{1,0},{2,3},{3,2},{4,5},{5,4},{6,7},{7,6},{8,9},{9,8},{10,11... | collective-permute-start | bytes 18440 | tf_op jit(solution)/shard_map/ppermute | solution.py:859

commit v5 on v4

--- a/solution.py
+++ b/solution.py
@@ -645,21 +645,37 @@
         spec[lax.rem(2 * count - parity - j, count), lift : 2 * lift, :] = both[1, lines, :]
 
 
+def stretch_table(z, parity, first, table):
+    count, height = z.tm // 2, z.lift * (z.tm // 2)
+    low = z.low_lanes(iota((height, LANES), 1))
+    residue = 2 * iota((count, LANES), 0) + parity
+    sine, cosine = sincos(turns_of((position("tm") * residue).astype(F32), z.tm))
+    f_re = first[:height].reshape(z.lift, count, LANES)
+    f_im = first[height:].reshape(z.lift, count, LANES)
+    for k, value in enumerate(
+        (f_re * cosine[None] + f_im * sine[None], f_im * cosine[None] - f_re * sine[None])
+    ):
+        value = value.reshape(height, LANES)
+        high = value.astype(BF).astype(F32)
+        table[k * height : (k + 1) * height, :] = jnp.where(low, value - high, high).astype(BF)
+
+
 def away_kernel(
-    z, flags, x, first, turn, message, stack, weight, home_table, home_turn, switch,
+    z, flags, x, first, turn, message, stack, weight, home_first, home_turn, switch,
     flags_s, x_v, first_v, turn_v, table, xs, sums, edges, acc, both, spec, sems,
 ):
     rows, pad, top = z.rows, z.pad, 8
-    count, height = z.tm // 2, z.lift * (z.tm // 2)
+    count = z.tm // 2
     here = position("tm")
     home = jnp.bitwise_and(here, 1)
     away = 1 - home
     copies = [
         pltpu.make_async_copy(x, x_v, sems.at[0]),
         pltpu.make_async_copy(flags, flags_s, sems.at[1]),
-        pltpu.make_async_copy(first, first_v, sems.at[2]),
+        pltpu.make_async_copy(first.at[away], first_v, sems.at[2]),
         pltpu.make_async_copy(turn.at[away], turn_v, sems.at[3]),
         pltpu.make_async_copy(turn.at[home], home_turn, sems.at[4]),
+        pltpu.make_async_copy(first.at[home], home_first, sems.at[5]),
     ]
     for copy in copies:
         copy.start()
@@ -678,33 +694,25 @@
         window(z, s, xs, sums)
         switch[s] = jnp.full((TILES, LANES), flags_s[s].astype(F32))
     level(z, 0, range(TILES), xs, sums, stack)
-    for copy in copies[2:]:
-        copy.wait()
-    low = z.low_lanes(iota((height, LANES), 1))
-    for parity, to in ((away, table), (home, home_table)):
-        residue = 2 * iota((count, LANES), 0) + parity
-        sine, cosine = sincos(turns_of((here * residue).astype(F32), z.tm))
-        f_re = first_v[parity, :height].reshape(z.lift, count, LANES)
-        f_im = first_v[parity, height:].reshape(z.lift, count, LANES)
-        for k, value in enumerate(
-            (f_re * cosine[None] + f_im * sine[None], f_im * cosine[None] - f_re * sine[None])
-        ):
-            value = value.reshape(height, LANES)
-            high = value.astype(BF).astype(F32)
-            to[k * height : (k + 1) * height, :] = jnp.where(low, value - high, high).astype(BF)
+    copies[2].wait()
+    copies[3].wait()
+    stretch_table(z, away, first_v, table)
     half_transform(
         z, away, table, turn_v, stack, weight, switch, acc, both, spec,
         lambda g: level(z, 1, range(2 * g, 2 * g + 2), xs, sums, stack),
     )
+    copies[4].wait()
+    copies[5].wait()
     for j in range(count):
         message[j] = halves(spec[j])
     message[count, 0 : z.edge_rows, :] = edges[...].astype(BF)
     message[count, z.edge_rows :, :] = jnp.zeros((z.spec_rows - z.edge_rows, LANES), BF)
 
 
-def home_kernel(z, stack, weight, table, turn, switch, kept, acc, both):
+def home_kernel(z, stack, weight, first, turn, switch, kept, table, acc, both):
     kept[:, z.spec_rows - 8 : z.spec_rows, :] = jnp.zeros((z.tm // 2, 8, LANES), F32)
     parity = jnp.bitwise_and(position("tm"), 1)
+    stretch_table(z, parity, first, table)
     half_transform(z, parity, table, turn, stack, weight, switch, acc, both, kept, None)
 
 
@@ -714,7 +722,7 @@
     state = [
         jax.ShapeDtypeStruct((z.stations, z.depth, SPAN), BF),
         jax.ShapeDtypeStruct((LANES, 2 * SPAN), BF),
-        jax.ShapeDtypeStruct(first.shape[1:], BF),
+        jax.ShapeDtypeStruct(first.shape[1:], F32),
         jax.ShapeDtypeStruct(turn.shape[1:], F32),
         jax.ShapeDtypeStruct((z.stations, TILES, LANES), F32),
     ]
@@ -731,7 +739,7 @@
         scratch_shapes=[
             pltpu.SMEM((z.stations,), jnp.int32),
             pltpu.VMEM(x.shape, BF),
-            pltpu.VMEM(first.shape, F32),
+            pltpu.VMEM(first.shape[1:], F32),
             pltpu.VMEM(turn.shape[1:], F32),
             pltpu.VMEM(first.shape[1:], BF),
             pltpu.VMEM((z.stations, 8 + z.pad, SPAN), F32),
@@ -739,7 +747,7 @@
             pltpu.VMEM((z.edge_rows, LANES), F32),
             *work,
             pltpu.VMEM((count, z.spec_rows, LANES), F32),
-            pltpu.SemaphoreType.DMA((5,)),
+            pltpu.SemaphoreType.DMA((6,)),
         ],
         compiler_params=params(),
         name="away",
@@ -751,7 +759,7 @@
             in_specs=[VMEM_SPEC] * 5,
             out_specs=VMEM_SPEC,
             out_shape=jax.ShapeDtypeStruct((count, z.spec_rows, LANES), F32),
-            scratch_shapes=work,
+            scratch_shapes=[pltpu.VMEM(first.shape[1:], BF), *work],
             compiler_params=params(),
             cost_estimate=pl.CostEstimate(flops=10**9, bytes_accessed=10**6, transcendentals=0),
             name="home",

time: 23.8 us -> 23.7 us (level)
  transfers between devices with their start and end apart: 6 -> 6, of which waited for: 5 -> 5; matrix products, arithmetic and copies ran while one was open for 0% -> 0% of each run, Pallas kernels for 8% -> 9%
where the time goes in v5:
time: 23.7 us; the launch traced here: 23.6 us
  starting transfers between devices  10.2 us (43%)
  waiting for transfers between devices  6.41 us (27%)
  Pallas kernels  6.21 us (26%)
  between operations  0.72 us (3%)
    ppermute x3, starting transfers between devices, shards(): came, went = (lax.ppermute(message, 'tm', swap), message)  8.3 us
    ppermute x3, waiting for transfers between devices, shards(): came, went = (lax.ppermute(message, 'tm', swap), message)  3.44 us
    ppermute x3, waiting for transfers between devices, shards(): pieces += [lax.ppermute(piece, 'sta', swap) for piece in pieces]  2.97 us
    pallas_call x1, Pallas kernels, split_transform(): pl.pallas_call(functools.partial(away_kernel, z), in_specs=[HBM_SPEC] * 4...  2.44 us
    ppermute x3, starting transfers between devices, shards(): pieces += [lax.ppermute(piece, 'sta', swap) for piece in pieces]  1.89 us
    pallas_call x1, Pallas kernels, tables(): pl.pallas_call(functools.partial(table_kernel, z, offsets, split), in_spe...  1.04 us
    pallas_call x1, Pallas kernels, home(): pl.pallas_call(functools.partial(home_kernel, z), in_specs=[VMEM_SPEC] *...  0.99 us
    pallas_call x1, Pallas kernels, gathered(): pl.pallas_call(functools.partial(gathered_kernel, z), in_specs=[VMEM_SPEC...  0.91 us
  transfers between devices with their start and end apart: 6, of which 5 were waited for; matrix products, arithmetic and copies ran while one was open for 0% of the time, Pallas kernels for 9%

profile of v5, /device:TPU:0, one launch (start us, length us, event | category | flops | bytes accessed | tf_op | source)
XLA Modules:
  0.0 23.6 jit_solution(17057457641758649025)
XLA Ops:
  0.0 2.4 %away.1 = (bf16[5,40,128]{2,1,0:T(8,128)(2,1)S(1)}, bf16[2,112,1024]{2,1,0:T(8,128)(2,1)S(1)}, bf16[128,2048]{1,0:T(8,128)(2,1)S(1)}, f32[144,128]{1,0:T(8,128)S...) custom-call(s32[2]{0:T(128)} %flags.3, bf16[2,33792]{1,0:T(2,128)(2,1)} %x.1, ...), custom_call_target="tpu_custom_call" | custom-call | tf_op jit(solution)/shard_map/away/pallas_call | solution.py:734
  2.4 3.1 %collective-permute-start = (bf16[5,40,128]{2,1,0:T(8,128)(2,1)S(1)}, bf16[5,40,128]{2,1,0:T(8,128)(2,1)S(1)}, u32[]{:S(2)}, u32[]{:S(2)}) collective-permute-start(bf16[5,40,128]{2,1,0:T(8,128)(2,1)S(1)} %get-tuple-element.29.went), channel_id=1, source_target_pairs={{0,4},{4,0},{8,12},{12,8},{16,20},{20,16},{24,28},{28,24},{1,5},{5... | collective-permute-start | bytes 153608 | tf_op jit(solution)/shard_map/ppermute | solution.py:850
  5.5 0.0 copy-start.1
  5.5 0.0 copy-start.2
  5.5 1.0 %home.1.kept = f32[4,40,128]{2,1,0:T(8,128)S(1)} custom-call(bf16[2,112,1024]{2,1,0:T(8,128)(2,1)S(1)} %get-tuple-element.24.stack, bf16[128,2048]{1,0:T(8,128)(2,1)S(1)} %get-tuple-element.25.weight, f32[144,128]{1,0:T(8,128)S(1)} %get-tuple-element.26.first, f32[4,2,72,256]{3,2,1,0:T(8,128)S(1)} %get-tuple-element.27.turn, ...), custom_call_target="tpu_custom_call" | custom-call | flops 1000000000 | bytes 1000000 | tf_op jit(solution)/shard_map/home/pallas_call | solution.py:757
  6.5 0.0 copy-start
  6.5 1.1 %collective-permute-done.came = bf16[5,40,128]{2,1,0:T(8,128)(2,1)S(1)} collective-permute-done((bf16[5,40,128]{2,1,0:T(8,128)(2,1)S(1)}, bf16[5,40,128]{2,1,0:T(8,128)(2,1)S(1)}, u32[]{:S(2)}, u32[]{:S(2)}) %collective-permute-start) | collective-permute-done | bytes 51232 | tf_op jit(solution)/shard_map/ppermute | solution.py:850
  7.6 0.1 merge.2
  7.7 2.1 %collective-permute-start.1 = (bf16[4,40,128]{2,1,0:T(8,128)(2,1)S(1)}, bf16[4,40,128]{2,1,0:T(8,128)(2,1)S(1)}, u32[]{:S(2)}, u32[]{:S(2)}) collective-permute-start(bf16[4,40,128]{2,1,0:T(8,128)(2,1)S(1)} %get-tuple-element.31.went), channel_id=1, source_target_pairs={{0,8},{4,12},{8,0},{12,4},{16,24},{20,28},{24,16},{28,20},{1,9},{5... | collective-permute-start | bytes 122888 | tf_op jit(solution)/shard_map/ppermute | solution.py:850
  9.8 2.0 %collective-permute-done.1.came = bf16[4,40,128]{2,1,0:T(8,128)(2,1)S(1)} collective-permute-done((bf16[4,40,128]{2,1,0:T(8,128)(2,1)S(1)}, bf16[4,40,128]{2,1,0:T(8,128)(2,1)S(1)}, u32[]{:S(2)}, u32[]{:S(2)}) %collective-permute-start.1) | collective-permute-done | bytes 40992 | tf_op jit(solution)/shard_map/ppermute | solution.py:850
  11.8 0.1 merge.3
  11.9 3.1 %collective-permute-start.2 = (bf16[5,40,128]{2,1,0:T(8,128)(2,1)S(1)}, bf16[5,40,128]{2,1,0:T(8,128)(2,1)S(1)}, u32[]{:S(2)}, u32[]{:S(2)}) collective-permute-start(bf16[5,40,128]{2,1,0:T(8,128)(2,1)S(1)} %get-tuple-element.33.went), channel_id=1, source_target_pairs={{0,16},{4,20},{8,24},{12,28},{16,0},{20,4},{24,8},{28,12},{1,17},{... | collective-permute-start | bytes 153608 | tf_op jit(solution)/shard_map/ppermute | solution.py:850
  15.7 0.0 copy-done.1
  15.7 0.0 copy-done.2
  15.7 1.0 %tables.1 = (bf16[1,40,384]{2,1,0:T(8,128)(2,1)S(1)}, f32[16,384]{1,0:T(8,128)S(1)}, bf16[64,768]{1,0:T(8,128)(2,1)S(1)}, f32[2,128,384]{2,1,0:T(8,128)S(1)}, bf...) custom-call(s32[1,1]{1,0:T(1,128)} %bitcast.1.band, ...), custom_call_target="tpu_custom_call" | custom-call | flops 4000000 | bytes 2000000 | tf_op jit(solution)/shard_map/tables/pallas_call | solution.py:433
  16.7 0.4 %collective-permute-done.2.came = bf16[5,40,128]{2,1,0:T(8,128)(2,1)S(1)} collective-permute-done((bf16[5,40,128]{2,1,0:T(8,128)(2,1)S(1)}, bf16[5,40,128]{2,1,0:T(8,128)(2,1)S(1)}, u32[]{:S(2)}, u32[]{:S(2)}) %collective-permute-start.2) | collective-permute-done | bytes 51232 | tf_op jit(solution)/shard_map/ppermute | solution.py:850
  17.1 0.9 %spectrum.1.refs_0_ = f32[4,384]{1,0:T(4,128)S(1)} custom-call(f32[1,40,128]{2,1,0:T(8,128)S(1)} %get-tuple-element.32.kept, bf16[5,40,128]{2,1,0:T(8,128)(2,1)S(1)} %collective-permute-done.2.came, bf16[5,40,128]{2,1,0:T(8,128)(2,1)S(1)} %get-tuple-element.33.went, bf16[1,40,384]{2,1,0:T(8,128)(2,1)S(1)} %get-tuple-element.34.choose, ...), custom_call_target="tpu_custom_call" | custom-call | tf_op jit(solution)/shard_map/spectrum/pallas_call | solution.py:587
  18.0 1.9 %collective-permute-start.3 = (f32[4,384]{1,0:T(4,128)S(1)}, f32[4,384]{1,0:T(4,128)S(1)}, u32[]{:S(2)}, u32[]{:S(2)}) collective-permute-start(f32[4,384]{1,0:T(4,128)S(1)} %spectrum.1.refs_0_), channel_id=1, source_target_pairs={{0,2},{1,3},{2,0},{3,1},{4,6},{5,7},{6,4},{7,5},{8,10},{9,11},{10,... | collective-permute-start | bytes 18440 | tf_op jit(solution)/shard_map/ppermute | solution.py:867
  19.9 0.0 collective-permute-start.4
  19.9 1.8 %collective-permute-done.3.refs_1_ = f32[4,384]{1,0:T(4,128)S(1)} collective-permute-done((f32[4,384]{1,0:T(4,128)S(1)}, f32[4,384]{1,0:T(4,128)S(1)}, u32[]{:S(2)}, u32[]{:S(2)}) %collective-permute-start.3) | collective-permute-done | bytes 6176 | tf_op jit(solution)/shard_map/ppermute | solution.py:867
  21.7 0.0 collective-permute-start.5
  21.7 0.0 collective-permute-done.4.refs_2_
  21.7 1.2 %collective-permute-done.5.refs_3_ = f32[4,384]{1,0:T(4,128)S(1)} collective-permute-done((f32[4,384]{1,0:T(4,128)S(1)}, f32[4,384]{1,0:T(4,128)S(1)}, u32[]{:S(2)}, u32[]{:S(2)}) %collective-permute-start.5) | collective-permute-done | bytes 6176 | tf_op jit(solution)/shard_map/ppermute | solution.py:867
  22.9 0.0 copy-done
  22.9 0.7 %cross.1 = f32[2,8,2,384]{3,2,1,0:T(2,128)} custom-call(f32[4,2,128]{2,1,0:T(2,128)S(1)} %get-tuple-element.23.pairs, f32[2,8,2,384]{3,2,1,0:T(2,128)S(1)} %copy-done, f32[4,384]{1,0:T(4,128)S(1)} %spectrum.1.refs_0_, f32[4,384]{1,0:T(4,128)S(1)} %collective-permute-done.3.refs_1_, f32[4,384]{1,0:T(4,128)S(1)} %collective-permute-done.4.refs_2_, ...), custom_call_target="tpu_custom_call" | custom-call | tf_op jit(solution)/shard_map/cross/pallas_call | solution.py:827
Async XLA Ops:
  2.4 5.2 %collective-permute-start = (bf16[5,40,128]{2,1,0:T(8,128)(2,1)S(1)}, bf16[5,40,128]{2,1,0:T(8,128)(2,1)S(1)}, u32[]{:S(2)}, u32[]{:S(2)}) collective-permute-start(bf16[5,40,128]{2,1,0:T(8,128)(2,1)S(1)} %get-tuple-element.29.went), channel_id=1, source_target_pairs={{0,4},{4,0},{8,12},{12,8},{16,20},{20,16},{24,28},{28,24},{1,5},{5... | collective-permute-start | bytes 153608 | tf_op jit(solution)/shard_map/ppermute | solution.py:850
  5.5 10.1 %copy-start.1 = (s32[2]{0:T(128)S(1)}, s32[2]{0:T(128)}, u32[]{:S(2)}) copy-start(s32[2]{0:T(128)} %flags.3) | copy-start | bytes 28
  5.5 10.2 %copy-start.2 = (s32[4,4]{1,0:T(4,128)S(1)}, s32[4,4]{1,0:T(4,128)}, u32[]{:S(2)}) copy-start(s32[4,4]{1,0:T(4,128)} %mask.1) | copy-start | bytes 196
  6.5 16.4 %copy-start = (f32[2,8,2,384]{3,2,1,0:T(2,128)S(1)}, f32[2,8,2,384]{3,2,1,0:T(2,128)}, u32[]{:S(2)}) copy-start(f32[2,8,2,384]{3,2,1,0:T(2,128)} %stacks.1) | copy-start | bytes 147460
  7.7 4.1 %collective-permute-start.1 = (bf16[4,40,128]{2,1,0:T(8,128)(2,1)S(1)}, bf16[4,40,128]{2,1,0:T(8,128)(2,1)S(1)}, u32[]{:S(2)}, u32[]{:S(2)}) collective-permute-start(bf16[4,40,128]{2,1,0:T(8,128)(2,1)S(1)} %get-tuple-element.31.went), channel_id=1, source_target_pairs={{0,8},{4,12},{8,0},{12,4},{16,24},{20,28},{24,16},{28,20},{1,9},{5... | collective-permute-start | bytes 122888 | tf_op jit(solution)/shard_map/ppermute | solution.py:850
  11.9 5.2 %collective-permute-start.2 = (bf16[5,40,128]{2,1,0:T(8,128)(2,1)S(1)}, bf16[5,40,128]{2,1,0:T(8,128)(2,1)S(1)}, u32[]{:S(2)}, u32[]{:S(2)}) collective-permute-start(bf16[5,40,128]{2,1,0:T(8,128)(2,1)S(1)} %get-tuple-element.33.went), channel_id=1, source_target_pairs={{0,16},{4,20},{8,24},{12,28},{16,0},{20,4},{24,8},{28,12},{1,17},{... | collective-permute-start | bytes 153608 | tf_op jit(solution)/shard_map/ppermute | solution.py:850
  18.0 3.7 %collective-permute-start.3 = (f32[4,384]{1,0:T(4,128)S(1)}, f32[4,384]{1,0:T(4,128)S(1)}, u32[]{:S(2)}, u32[]{:S(2)}) collective-permute-start(f32[4,384]{1,0:T(4,128)S(1)} %spectrum.1.refs_0_), channel_id=1, source_target_pairs={{0,2},{1,3},{2,0},{3,1},{4,6},{5,7},{6,4},{7,5},{8,10},{9,11},{10,... | collective-permute-start | bytes 18440 | tf_op jit(solution)/shard_map/ppermute | solution.py:867
  19.9 1.8 %collective-permute-start.4 = (f32[4,384]{1,0:T(4,128)S(1)}, f32[4,384]{1,0:T(4,128)S(1)}, u32[]{:S(2)}, u32[]{:S(2)}) collective-permute-start(f32[4,384]{1,0:T(4,128)S(1)} %spectrum.1.refs_0_), channel_id=1, source_target_pairs={{0,1},{1,0},{2,3},{3,2},{4,5},{5,4},{6,7},{7,6},{8,9},{9,8},{10,11... | collective-permute-start | bytes 18440 | tf_op jit(solution)/shard_map/ppermute | solution.py:867
  21.7 1.2 %collective-permute-start.5 = (f32[4,384]{1,0:T(4,128)S(1)}, f32[4,384]{1,0:T(4,128)S(1)}, u32[]{:S(2)}, u32[]{:S(2)}) collective-permute-start(f32[4,384]{1,0:T(4,128)S(1)} %collective-permute-done.3.refs_1_), channel_id=1, source_target_pairs={{0,1},{1,0},{2,3},{3,2},{4,5},{5,4},{6,7},{7,6},{8,9},{9,8},{10,11... | collective-permute-start | bytes 18440 | tf_op jit(solution)/shard_map/ppermute | solution.py:867

commit v6 on v5

--- a/solution.py
+++ b/solution.py
@@ -480,7 +480,7 @@
     z, kept, came, went, choose, keep, steps, turns, near, phase, switch, out, ends
 ):
     tm = z.tm
-    piece = came[0].astype(F32)
+    piece = came[0 : z.spec_rows, :].astype(F32)
     total = kept[0] + (piece + pltpu.roll(piece, LANES // 2, 1))
     placed = lax.dot_general(
         halves(total), choose[0], (((0,), (0,)), ((), ())), preferred_element_type=F32
@@ -488,7 +488,8 @@
     here = position("tm")
     for s in range(tm):
         source, slot = (went, s) if s < tm // 2 else (came, s - tm // 2)
-        ends[here ^ s] = source[1 + slot, 0 : z.edge_rows, :].astype(F32)
+        at = z.spec_rows + slot * z.edge_rows
+        ends[here ^ s] = source[at : at + z.edge_rows, :].astype(F32)
     side_rows = z.stations * TILES
     sides = [ends[:, k * side_rows : (k + 1) * side_rows, :].reshape(-1, LANES) for k in range(2)]
     whiten(z, placed, sides, keep, steps, turns, near, phase, switch, out)
@@ -704,9 +705,8 @@
     copies[4].wait()
     copies[5].wait()
     for j in range(count):
-        message[j] = halves(spec[j])
-    message[count, 0 : z.edge_rows, :] = edges[...].astype(BF)
-    message[count, z.edge_rows :, :] = jnp.zeros((z.spec_rows - z.edge_rows, LANES), BF)
+        message[j * z.spec_rows : (j + 1) * z.spec_rows, :] = halves(spec[j])
+    message[count * z.spec_rows :, :] = edges[...].astype(BF)
 
 
 def home_kernel(z, stack, weight, first, turn, switch, kept, table, acc, both):
@@ -735,7 +735,7 @@
         functools.partial(away_kernel, z),
         in_specs=[HBM_SPEC] * 4,
         out_specs=[VMEM_SPEC] * 6,
-        out_shape=[jax.ShapeDtypeStruct((count + 1, z.spec_rows, LANES), BF)] + state,
+        out_shape=[jax.ShapeDtypeStruct((count * z.spec_rows + z.edge_rows, LANES), BF)] + state,
         scratch_shapes=[
             pltpu.SMEM((z.stations,), jnp.int32),
             pltpu.VMEM(x.shape, BF),
@@ -774,29 +774,30 @@
 
 def merge_kernel(z, bit, kept, came, went, message, left):
     slots = kept.shape[0]
-    ends = came.shape[0] - slots
+    at, to = slots * z.spec_rows, slots // 2 * z.spec_rows
+    ends = came.shape[0] - at
     side = jnp.bitwise_and(position("tm") >> bit, 1)
     for i in range(slots // 2):
         pair = []
         for j in (2 * i, 2 * i + 1):
-            piece = came[j].astype(F32)
+            piece = came[j * z.spec_rows : (j + 1) * z.spec_rows, :].astype(F32)
             pair.append(kept[j] + (piece + pltpu.roll(piece, LANES // 2, 1)))
         left[i] = jnp.where(side == 1, pair[1], pair[0])
-        message[i] = halves(jnp.where(side == 1, pair[0], pair[1]))
-    for s in range(ends):
-        message[slots // 2 + s] = went[slots + s]
-        message[slots // 2 + ends + s] = came[slots + s]
+        lines = slice(i * z.spec_rows, (i + 1) * z.spec_rows)
+        message[lines, :] = halves(jnp.where(side == 1, pair[0], pair[1]))
+    message[to : to + ends, :] = went[at:, :]
+    message[to + ends :, :] = came[at:, :]
 
 
 def merge(z, bit, kept, came, went):
     slots = kept.shape[0]
-    ends = came.shape[0] - slots
+    ends = came.shape[0] - slots * z.spec_rows
     return pl.pallas_call(
         functools.partial(merge_kernel, z, bit),
         in_specs=[VMEM_SPEC] * 3,
         out_specs=[VMEM_SPEC] * 2,
         out_shape=[
-            jax.ShapeDtypeStruct((slots // 2 + 2 * ends, z.spec_rows, LANES), BF),
+            jax.ShapeDtypeStruct((slots // 2 * z.spec_rows + 2 * ends, LANES), BF),
             jax.ShapeDtypeStruct((slots // 2, z.spec_rows, LANES), F32),
         ],
         compiler_params=params(),

time: 23.7 us -> 23.5 us (level)
  no operation moved by 1% of the time
where the time goes in v6:
time: 23.5 us; the launch traced here: 23.4 us
  starting transfers between devices  10.2 us (43%)
  waiting for transfers between devices  6.26 us (27%)
  Pallas kernels  6.2 us (26%)
  between operations  0.72 us (3%)
    ppermute x3, starting transfers between devices, shards(): came, went = (lax.ppermute(message, 'tm', swap), message)  8.3 us
    ppermute x3, waiting for transfers between devices, shards(): came, went = (lax.ppermute(message, 'tm', swap), message)  3.28 us
    ppermute x3, waiting for transfers between devices, shards(): pieces += [lax.ppermute(piece, 'sta', swap) for piece in pieces]  2.97 us
    pallas_call x1, Pallas kernels, split_transform(): pl.pallas_call(functools.partial(away_kernel, z), in_specs=[HBM_SPEC] * 4...  2.42 us
    ppermute x3, starting transfers between devices, shards(): pieces += [lax.ppermute(piece, 'sta', swap) for piece in pieces]  1.89 us
    pallas_call x1, Pallas kernels, tables(): pl.pallas_call(functools.partial(table_kernel, z, offsets, split), in_spe...  1.04 us
    pallas_call x1, Pallas kernels, home(): pl.pallas_call(functools.partial(home_kernel, z), in_specs=[VMEM_SPEC] *...  0.99 us
    pallas_call x1, Pallas kernels, gathered(): pl.pallas_call(functools.partial(gathered_kernel, z), in_specs=[VMEM_SPEC...  0.91 us
  transfers between devices with their start and end apart: 6, of which 5 were waited for; matrix products, arithmetic and copies ran while one was open for 0% of the time, Pallas kernels for 9%

profile of v6, /device:TPU:0, one launch (start us, length us, event | category | flops | bytes accessed | tf_op | source)
XLA Modules:
  0.0 23.4 jit_solution(480617026262940952)
XLA Ops:
  0.0 2.4 %away.1 = (bf16[192,128]{1,0:T(8,128)(2,1)S(1)}, bf16[2,112,1024]{2,1,0:T(8,128)(2,1)S(1)}, bf16[128,2048]{1,0:T(8,128)(2,1)S(1)}, f32[144,128]{1,0:T(8,128)S(1)...) custom-call(s32[2]{0:T(128)} %flags.3, bf16[2,33792]{1,0:T(2,128)(2,1)} %x.1, ...), custom_call_target="tpu_custom_call" | custom-call | tf_op jit(solution)/shard_map/away/pallas_call | solution.py:734
  2.4 3.1 %collective-permute-start = (bf16[192,128]{1,0:T(8,128)(2,1)S(1)}, bf16[192,128]{1,0:T(8,128)(2,1)S(1)}, u32[]{:S(2)}, u32[]{:S(2)}) collective-permute-start(bf16[192,128]{1,0:T(8,128)(2,1)S(1)} %get-tuple-element.29.went), channel_id=1, source_target_pairs={{0,4},{4,0},{8,12},{12,8},{16,20},{20,16},{24,28},{28,24},{1,5},{5... | collective-permute-start | bytes 147464 | tf_op jit(solution)/shard_map/ppermute | solution.py:851
  5.5 0.0 copy-start.1
  5.5 0.0 copy-start.2
  5.5 1.0 %home.1.kept = f32[4,40,128]{2,1,0:T(8,128)S(1)} custom-call(bf16[2,112,1024]{2,1,0:T(8,128)(2,1)S(1)} %get-tuple-element.24.stack, bf16[128,2048]{1,0:T(8,128)(2,1)S(1)} %get-tuple-element.25.weight, f32[144,128]{1,0:T(8,128)S(1)} %get-tuple-element.26.first, f32[4,2,72,256]{3,2,1,0:T(8,128)S(1)} %get-tuple-element.27.turn, ...), custom_call_target="tpu_custom_call" | custom-call | flops 1000000000 | bytes 1000000 | tf_op jit(solution)/shard_map/home/pallas_call | solution.py:757
  6.5 0.0 copy-start
  6.5 1.1 %collective-permute-done.came = bf16[192,128]{1,0:T(8,128)(2,1)S(1)} collective-permute-done((bf16[192,128]{1,0:T(8,128)(2,1)S(1)}, bf16[192,128]{1,0:T(8,128)(2,1)S(1)}, u32[]{:S(2)}, u32[]{:S(2)}) %collective-permute-start) | collective-permute-done | bytes 49184 | tf_op jit(solution)/shard_map/ppermute | solution.py:851
  7.6 0.1 merge.2
  7.7 2.1 %collective-permute-start.1 = (bf16[144,128]{1,0:T(8,128)(2,1)S(1)}, bf16[144,128]{1,0:T(8,128)(2,1)S(1)}, u32[]{:S(2)}, u32[]{:S(2)}) collective-permute-start(bf16[144,128]{1,0:T(8,128)(2,1)S(1)} %get-tuple-element.31.went), channel_id=1, source_target_pairs={{0,8},{4,12},{8,0},{12,4},{16,24},{20,28},{24,16},{28,20},{1,9},{5... | collective-permute-start | bytes 110600 | tf_op jit(solution)/shard_map/ppermute | solution.py:851
  9.8 1.9 %collective-permute-done.1.came = bf16[144,128]{1,0:T(8,128)(2,1)S(1)} collective-permute-done((bf16[144,128]{1,0:T(8,128)(2,1)S(1)}, bf16[144,128]{1,0:T(8,128)(2,1)S(1)}, u32[]{:S(2)}, u32[]{:S(2)}) %collective-permute-start.1) | collective-permute-done | bytes 36896 | tf_op jit(solution)/shard_map/ppermute | solution.py:851
  11.7 0.1 merge.3
  11.8 3.1 %collective-permute-start.2 = (bf16[168,128]{1,0:T(8,128)(2,1)S(1)}, bf16[168,128]{1,0:T(8,128)(2,1)S(1)}, u32[]{:S(2)}, u32[]{:S(2)}) collective-permute-start(bf16[168,128]{1,0:T(8,128)(2,1)S(1)} %get-tuple-element.33.went), channel_id=1, source_target_pairs={{0,16},{4,20},{8,24},{12,28},{16,0},{20,4},{24,8},{28,12},{1,17},{... | collective-permute-start | bytes 129032 | tf_op jit(solution)/shard_map/ppermute | solution.py:851
  15.6 0.0 copy-done.1
  15.6 0.0 copy-done.2
  15.6 1.0 %tables.1 = (bf16[1,40,384]{2,1,0:T(8,128)(2,1)S(1)}, f32[16,384]{1,0:T(8,128)S(1)}, bf16[64,768]{1,0:T(8,128)(2,1)S(1)}, f32[2,128,384]{2,1,0:T(8,128)S(1)}, bf...) custom-call(s32[1,1]{1,0:T(1,128)} %bitcast.1.band, ...), custom_call_target="tpu_custom_call" | custom-call | flops 4000000 | bytes 2000000 | tf_op jit(solution)/shard_map/tables/pallas_call | solution.py:433
  16.6 0.3 %collective-permute-done.2.came = bf16[168,128]{1,0:T(8,128)(2,1)S(1)} collective-permute-done((bf16[168,128]{1,0:T(8,128)(2,1)S(1)}, bf16[168,128]{1,0:T(8,128)(2,1)S(1)}, u32[]{:S(2)}, u32[]{:S(2)}) %collective-permute-start.2) | collective-permute-done | bytes 43040 | tf_op jit(solution)/shard_map/ppermute | solution.py:851
  16.9 0.9 %spectrum.1.refs_0_ = f32[4,384]{1,0:T(4,128)S(1)} custom-call(f32[1,40,128]{2,1,0:T(8,128)S(1)} %get-tuple-element.32.kept, bf16[168,128]{1,0:T(8,128)(2,1)S(1)} %collective-permute-done.2.came, bf16[168,128]{1,0:T(8,128)(2,1)S(1)} %get-tuple-element.33.went, bf16[1,40,384]{2,1,0:T(8,128)(2,1)S(1)} %get-tuple-element.34.choose, ...), custom_call_target="tpu_custom_call" | custom-call | tf_op jit(solution)/shard_map/spectrum/pallas_call | solution.py:588
  17.8 1.9 %collective-permute-start.3 = (f32[4,384]{1,0:T(4,128)S(1)}, f32[4,384]{1,0:T(4,128)S(1)}, u32[]{:S(2)}, u32[]{:S(2)}) collective-permute-start(f32[4,384]{1,0:T(4,128)S(1)} %spectrum.1.refs_0_), channel_id=1, source_target_pairs={{0,2},{1,3},{2,0},{3,1},{4,6},{5,7},{6,4},{7,5},{8,10},{9,11},{10,... | collective-permute-start | bytes 18440 | tf_op jit(solution)/shard_map/ppermute | solution.py:868
  19.7 0.0 collective-permute-start.4
  19.7 1.8 %collective-permute-done.3.refs_1_ = f32[4,384]{1,0:T(4,128)S(1)} collective-permute-done((f32[4,384]{1,0:T(4,128)S(1)}, f32[4,384]{1,0:T(4,128)S(1)}, u32[]{:S(2)}, u32[]{:S(2)}) %collective-permute-start.3) | collective-permute-done | bytes 6176 | tf_op jit(solution)/shard_map/ppermute | solution.py:868
  21.5 0.0 collective-permute-start.5
  21.5 0.0 collective-permute-done.4.refs_2_
  21.5 1.2 %collective-permute-done.5.refs_3_ = f32[4,384]{1,0:T(4,128)S(1)} collective-permute-done((f32[4,384]{1,0:T(4,128)S(1)}, f32[4,384]{1,0:T(4,128)S(1)}, u32[]{:S(2)}, u32[]{:S(2)}) %collective-permute-start.5) | collective-permute-done | bytes 6176 | tf_op jit(solution)/shard_map/ppermute | solution.py:868
  22.7 0.0 copy-done
  22.7 0.7 %cross.1 = f32[2,8,2,384]{3,2,1,0:T(2,128)} custom-call(f32[4,2,128]{2,1,0:T(2,128)S(1)} %get-tuple-element.23.pairs, f32[2,8,2,384]{3,2,1,0:T(2,128)S(1)} %copy-done, f32[4,384]{1,0:T(4,128)S(1)} %spectrum.1.refs_0_, f32[4,384]{1,0:T(4,128)S(1)} %collective-permute-done.3.refs_1_, f32[4,384]{1,0:T(4,128)S(1)} %collective-permute-done.4.refs_2_, ...), custom_call_target="tpu_custom_call" | custom-call | tf_op jit(solution)/shard_map/cross/pallas_call | solution.py:828
Async XLA Ops:
  2.4 5.1 %collective-permute-start = (bf16[192,128]{1,0:T(8,128)(2,1)S(1)}, bf16[192,128]{1,0:T(8,128)(2,1)S(1)}, u32[]{:S(2)}, u32[]{:S(2)}) collective-permute-start(bf16[192,128]{1,0:T(8,128)(2,1)S(1)} %get-tuple-element.29.went), channel_id=1, source_target_pairs={{0,4},{4,0},{8,12},{12,8},{16,20},{20,16},{24,28},{28,24},{1,5},{5... | collective-permute-start | bytes 147464 | tf_op jit(solution)/shard_map/ppermute | solution.py:851
  5.5 10.1 %copy-start.1 = (s32[2]{0:T(128)S(1)}, s32[2]{0:T(128)}, u32[]{:S(2)}) copy-start(s32[2]{0:T(128)} %flags.3) | copy-start | bytes 28
  5.5 10.1 %copy-start.2 = (s32[4,4]{1,0:T(4,128)S(1)}, s32[4,4]{1,0:T(4,128)}, u32[]{:S(2)}) copy-start(s32[4,4]{1,0:T(4,128)} %mask.1) | copy-start | bytes 196
  6.5 16.2 %copy-start = (f32[2,8,2,384]{3,2,1,0:T(2,128)S(1)}, f32[2,8,2,384]{3,2,1,0:T(2,128)}, u32[]{:S(2)}) copy-start(f32[2,8,2,384]{3,2,1,0:T(2,128)} %stacks.1) | copy-start | bytes 147460
  7.7 4.1 %collective-permute-start.1 = (bf16[144,128]{1,0:T(8,128)(2,1)S(1)}, bf16[144,128]{1,0:T(8,128)(2,1)S(1)}, u32[]{:S(2)}, u32[]{:S(2)}) collective-permute-start(bf16[144,128]{1,0:T(8,128)(2,1)S(1)} %get-tuple-element.31.went), channel_id=1, source_target_pairs={{0,8},{4,12},{8,0},{12,4},{16,24},{20,28},{24,16},{28,20},{1,9},{5... | collective-permute-start | bytes 110600 | tf_op jit(solution)/shard_map/ppermute | solution.py:851
  11.8 5.1 %collective-permute-start.2 = (bf16[168,128]{1,0:T(8,128)(2,1)S(1)}, bf16[168,128]{1,0:T(8,128)(2,1)S(1)}, u32[]{:S(2)}, u32[]{:S(2)}) collective-permute-start(bf16[168,128]{1,0:T(8,128)(2,1)S(1)} %get-tuple-element.33.went), channel_id=1, source_target_pairs={{0,16},{4,20},{8,24},{12,28},{16,0},{20,4},{24,8},{28,12},{1,17},{... | collective-permute-start | bytes 129032 | tf_op jit(solution)/shard_map/ppermute | solution.py:851
  17.8 3.7 %collective-permute-start.3 = (f32[4,384]{1,0:T(4,128)S(1)}, f32[4,384]{1,0:T(4,128)S(1)}, u32[]{:S(2)}, u32[]{:S(2)}) collective-permute-start(f32[4,384]{1,0:T(4,128)S(1)} %spectrum.1.refs_0_), channel_id=1, source_target_pairs={{0,2},{1,3},{2,0},{3,1},{4,6},{5,7},{6,4},{7,5},{8,10},{9,11},{10,... | collective-permute-start | bytes 18440 | tf_op jit(solution)/shard_map/ppermute | solution.py:868
  19.7 1.8 %collective-permute-start.4 = (f32[4,384]{1,0:T(4,128)S(1)}, f32[4,384]{1,0:T(4,128)S(1)}, u32[]{:S(2)}, u32[]{:S(2)}) collective-permute-start(f32[4,384]{1,0:T(4,128)S(1)} %spectrum.1.refs_0_), channel_id=1, source_target_pairs={{0,1},{1,0},{2,3},{3,2},{4,5},{5,4},{6,7},{7,6},{8,9},{9,8},{10,11... | collective-permute-start | bytes 18440 | tf_op jit(solution)/shard_map/ppermute | solution.py:868
  21.5 1.2 %collective-permute-start.5 = (f32[4,384]{1,0:T(4,128)S(1)}, f32[4,384]{1,0:T(4,128)S(1)}, u32[]{:S(2)}, u32[]{:S(2)}) collective-permute-start(f32[4,384]{1,0:T(4,128)S(1)} %collective-permute-done.3.refs_1_), channel_id=1, source_target_pairs={{0,1},{1,0},{2,3},{3,2},{4,5},{5,4},{6,7},{7,6},{8,9},{9,8},{10,11... | collective-permute-start | bytes 18440 | tf_op jit(solution)/shard_map/ppermute | solution.py:868

commit v7 on v6

--- a/solution.py
+++ b/solution.py
@@ -167,7 +167,8 @@
 
 def level(z, s, tiles, xs, sums, stack):
     rows, top = z.rows, 8
-    short = up_to(rows, 8)
+    skip = z.tail == 1 and tiles[0] >= HALF_TILES
+    short = z.full if skip else up_to(rows, 8)
 
     def tile(kind, c):
         turn, cc = divmod(c, TILES)
@@ -186,6 +187,9 @@
         lanes = slice(c * LANES, (c + 1) * LANES)
         for k2, part in enumerate((high, low, high)):
             stack[s, k2 * z.full : (k2 + 1) * z.full, lanes] = part
+        if skip:
+            stack[s, 3 * z.full :, lanes] = jnp.zeros((PAD, LANES), BF)
+            continue
         rest = value[z.full :]
         high = rest.astype(BF).astype(F32)
         rest = high + pltpu.roll(rest - high, z.tail, 0) + pltpu.roll(high, 2 * z.tail, 0)
@@ -568,7 +572,7 @@
     )
     for s in range(z.stations):
         mean = smooth[3 * s : 3 * s + 1] + smooth[3 * s + 1 : 3 * s + 2] + smooth[3 * s + 2 : 3 * s + 3]
-        scale = 1.0 / jnp.sqrt(mean * (1.0 / (2 * SMOOTH + 1)) + EPS_POWER)
+        scale = lax.rsqrt(mean * (1.0 / (2 * SMOOTH + 1)) + EPS_POWER)
         out[2 * s : 2 * s + 1, :] = spec[2 * s] * scale
         out[2 * s + 1 : 2 * s + 2, :] = spec[2 * s + 1] * scale
 
@@ -694,7 +698,8 @@
     for s in range(z.stations):
         window(z, s, xs, sums)
         switch[s] = jnp.full((TILES, LANES), flags_s[s].astype(F32))
-    level(z, 0, range(TILES), xs, sums, stack)
+    for g in range(0, TILES, HALF_TILES):
+        level(z, 0, range(g, g + HALF_TILES), xs, sums, stack)
     copies[2].wait()
     copies[3].wait()
     stretch_table(z, away, first_v, table)

time: 23.5 us -> 23.5 us (level)
  no operation moved by 1% of the time
where the time goes in v7:
time: 23.5 us; the launch traced here: 23.3 us
  starting transfers between devices  10.2 us (43%)
  waiting for transfers between devices  6.26 us (27%)
  Pallas kernels  6.14 us (26%)
  between operations  0.72 us (3%)
    ppermute x3, starting transfers between devices, shards(): came, went = (lax.ppermute(message, 'tm', swap), message)  8.3 us
    ppermute x3, waiting for transfers between devices, shards(): came, went = (lax.ppermute(message, 'tm', swap), message)  3.28 us
    ppermute x3, waiting for transfers between devices, shards(): pieces += [lax.ppermute(piece, 'sta', swap) for piece in pieces]  2.97 us
    pallas_call x1, Pallas kernels, split_transform(): pl.pallas_call(functools.partial(away_kernel, z), in_specs=[HBM_SPEC] * 4...  2.37 us
    ppermute x3, starting transfers between devices, shards(): pieces += [lax.ppermute(piece, 'sta', swap) for piece in pieces]  1.89 us
    pallas_call x1, Pallas kernels, tables(): pl.pallas_call(functools.partial(table_kernel, z, offsets, split), in_spe...  1.04 us
    pallas_call x1, Pallas kernels, home(): pl.pallas_call(functools.partial(home_kernel, z), in_specs=[VMEM_SPEC] *...  0.99 us
    pallas_call x1, Pallas kernels, gathered(): pl.pallas_call(functools.partial(gathered_kernel, z), in_specs=[VMEM_SPEC...  0.9 us
  transfers between devices with their start and end apart: 6, of which 5 were waited for; matrix products, arithmetic and copies ran while one was open for 0% of the time, Pallas kernels for 9%

profile of v7, /device:TPU:0, one launch (start us, length us, event | category | flops | bytes accessed | tf_op | source)
XLA Modules:
  0.0 23.3 jit_solution(3976786653251674517)
XLA Ops:
  0.0 2.4 %away.1 = (bf16[192,128]{1,0:T(8,128)(2,1)S(1)}, bf16[2,112,1024]{2,1,0:T(8,128)(2,1)S(1)}, bf16[128,2048]{1,0:T(8,128)(2,1)S(1)}, f32[144,128]{1,0:T(8,128)S(1)...) custom-call(s32[2]{0:T(128)} %flags.3, bf16[2,33792]{1,0:T(2,128)(2,1)} %x.1, ...), custom_call_target="tpu_custom_call" | custom-call | tf_op jit(solution)/shard_map/away/pallas_call | solution.py:739
  2.4 3.1 %collective-permute-start = (bf16[192,128]{1,0:T(8,128)(2,1)S(1)}, bf16[192,128]{1,0:T(8,128)(2,1)S(1)}, u32[]{:S(2)}, u32[]{:S(2)}) collective-permute-start(bf16[192,128]{1,0:T(8,128)(2,1)S(1)} %get-tuple-element.29.went), channel_id=1, source_target_pairs={{0,4},{4,0},{8,12},{12,8},{16,20},{20,16},{24,28},{28,24},{1,5},{5... | collective-permute-start | bytes 147464 | tf_op jit(solution)/shard_map/ppermute | solution.py:856
  5.4 0.0 copy-start.1
  5.4 0.0 copy-start.2
  5.4 1.0 %home.1.kept = f32[4,40,128]{2,1,0:T(8,128)S(1)} custom-call(bf16[2,112,1024]{2,1,0:T(8,128)(2,1)S(1)} %get-tuple-element.24.stack, bf16[128,2048]{1,0:T(8,128)(2,1)S(1)} %get-tuple-element.25.weight, f32[144,128]{1,0:T(8,128)S(1)} %get-tuple-element.26.first, f32[4,2,72,256]{3,2,1,0:T(8,128)S(1)} %get-tuple-element.27.turn, ...), custom_call_target="tpu_custom_call" | custom-call | flops 1000000000 | bytes 1000000 | tf_op jit(solution)/shard_map/home/pallas_call | solution.py:762
  6.4 0.0 copy-start
  6.5 1.1 %collective-permute-done.came = bf16[192,128]{1,0:T(8,128)(2,1)S(1)} collective-permute-done((bf16[192,128]{1,0:T(8,128)(2,1)S(1)}, bf16[192,128]{1,0:T(8,128)(2,1)S(1)}, u32[]{:S(2)}, u32[]{:S(2)}) %collective-permute-start) | collective-permute-done | bytes 49184 | tf_op jit(solution)/shard_map/ppermute | solution.py:856
  7.5 0.1 merge.2
  7.6 2.1 %collective-permute-start.1 = (bf16[144,128]{1,0:T(8,128)(2,1)S(1)}, bf16[144,128]{1,0:T(8,128)(2,1)S(1)}, u32[]{:S(2)}, u32[]{:S(2)}) collective-permute-start(bf16[144,128]{1,0:T(8,128)(2,1)S(1)} %get-tuple-element.31.went), channel_id=1, source_target_pairs={{0,8},{4,12},{8,0},{12,4},{16,24},{20,28},{24,16},{28,20},{1,9},{5... | collective-permute-start | bytes 110600 | tf_op jit(solution)/shard_map/ppermute | solution.py:856
  9.8 1.9 %collective-permute-done.1.came = bf16[144,128]{1,0:T(8,128)(2,1)S(1)} collective-permute-done((bf16[144,128]{1,0:T(8,128)(2,1)S(1)}, bf16[144,128]{1,0:T(8,128)(2,1)S(1)}, u32[]{:S(2)}, u32[]{:S(2)}) %collective-permute-start.1) | collective-permute-done | bytes 36896 | tf_op jit(solution)/shard_map/ppermute | solution.py:856
  11.7 0.1 merge.3
  11.8 3.1 %collective-permute-start.2 = (bf16[168,128]{1,0:T(8,128)(2,1)S(1)}, bf16[168,128]{1,0:T(8,128)(2,1)S(1)}, u32[]{:S(2)}, u32[]{:S(2)}) collective-permute-start(bf16[168,128]{1,0:T(8,128)(2,1)S(1)} %get-tuple-element.33.went), channel_id=1, source_target_pairs={{0,16},{4,20},{8,24},{12,28},{16,0},{20,4},{24,8},{28,12},{1,17},{... | collective-permute-start | bytes 129032 | tf_op jit(solution)/shard_map/ppermute | solution.py:856
  15.5 0.0 copy-done.1
  15.5 0.0 copy-done.2
  15.5 1.0 %tables.1 = (bf16[1,40,384]{2,1,0:T(8,128)(2,1)S(1)}, f32[16,384]{1,0:T(8,128)S(1)}, bf16[64,768]{1,0:T(8,128)(2,1)S(1)}, f32[2,128,384]{2,1,0:T(8,128)S(1)}, bf...) custom-call(s32[1,1]{1,0:T(1,128)} %bitcast.1.band, ...), custom_call_target="tpu_custom_call" | custom-call | flops 4000000 | bytes 2000000 | tf_op jit(solution)/shard_map/tables/pallas_call | solution.py:437
  16.6 0.3 %collective-permute-done.2.came = bf16[168,128]{1,0:T(8,128)(2,1)S(1)} collective-permute-done((bf16[168,128]{1,0:T(8,128)(2,1)S(1)}, bf16[168,128]{1,0:T(8,128)(2,1)S(1)}, u32[]{:S(2)}, u32[]{:S(2)}) %collective-permute-start.2) | collective-permute-done | bytes 43040 | tf_op jit(solution)/shard_map/ppermute | solution.py:856
  16.9 0.9 %spectrum.1.refs_0_ = f32[4,384]{1,0:T(4,128)S(1)} custom-call(f32[1,40,128]{2,1,0:T(8,128)S(1)} %get-tuple-element.32.kept, bf16[168,128]{1,0:T(8,128)(2,1)S(1)} %collective-permute-done.2.came, bf16[168,128]{1,0:T(8,128)(2,1)S(1)} %get-tuple-element.33.went, bf16[1,40,384]{2,1,0:T(8,128)(2,1)S(1)} %get-tuple-element.34.choose, ...), custom_call_target="tpu_custom_call" | custom-call | tf_op jit(solution)/shard_map/spectrum/pallas_call | solution.py:592
  17.8 1.9 %collective-permute-start.3 = (f32[4,384]{1,0:T(4,128)S(1)}, f32[4,384]{1,0:T(4,128)S(1)}, u32[]{:S(2)}, u32[]{:S(2)}) collective-permute-start(f32[4,384]{1,0:T(4,128)S(1)} %spectrum.1.refs_0_), channel_id=1, source_target_pairs={{0,2},{1,3},{2,0},{3,1},{4,6},{5,7},{6,4},{7,5},{8,10},{9,11},{10,... | collective-permute-start | bytes 18440 | tf_op jit(solution)/shard_map/ppermute | solution.py:873
  19.7 0.0 collective-permute-start.4
  19.7 1.8 %collective-permute-done.3.refs_1_ = f32[4,384]{1,0:T(4,128)S(1)} collective-permute-done((f32[4,384]{1,0:T(4,128)S(1)}, f32[4,384]{1,0:T(4,128)S(1)}, u32[]{:S(2)}, u32[]{:S(2)}) %collective-permute-start.3) | collective-permute-done | bytes 6176 | tf_op jit(solution)/shard_map/ppermute | solution.py:873
  21.5 0.0 collective-permute-start.5
  21.5 0.0 collective-permute-done.4.refs_2_
  21.5 1.2 %collective-permute-done.5.refs_3_ = f32[4,384]{1,0:T(4,128)S(1)} collective-permute-done((f32[4,384]{1,0:T(4,128)S(1)}, f32[4,384]{1,0:T(4,128)S(1)}, u32[]{:S(2)}, u32[]{:S(2)}) %collective-permute-start.5) | collective-permute-done | bytes 6176 | tf_op jit(solution)/shard_map/ppermute | solution.py:873
  22.6 0.0 copy-done
  22.6 0.7 %cross.1 = f32[2,8,2,384]{3,2,1,0:T(2,128)} custom-call(f32[4,2,128]{2,1,0:T(2,128)S(1)} %get-tuple-element.23.pairs, f32[2,8,2,384]{3,2,1,0:T(2,128)S(1)} %copy-done, f32[4,384]{1,0:T(4,128)S(1)} %spectrum.1.refs_0_, f32[4,384]{1,0:T(4,128)S(1)} %collective-permute-done.3.refs_1_, f32[4,384]{1,0:T(4,128)S(1)} %collective-permute-done.4.refs_2_, ...), custom_call_target="tpu_custom_call" | custom-call | tf_op jit(solution)/shard_map/cross/pallas_call | solution.py:833
Async XLA Ops:
  2.4 5.1 %collective-permute-start = (bf16[192,128]{1,0:T(8,128)(2,1)S(1)}, bf16[192,128]{1,0:T(8,128)(2,1)S(1)}, u32[]{:S(2)}, u32[]{:S(2)}) collective-permute-start(bf16[192,128]{1,0:T(8,128)(2,1)S(1)} %get-tuple-element.29.went), channel_id=1, source_target_pairs={{0,4},{4,0},{8,12},{12,8},{16,20},{20,16},{24,28},{28,24},{1,5},{5... | collective-permute-start | bytes 147464 | tf_op jit(solution)/shard_map/ppermute | solution.py:856
  5.4 10.1 %copy-start.1 = (s32[2]{0:T(128)S(1)}, s32[2]{0:T(128)}, u32[]{:S(2)}) copy-start(s32[2]{0:T(128)} %flags.3) | copy-start | bytes 28
  5.4 10.1 %copy-start.2 = (s32[4,4]{1,0:T(4,128)S(1)}, s32[4,4]{1,0:T(4,128)}, u32[]{:S(2)}) copy-start(s32[4,4]{1,0:T(4,128)} %mask.1) | copy-start | bytes 196
  6.4 16.2 %copy-start = (f32[2,8,2,384]{3,2,1,0:T(2,128)S(1)}, f32[2,8,2,384]{3,2,1,0:T(2,128)}, u32[]{:S(2)}) copy-start(f32[2,8,2,384]{3,2,1,0:T(2,128)} %stacks.1) | copy-start | bytes 147460
  7.6 4.1 %collective-permute-start.1 = (bf16[144,128]{1,0:T(8,128)(2,1)S(1)}, bf16[144,128]{1,0:T(8,128)(2,1)S(1)}, u32[]{:S(2)}, u32[]{:S(2)}) collective-permute-start(bf16[144,128]{1,0:T(8,128)(2,1)S(1)} %get-tuple-element.31.went), channel_id=1, source_target_pairs={{0,8},{4,12},{8,0},{12,4},{16,24},{20,28},{24,16},{28,20},{1,9},{5... | collective-permute-start | bytes 110600 | tf_op jit(solution)/shard_map/ppermute | solution.py:856
  11.8 5.1 %collective-permute-start.2 = (bf16[168,128]{1,0:T(8,128)(2,1)S(1)}, bf16[168,128]{1,0:T(8,128)(2,1)S(1)}, u32[]{:S(2)}, u32[]{:S(2)}) collective-permute-start(bf16[168,128]{1,0:T(8,128)(2,1)S(1)} %get-tuple-element.33.went), channel_id=1, source_target_pairs={{0,16},{4,20},{8,24},{12,28},{16,0},{20,4},{24,8},{28,12},{1,17},{... | collective-permute-start | bytes 129032 | tf_op jit(solution)/shard_map/ppermute | solution.py:856
  17.8 3.7 %collective-permute-start.3 = (f32[4,384]{1,0:T(4,128)S(1)}, f32[4,384]{1,0:T(4,128)S(1)}, u32[]{:S(2)}, u32[]{:S(2)}) collective-permute-start(f32[4,384]{1,0:T(4,128)S(1)} %spectrum.1.refs_0_), channel_id=1, source_target_pairs={{0,2},{1,3},{2,0},{3,1},{4,6},{5,7},{6,4},{7,5},{8,10},{9,11},{10,... | collective-permute-start | bytes 18440 | tf_op jit(solution)/shard_map/ppermute | solution.py:873
  19.7 1.8 %collective-permute-start.4 = (f32[4,384]{1,0:T(4,128)S(1)}, f32[4,384]{1,0:T(4,128)S(1)}, u32[]{:S(2)}, u32[]{:S(2)}) collective-permute-start(f32[4,384]{1,0:T(4,128)S(1)} %spectrum.1.refs_0_), channel_id=1, source_target_pairs={{0,1},{1,0},{2,3},{3,2},{4,5},{5,4},{6,7},{7,6},{8,9},{9,8},{10,11... | collective-permute-start | bytes 18440 | tf_op jit(solution)/shard_map/ppermute | solution.py:873
  21.5 1.2 %collective-permute-start.5 = (f32[4,384]{1,0:T(4,128)S(1)}, f32[4,384]{1,0:T(4,128)S(1)}, u32[]{:S(2)}, u32[]{:S(2)}) collective-permute-start(f32[4,384]{1,0:T(4,128)S(1)} %collective-permute-done.3.refs_1_), channel_id=1, source_target_pairs={{0,1},{1,0},{2,3},{3,2},{4,5},{5,4},{6,7},{7,6},{8,9},{9,8},{10,11... | collective-permute-start | bytes 18440 | tf_op jit(solution)/shard_map/ppermute | solution.py:873
